TPU v7x, 32 devices: a whole 2x2x4 slice. The times are simulated.
32 devices in a mesh: slab: 16 (over z, y, x), grp: 2 (over core).
Axes of the slice: x: 2, y: 2, z: 4, core: 2. Of those that a mesh axis runs over, the one named last changes fastest.
Arguments:
- photon_table: float32 [32, 10, 3200], P('slab', 'grp'), may hold values from -30 to 30
- bin_weights: float32 [32, 10, 3200], P('slab', 'grp'), may hold values from 0.005 to 0.03
- first_start: int32 [32], replicated, may hold values from 0 to 60, as said below
- first_band: float32 [32, 4], replicated, may hold values from 0.2 to 1
- second_start: int32 [10], replicated, may hold values from 0 to 60, as said below
- second_band: float32 [10, 4], replicated, may hold values from 0.2 to 1
- third_start: int32 [64], replicated, may hold values from 0 to 28, as said below
- third_band: float32 [64, 4], replicated, may hold values from 0.2 to 1
- fourth_start: int32 [50], replicated, may hold values from 0 to 28, as said below
- fourth_band: float32 [50, 4], replicated, may hold values from 0.2 to 1
Outputs:
- solution: float32 [64, 64, 1024], P('slab', 'grp')
- residual: float32 [64, 64, 1024], P('slab', 'grp')
Inputs may be any that keep to these rules, and one draw needn't show every extreme that they name: Bin i of the first dimension uses coefficients first_start[i] to first_start[i] + 3; the starts never fall from one bin to the next, the first bin starts at 0 and the last at 60. Bin i of the second dimension uses coefficients second_start[i] to second_start[i] + 3; the starts never fall, the first is 0 and the last 60. Bin i of the third dimension uses coefficients third_start[i] to third_start[i] + 3; the starts never fall, the first is 0 and the last 28. Bin i of the fourth dimension uses coefficients fourth_start[i] to fourth_start[i] + 3; the starts never fall, the first is 0 and the last 28.
All inputs are finite; a program needn't handle non-finite values.
Results may differ from a plain program's by a relative error of at most 0.0003.
Values sent between devices are 32-bit elements; how exact they have to be, the bound alone decides.
No kernel may reach another device: no remote copies, remote signals or barrier semaphores. Data moves between devices by JAX's collectives and lax.ppermute only.
A program may use at most 64 MiB of HBM per device.

v0:
```python
import jax
import jax.numpy as jnp
from jax import lax
from jax.experimental import pallas as pl
from jax.experimental.pallas import tpu as pltpu
from jax.sharding import PartitionSpec as P

K0 = 64
K1 = 64
K2 = 32
K3 = 32
ITERS = 2


highest = lax.Precision.HIGHEST
smoothing = 0.1
stencil_weights = (1.0, -4.0, 6.0, -4.0, 1.0)


def with_halo(value, sides, width):
    for axis, dim in sides:
        count, length = (lax.axis_size(axis), value.shape[dim])
        up = [(i, (i + 1) % count) for i in range(count - 1)]
        down = [(j, i) for i, j in up]
        last = lax.slice_in_dim(value, length - width, length, axis=dim)
        initial = lax.slice_in_dim(value, 0, width, axis=dim)
        before = lax.ppermute(last, axis, up)
        after = lax.ppermute(initial, axis, down)
        value = jnp.concatenate([before, value, after], axis=dim)
    return value


def dense_basis(starts, values, coef_count):
    relative = jnp.arange(coef_count, dtype=jnp.int32)[None, :] - starts[:, None]
    matrix = jnp.zeros((starts.shape[0], coef_count), jnp.float32)
    for offset in range(4):
        matrix = matrix + jnp.where(relative == offset, values[:, offset : offset + 1], 0.0)
    return matrix


def five_point(source, along, extent):
    running = stencil_weights[0] * lax.slice_in_dim(source, 0, extent, axis=along)
    for offset in range(1, 5):
        running = running + stencil_weights[offset] * lax.slice_in_dim(
            source, offset, offset + extent, axis=along
        )
    return running


def local_stencil(tensor, along):
    widths = [(0, 0)] * tensor.ndim
    widths[along] = (2, 2)
    return five_point(jnp.pad(tensor, widths), along, tensor.shape[along])


def inner_forward(tensor, third_basis, fourth_basis):
    leading, middle = (tensor.shape[0], tensor.shape[1])
    blocked = tensor.reshape(leading, middle, third_basis.shape[1], fourth_basis.shape[1])
    blocked = jnp.einsum("abcd,nd->abcn", blocked, fourth_basis, precision=highest)
    blocked = jnp.einsum("abcn,mc->abmn", blocked, third_basis, precision=highest)
    return blocked.reshape(leading, middle, third_basis.shape[0] * fourth_basis.shape[0])


def inner_adjoint(tensor, third_basis, fourth_basis):
    leading, middle = (tensor.shape[0], tensor.shape[1])
    blocked = tensor.reshape(leading, middle, third_basis.shape[0], fourth_basis.shape[0])
    blocked = jnp.einsum("abmn,mc->abcn", blocked, third_basis, precision=highest)
    blocked = jnp.einsum("abcn,nd->abcd", blocked, fourth_basis, precision=highest)
    return blocked.reshape(leading, middle, third_basis.shape[1] * fourth_basis.shape[1])


def lead_product(tensor, matrix):
    combined = jnp.einsum(
        "ka,ain->kin",
        matrix,
        lax.all_to_all(tensor, "slab", split_axis=2, concat_axis=0, tiled=True),
        precision=highest,
    )
    return lax.all_to_all(combined, "slab", split_axis=0, concat_axis=2, tiled=True)


def second_product(tensor, matrix):
    return jnp.einsum(
        "lp,apn->aln", matrix, lax.all_gather(tensor, "grp", axis=1, tiled=True), precision=highest
    )


def penalty(coeffs):
    leading, middle = (coeffs.shape[0], coeffs.shape[1])
    padded = with_halo(coeffs, (("slab", 0), ("grp", 1)), 2)
    along_lead = five_point(padded[:, 2 : 2 + middle], 0, leading)
    along_rows = five_point(padded[2 : 2 + leading, :], 1, middle)
    blocked = coeffs.reshape(leading, middle, K2, K3)
    inner_part = local_stencil(blocked, 2) + local_stencil(blocked, 3)
    return along_lead + along_rows + inner_part.reshape(leading, middle, K2 * K3)


def squared_total(vector):
    return lax.psum(jnp.sum(vector * vector), ("slab", "grp"))


def per_device(
    photon_table,
    bin_weights,
    first_start,
    first_band,
    second_start,
    second_band,
    third_start,
    third_band,
    fourth_start,
    fourth_band,
):
    first_basis = dense_basis(first_start, first_band, K0)
    second_basis = dense_basis(second_start, second_band, K1)
    third_basis = dense_basis(third_start, third_band, K2)
    fourth_basis = dense_basis(fourth_start, fourth_band, K3)
    first_back = first_basis.T
    group_index = lax.axis_index("grp")
    row_count = photon_table.shape[1]
    coef_rows = K1 // lax.axis_size("grp")
    near_rows = lax.dynamic_slice_in_dim(second_basis, group_index * row_count, row_count, 0)
    back_rows = lax.dynamic_slice_in_dim(second_basis.T, group_index * coef_rows, coef_rows, 0)

    def adjoint(table):
        tensor = lead_product(table, first_back)
        tensor = second_product(tensor, back_rows)
        return inner_adjoint(tensor, third_basis, fourth_basis)

    right_side = adjoint(bin_weights * photon_table)
    solution = jnp.zeros_like(right_side)
    residual = right_side
    direction = right_side
    norm_now = squared_total(residual)
    for sweep in range(ITERS):
        forward_tensor = inner_forward(direction, third_basis, fourth_basis)
        forward_tensor = second_product(forward_tensor, near_rows)
        mapped = adjoint(
            bin_weights * lead_product(forward_tensor, first_basis)
        ) + smoothing * penalty(direction)
        curve_total = lax.psum(jnp.sum(direction * mapped), ("slab", "grp"))
        step_size = norm_now / curve_total
        solution = solution + step_size * direction
        residual = residual - step_size * mapped
        norm_next = squared_total(residual)
        direction = residual + norm_next / norm_now * direction
        norm_now = norm_next
    return (solution, residual)


SLABS, GRPS = 16, 2
DEVICES = SLABS * GRPS
L0, L1 = 2, 5
ROWS = L0 * L1
N2, N3 = 64, 50
N0, N1 = 32, 10
HI = lax.Precision.HIGHEST
f32 = jnp.float32


def iota(shape, dim):
    return lax.broadcasted_iota(jnp.int32, shape, dim)


def mm(a, b):
    return jnp.dot(a, b, precision=HI, preferred_element_type=f32)


def mm_t(a, b):
    return lax.dot_general(
        a, b, (((1,), (1,)), ((), ())), precision=HI, preferred_element_type=f32
    )


def move(block, source, target):
    shift = (target - source) * 32 % 128
    return pltpu.roll(block, shift, 1) if shift else block


def merge(parts):
    lane = iota(parts[0].shape, 1)
    out = parts[-1]
    for q in range(len(parts) - 2, -1, -1):
        out = jnp.where(lane < 32 * (q + 1), parts[q], out)
    return out


def slot(r):
    return 8 * (r // L1) + r % L1


def banded(start_ref, band_ref, width, wrap):
    n = start_ref.shape[0]
    row = start_ref[...].reshape(1, n)
    eye = iota((n, n), 0) == iota((n, n), 1)
    start = jnp.sum(jnp.where(eye, row.astype(f32), 0.0), axis=1, keepdims=True)
    relative = (iota((n, width), 1) % wrap) - start.astype(jnp.int32)
    band = band_ref[...]
    out = jnp.zeros((n, width), f32)
    for offset in range(4):
        out = out + jnp.where(relative == offset, band[:, offset : offset + 1], 0.0)
    return out


def expand(ref, a, p):
    first = 200 * p
    tile, off = first // 128, first % 128
    lane = iota((L1, 128), 1)

    def window(t):
        low = ref[a, :, t * 128 : (t + 1) * 128]
        if off == 0:
            return low
        t1 = min(t + 1, 24)
        high = ref[a, :, t1 * 128 : (t1 + 1) * 128]
        return jnp.where(
            lane < 128 - off, pltpu.roll(low, 128 - off, 1), pltpu.roll(high, 128 - off, 1)
        )

    return window(tile), window(min(tile + 1, 24))


def table_to_mixed(field, kron_third, second_t, rows_ref, stack_ref):
    rows_ref[...] = mm(field, kron_third)
    for c in range(4):
        for j in range(3):
            parts = []
            for q in range(4):
                r = 4 * j + q
                if r < ROWS:
                    part = rows_ref[pl.ds(slot(r), 16, stride=16), :]
                    parts.append(move(part, c, q))
                else:
                    parts.append(jnp.zeros((16, 128), f32))
            stack_ref[16 * c : 16 * c + 16, 128 * j : 128 * j + 128] = merge(parts)
    return mm(second_t, stack_ref[...])


def mixed_to_table(value, kron_third, second, rows_ref, stack_ref):
    stack_ref[...] = mm(second, value)
    rows_ref[...] = jnp.zeros((256, 128), f32)
    for r in range(ROWS):
        j, q = r // 4, r % 4
        parts = [
            move(stack_ref[16 * c : 16 * c + 16, 128 * j : 128 * j + 128], q, c) for c in range(4)
        ]
        rows_ref[pl.ds(slot(r), 16, stride=16), :] = merge(parts)
    return mm_t(rows_ref[...], kron_third)


def inner_penalty(value):
    out = 12.0 * value
    row = iota((32, 128), 0)
    inside = iota((32, 128), 1) % 32
    tiles = []
    for j in range(3):
        tile = value[:, 128 * j : 128 * j + 128]
        total = 12.0 * tile
        for d, weight in ((1, -4.0), (2, 1.0)):
            total = total + weight * (
                jnp.where(row >= d, pltpu.roll(tile, d, 0), 0.0)
                + jnp.where(row < 32 - d, pltpu.roll(tile, 32 - d, 0), 0.0)
                + jnp.where(inside >= d, pltpu.roll(tile, d, 1), 0.0)
                + jnp.where(inside < 32 - d, pltpu.roll(tile, 128 - d, 1), 0.0)
            )
        tiles.append(total)
    return jnp.concatenate(tiles, axis=1)


def tile_of(value, j):
    return value[:, 128 * j : 128 * j + 128]


def put(ref, row, count, value):
    ref[pl.ds(row, 32, stride=count), :] = value


def lanes(values):
    lane = iota((8, 128), 1)
    out = jnp.zeros((8, 128), f32)
    for k, value in enumerate(values):
        out = jnp.where(lane == k, value, out)
    return out


def spread(ref, row, count, values):
    one = lanes(values)
    put(ref, row, count, jnp.concatenate([one] * 4, axis=0))


def totals(ref, row, count, number):
    summed = jnp.sum(ref[pl.ds(row, 32, stride=count), :], axis=0, keepdims=True)
    lane = iota((1, 128), 1)
    return [jnp.sum(jnp.where(lane == k, summed, 0.0)) for k in range(number)]


def pick(ref, k):
    lane = iota((1, 128), 1)
    return jnp.sum(jnp.where(lane == k, ref[0:1, :], 0.0))


def start_kernel(
    table_ref, weight_ref, start2_ref, band2_ref, start3_ref, band3_ref,
    send_ref, wide_ref, kron_ref, second_ref, second_t_ref, field_ref, rows_ref, stack_ref,
):
    fourth = banded(start3_ref, band3_ref, 128, 32)
    pick_bin = (iota((256, N3), 0) % N3 == iota((256, N3), 1)) & (iota((256, N3), 0) < 4 * N3)
    kron = mm(jnp.where(pick_bin, 1.0, 0.0), fourth)
    same = iota((256, 128), 0) // N3 == iota((256, 128), 1) // 32
    kron = jnp.where(same, kron, 0.0)
    kron_ref[...] = kron
    third = banded(start2_ref, band2_ref, 32, 32)
    order = iota((N2, N2), 0)
    permute = (order % 16) * 4 + order // 16 == iota((N2, N2), 1)
    second = mm(jnp.where(permute, 1.0, 0.0), third)
    second_ref[...] = second
    second_t = second.T
    second_t_ref[...] = second_t
    wide_ref[...] = jnp.zeros((256, 256), f32)
    field_ref[...] = jnp.zeros((256, 256), f32)
    for p in range(16):
        for a in range(L0):
            base = 16 * p + 8 * a
            low, high = expand(weight_ref, a, p)
            wide_ref[base : base + L1, 0:128] = low
            wide_ref[base : base + L1, 128:256] = high
            t_low, t_high = expand(table_ref, a, p)
            field_ref[base : base + L1, 0:128] = t_low * low
            field_ref[base : base + L1, 128:256] = t_high * high
    mixed = table_to_mixed(field_ref[...], kron, second_t, rows_ref, stack_ref)
    once = inner_penalty(mixed)
    twice = inner_penalty(once)
    for base, value in ((0, mixed), (3, once), (5, twice)):
        put(send_ref, base, 8, tile_of(value, 0))
        put(send_ref, base + 1, 8, tile_of(value, 1))
    lane = iota((32, 128), 1)
    put(send_ref, 2, 8, jnp.where(lane < 64, tile_of(mixed, 2), pltpu.roll(tile_of(once, 2), 64, 1)))
    put(send_ref, 7, 8, tile_of(twice, 2))


def pentadiagonal(n):
    gap = jnp.abs(iota((n, n), 0) - iota((n, n), 1))
    return jnp.where(gap == 0, 6.0, jnp.where(gap == 1, -4.0, jnp.where(gap == 2, 1.0, 0.0)))


def three_terms(value):
    high = value.astype(jnp.bfloat16)
    rest = value - high.astype(f32)
    middle = rest.astype(jnp.bfloat16)
    low = (rest - middle.astype(f32)).astype(jnp.bfloat16)
    return high, middle, low


def choose(pieces, selector):
    out = None
    for piece in pieces:
        term = jnp.dot(piece, selector, preferred_element_type=f32)
        out = term if out is None else out + term
    return out


def matrix_kernel(
    group_ref, start0_ref, band0_ref, start1_ref, band1_ref,
    gram_ref, high_ref, lift_ref, side_ref, rows0_ref, rows1_ref,
):
    first = banded(start0_ref, band0_ref, K0, K0)
    second = banded(start1_ref, band1_ref, K1, K1)
    penalty_matrix = pentadiagonal(K0)

    def powers(basis):
        out = [basis]
        for _ in range(3):
            out.append(mm(out[-1], penalty_matrix))
        return out

    total = DEVICES * ROWS
    row0 = iota((total, N0), 0)
    pick0 = 2 * (row0 % 32 // 2) + row0 // 32 // L1 == iota((total, N0), 1)
    row1 = iota((total, N1), 0)
    pick1 = L1 * (row1 % 2) + row1 // 32 % L1 == iota((total, N1), 1)
    powers0, powers1 = powers(first), powers(second)
    wide0 = mm(jnp.where(pick0, 1.0, 0.0), first)
    wide1 = mm(jnp.where(pick1, 1.0, 0.0), second)
    for k in range(4):
        rows0_ref[:, 32 * k : 32 * k + 32] = mm_t(wide0, powers0[k])
        rows1_ref[:, 16 * k : 16 * k + N1] = mm_t(wide1, powers1[k])
    col0 = iota((N0, total), 1)
    select0 = jnp.where(
        2 * (col0 % 32 // 2) + col0 // 32 // L1 == iota((N0, total), 0), 1.0, 0.0
    ).astype(jnp.bfloat16)
    col1 = iota((N1, total), 1)
    select1 = jnp.where(
        L1 * (col1 % 2) + col1 // 32 % L1 == iota((N1, total), 0), 1.0, 0.0
    ).astype(jnp.bfloat16)

    @pl.loop(0, ROWS)
    def _(step):
        base = pl.multiple_of(step * 32, 32)
        block0 = rows0_ref[pl.ds(base, 32), :]
        block1 = rows1_ref[pl.ds(base, 32), :]
        g = [choose(three_terms(block0[:, 32 * k : 32 * k + 32]), select0) for k in range(4)]
        h = [choose(three_terms(block1[:, 16 * k : 16 * k + N1]), select1) for k in range(4)]
        gram_ref[pl.ds(base, 32), :] = g[0] * h[0]
        gram_ref[pl.ds(base + total, 32), :] = g[1] * h[0] + g[0] * h[1]
        high_ref[pl.ds(base, 32), :] = g[2] * h[0] + 2.0 * g[1] * h[1] + g[0] * h[2]
        high_ref[pl.ds(base + total, 32), :] = (
            g[3] * h[0] + 3.0 * (g[2] * h[1] + g[1] * h[2]) + g[0] * h[3]
        )

    lifted = choose(three_terms(first.T), select0)
    column = iota((K0, total), 1)
    owner = L1 * (column % 2) + column // 32 % L1
    for n in range(N1):
        lift_ref[K0 * n : K0 * n + K0, :] = jnp.where(owner == n, lifted, 0.0)

    coef = iota((128, K1), 0) % 32 + 32 * group_ref[0]
    pick_coef = jnp.where(coef == iota((128, K1), 1), 1.0, 0.0)
    side_ref[...] = jnp.zeros((128, 128), f32)
    spot = iota((N1, 128), 1)
    for k in range(3):
        own = mm_t(pick_coef, powers1[k])
        for alpha in range(4):
            rows = slice(32 * alpha, 32 * alpha + 32)
            side_ref[rows, 40 * k + 10 * alpha : 40 * k + 10 * alpha + 10] = own[rows, :]


def unpack(ref, row, count, r, source, target):
    return move(ref[pl.ds(row, 32, stride=count), :], source, target)


def first_column_kernel(recv_ref, gram_ref, send_ref, fields_ref, images_ref):
    total = DEVICES * ROWS
    zero = jnp.zeros((32, 128), f32)
    for r in range(ROWS):
        j, q = r // 4, r % 4
        where0 = (j, q) if j < 2 else (2, q)
        where1 = (3 + j, q) if j < 2 else (2, q + 2)
        where2 = (5 + j, q) if j < 2 else (7, q)
        parts = [
            unpack(recv_ref, place[0], 8, r, place[1], k)
            for k, place in enumerate((where0, where1, where2))
        ]
        fields_ref[32 * r : 32 * r + 32, :] = merge(parts + [zero])
    fields = fields_ref[...]
    product = mm(gram_ref[...], fields)
    lane = iota((total, 128), 1)
    images = product[:total] + jnp.where(
        (lane >= 32) & (lane < 64), pltpu.roll(product[total:], 32, 1), 0.0
    )
    images_ref[...] = images
    norm = jnp.sum(jnp.where(lane < 32, fields * images, 0.0))
    bend = jnp.sum(jnp.where(lane < 32, fields * pltpu.roll(images, 96, 1), 0.0))
    send_rows(send_ref, images_ref)
    spread(send_ref, 3, 4, (norm, bend))


def send_rows(send_ref, value_ref):
    for j in range(3):
        parts = []
        for q in range(4):
            r = 4 * j + q
            if r < ROWS:
                parts.append(move(value_ref[32 * r : 32 * r + 32, :], 0, q))
            else:
                parts.append(jnp.zeros((32, 128), f32))
        put(send_ref, j, 4, merge(parts))


def received_rows(recv_ref):
    return jnp.concatenate([recv_ref[pl.ds(j, 32, stride=4), :] for j in range(3)], axis=1)


def first_row_kernel(
    recv_ref, wide_ref, kron_ref, second_ref, second_t_ref,
    send_ref, scalar_ref, rows_ref, stack_ref,
):
    norm, bend = totals(recv_ref, 3, 4, 2)
    scalar_ref[...] = lanes((norm, bend))
    kron = kron_ref[...]
    field = mixed_to_table(received_rows(recv_ref), kron, second_ref[...], rows_ref, stack_ref)
    weighted = wide_ref[...] * field
    energy = jnp.sum(field * weighted)
    mixed = table_to_mixed(weighted, kron, second_t_ref[...], rows_ref, stack_ref)
    once = inner_penalty(mixed)
    for base, value in ((0, mixed), (3, once)):
        put(send_ref, base, 8, tile_of(value, 0))
        put(send_ref, base + 1, 8, tile_of(value, 1))
    lane = iota((32, 128), 1)
    put(send_ref, 2, 8, jnp.where(lane < 64, tile_of(mixed, 2), pltpu.roll(tile_of(once, 2), 64, 1)))
    spread(send_ref, 5, 8, (energy,))
    for row in (6, 7):
        put(send_ref, row, 8, jnp.zeros((32, 128), f32))


def second_column_kernel(
    recv_ref, gram_ref, fields_ref, images_ref, scalar_ref,
    send_ref, blend_ref, out_scalar_ref, next_ref, image_ref,
):
    zero = jnp.zeros((32, 128), f32)
    for r in range(ROWS):
        j, q = r // 4, r % 4
        where0 = (j, q) if j < 2 else (2, q)
        where1 = (3 + j, q) if j < 2 else (2, q + 2)
        parts = [
            unpack(recv_ref, place[0], 8, r, place[1], k) for k, place in enumerate((where0, where1))
        ]
        next_ref[32 * r : 32 * r + 32, :] = merge(parts + [zero])
    (energy,) = totals(recv_ref, 5, 8, 1)
    norm, bend = pick(scalar_ref, 0), pick(scalar_ref, 1)
    step = norm / (energy + 0.1 * bend)
    out_scalar_ref[...] = lanes((norm, step))
    fields, images, following = fields_ref[...], images_ref[...], next_ref[...]
    image = mm(gram_ref[0 : DEVICES * ROWS, :], following)
    image_ref[...] = images - step * (image + 0.1 * pltpu.roll(images, 96, 1))
    send_rows(send_ref, image_ref)
    put(send_ref, 3, 4, zero)
    lane = iota(fields.shape, 1)
    reduced = fields - step * (following + 0.1 * pltpu.roll(fields, 96, 1))
    blend_ref[...] = jnp.where(lane < 64, reduced, pltpu.roll(fields, 64, 1))


def coefficient_penalty(value):
    k = iota(value.shape, 0) % K0
    count = value.shape[0]
    total = 6.0 * value
    for d, weight in ((1, -4.0), (2, 1.0)):
        total = total + weight * (
            jnp.where(k >= d, pltpu.roll(value, d, 0), 0.0)
            + jnp.where(k < K0 - d, pltpu.roll(value, count - d, 0), 0.0)
        )
    return total


def send_blocks(send_ref, count, base, value_ref, block):
    for j in range(10):
        parts = []
        for q in range(4):
            m = 4 * j + q
            alpha, n = m // 10, m % 10
            parts.append(move(value_ref[pl.ds(K0 * n + alpha, 16, stride=4), :], block, q))
        merged = merge(parts)
        for g in range(GRPS):
            send_ref[pl.ds(g * count + base + j, 16, stride=2 * count), :] = merged


def middle_kernel(blend_ref, gram_ref, high_ref, lift_ref, scalar_ref, send_ref, keep_ref, sums_ref):
    total = DEVICES * ROWS
    step = pick(scalar_ref, 1)
    small = 0.1 * step
    blend = blend_ref[...]
    lane = iota(blend.shape, 1)
    product, higher = mm(gram_ref[...], blend), mm(high_ref[...], blend)
    g0, g1, g2, g3 = product[:total], product[total:], higher[:total], higher[total:]
    head = g0 - small * pltpu.roll(g1, 64, 1)
    tail = g1 - small * pltpu.roll(g2, 64, 1)
    end = g2 - small * pltpu.roll(g3, 64, 1)
    scaled = pltpu.roll(blend, 64, 1)
    low = lane < 32
    norm = jnp.sum(jnp.where(low, blend * head - small * scaled * tail, 0.0))
    head_p = tail + pltpu.roll(head, 96, 1)
    tail_p = end + pltpu.roll(tail, 96, 1)
    bend = jnp.sum(jnp.where(low, blend * head_p - small * scaled * tail_p, 0.0))
    sums_ref[...] = lanes((norm, bend))
    lifted = mm(lift_ref[...], blend)
    once = coefficient_penalty(lifted)
    twice = coefficient_penalty(once)
    h_a = lifted - small * pltpu.roll(once, 64, 1)
    y_1 = once + pltpu.roll(lifted, 96, 1)
    x_a = once + pltpu.roll(lifted, 96, 1) - small * (
        pltpu.roll(twice, 64, 1) + pltpu.roll(once, 32, 1)
    )
    h_0 = pltpu.roll(lifted, 64, 1)
    wide = iota(lifted.shape, 1)
    keep = jnp.where(
        wide < 32, h_0, jnp.where(wide < 64, pltpu.roll(h_a, 32, 1), jnp.where(wide < 96, y_1, pltpu.roll(x_a, 96, 1)))
    )
    keep_ref[...] = keep
    for block in range(3):
        send_blocks(send_ref, 30, 10 * block, keep_ref, block)


def second_row_kernel(
    recv_ref, sums_ref, wide_ref, kron_ref, second_ref, second_t_ref,
    send_ref, rows_ref, stack_ref,
):
    kron = kron_ref[...]
    field = mixed_to_table(received_rows(recv_ref), kron, second_ref[...], rows_ref, stack_ref)
    weighted = wide_ref[...] * field
    energy = jnp.sum(field * weighted)
    mixed = table_to_mixed(weighted, kron, second_t_ref[...], rows_ref, stack_ref)
    for j in range(3):
        put(send_ref, j, 4, tile_of(mixed, j))
    spread(send_ref, 3, 4, (energy, pick(sums_ref, 0), pick(sums_ref, 1)))


def third_column_kernel(
    recv_ref, lift_ref, keep_ref, scalar_ref, send_ref, out_scalar_ref, last_ref, mixed_ref
):
    zero = jnp.zeros((32, 128), f32)
    for r in range(ROWS):
        j, q = r // 4, r % 4
        last_ref[32 * r : 32 * r + 32, :] = unpack(recv_ref, j, 4, r, q, 0)
    energy, norm_next, bend = totals(recv_ref, 3, 4, 3)
    norm, step = pick(scalar_ref, 0), pick(scalar_ref, 1)
    ratio = norm_next / norm
    curve = energy + 0.1 * bend - ratio * norm_next / step
    step_next = norm_next / curve
    out_scalar_ref[...] = lanes((norm, step, ratio, step_next))
    lifted = mm(lift_ref[...], last_ref[...])
    keep = keep_ref[...]
    h_a, x_a = pltpu.roll(keep, 96, 1), pltpu.roll(keep, 32, 1)
    mixed_ref[...] = (
        h_a - step_next * (lifted + 0.1 * x_a) - (step_next * ratio / step) * (keep - h_a)
    )
    send_blocks(send_ref, 10, 0, mixed_ref, 0)


def gather_blocks(ref, count, base, out_ref, row):
    for j in range(10):
        rows = [ref[pl.ds(rho * count + base + j, 8, stride=4 * count), :] for rho in range(4)]
        for q in range(4):
            m = row + 4 * j + q
            merged = merge([move(rows[rho], q, rho) for rho in range(4)])
            out_ref[pl.ds(m // 8 * 64 + m % 8, 8, stride=8), :] = merged


def final_kernel(early_ref, late_ref, side_ref, scalar_ref, solution_ref, residual_ref, early, late):
    for block in range(3):
        gather_blocks(early_ref, 30, 10 * block, early, 40 * block)
    gather_blocks(late_ref, 10, 0, late, 0)
    step, ratio, step_next = pick(scalar_ref, 1), pick(scalar_ref, 2), pick(scalar_ref, 3)
    small = 0.1 * step
    side = side_ref[...]
    for tile in range(8):
        def take(ref, block):
            return jnp.concatenate(
                [ref[pl.ds((5 * block + t) * 64 + 8 * tile, 8), :] for t in range(5)], axis=0
            )
        h_0, h_a, y_1, h_r = take(early, 0), take(early, 1), take(early, 2), take(late, 0)
        right = jnp.concatenate(
            [(step + step_next * ratio) * h_0 + step_next * h_a, (-step_next * small) * h_0], axis=0
        )
        columns = slice(128 * tile, 128 * tile + 128)
        solution_ref[:, :, columns] = mm(side[:, 0:80], right).reshape(4, 32, 128)
        right = jnp.concatenate(
            [
                h_r,
                (-small * (1.0 + step_next * ratio / step)) * h_0
                - (0.1 * step_next) * (h_a - small * y_1),
                (0.1 * step_next * small) * h_0,
            ],
            axis=0,
        )
        residual_ref[:, :, columns] = mm(side[:, 0:120], right).reshape(4, 32, 128)


def call(kernel, outputs, scratch, *operands):
    smem = [pl.BlockSpec(memory_space=pltpu.VMEM)] * len(operands)
    if kernel is matrix_kernel:
        smem[0] = pl.BlockSpec(memory_space=pltpu.SMEM)
    return pl.pallas_call(
        kernel,
        out_shape=[jax.ShapeDtypeStruct(shape, f32) for shape in outputs],
        in_specs=smem,
        out_specs=[pl.BlockSpec(memory_space=pltpu.VMEM)] * len(outputs),
        scratch_shapes=[pltpu.VMEM(shape, f32) for shape in scratch],
        compiler_params=pltpu.CompilerParams(vmem_limit_bytes=32 * 2**20),
    )(*operands)


def exchange(buffer):
    count = buffer.shape[0] // DEVICES
    shaped = buffer.reshape(DEVICES, count, 128) if count % 4 == 0 else buffer.reshape(DEVICES, 1, count * 128)
    moved = lax.all_to_all(shaped, ("slab", "grp"), 0, 0, tiled=True)
    return moved.reshape(buffer.shape)


def fast_program(
    photon_table,
    bin_weights,
    first_start,
    first_band,
    second_start,
    second_band,
    third_start,
    third_band,
    fourth_start,
    fourth_band,
):
    total = DEVICES * ROWS
    work = [(256, 128), (64, 384)]
    send, wide, kron, second, second_t = call(
        start_kernel,
        [(256, 128), (256, 256), (256, 128), (64, 32), (32, 64)],
        [(256, 256)] + work,
        photon_table, bin_weights, third_start, third_band, fourth_start, fourth_band,
    )
    recv = exchange(send)
    group = lax.axis_index("grp").reshape(1)
    gram, high, lift, side = call(
        matrix_kernel,
        [(2 * total, total), (2 * total, total), (K0 * N1, total), (128, 128)],
        [(total, 128), (total, 64)],
        group, first_start, first_band, second_start, second_band,
    )
    send, fields, images = call(
        first_column_kernel,
        [(128, 128), (total, 128), (total, 128)],
        [],
        recv, gram,
    )
    recv = exchange(send)
    send, scalars = call(
        first_row_kernel, [(256, 128), (8, 128)], work, recv, wide, kron, second, second_t
    )
    recv = exchange(send)
    send, blend, scalars = call(
        second_column_kernel,
        [(128, 128), (total, 128), (8, 128)],
        [(total, 128), (total, 128)],
        recv, gram, fields, images, scalars,
    )
    recv = exchange(send)
    early_send, keep, sums = call(
        middle_kernel,
        [(DEVICES * 30, 128), (K0 * N1, 128), (8, 128)],
        [],
        blend, gram, high, lift, scalars,
    )
    (send,) = call(
        second_row_kernel, [(128, 128)], work, recv, sums, wide, kron, second, second_t
    )
    early = exchange(early_send)
    recv = exchange(send)
    send, scalars = call(
        third_column_kernel,
        [(DEVICES * 10, 128), (8, 128)],
        [(total, 128), (K0 * N1, 128)],
        recv, lift, keep, scalars,
    )
    late = exchange(send)
    return call(
        final_kernel,
        [(4, 32, 1024), (4, 32, 1024)],
        [(960, 128), (320, 128)],
        early, late, side, scalars,
    )


def fits(mesh):
    return (mesh.shape["slab"], mesh.shape["grp"]) == (SLABS, GRPS)


def solution(mesh):
    placed = (
        P("slab", "grp", None),
        P("slab", "grp", None),
        P(),
        P(),
        P(),
        P(),
        P(),
        P(),
        P(),
        P(),
    )
    return jax.shard_map(
        fast_program if fits(mesh) else per_device,
        mesh=mesh,
        in_specs=placed,
        out_specs=(P("slab", "grp", None), P("slab", "grp", None)),
        check_vma=False,
    )
```

profile of v0, /device:TPU:0, one launch (start us, length us, event | category | flops | bytes accessed | tf_op | source)
XLA Modules:
  0.0 104.0 jit_solution(14336825712621357878)
XLA Ops:
  0.6 0.8 copy.21.band3_ref
  1.4 0.1 copy.20.band2_ref
  1.5 1.0 copy.18.table_ref
  2.6 0.6 copy-done.8
  3.2 0.0 copy-done.9
  3.2 2.1 %shard_map.113 = (f32[256,128]{1,0:T(8,128)}, f32[256,256]{1,0:T(8,128)S(1)}, f32[256,128]{1,0:T(8,128)S(1)}, f32[64,32]{1,0:T(8,128)S(1)}, f32[32,64]{1,0:T(8,128)S(1)}) custom-call(f32[2,5,3200]{2,1,0:T(8,128)S(1)} %copy.18.table_ref, f32[2,5,3200]{2,1,0:T(8,128)S(1)} %copy.19.weight_ref, s32[64]{0:T(128)S(1)} %copy-done.8, f32[64,4]{1,0:T(8,128)S(1)} %copy.20.band2_ref, ...), custom_call_target="tpu_custom_call" | custom-call | tf_op jit(solution)/shard_map/pallas_call | solution.py:661
  5.3 7.3 %all-to-all-start = ((f32[32,8,128]{2,1,0:T(8,128)}), f32[32,8,128]{2,1,0:T(8,128)S(1)}, u32[]{:S(2)}, u32[]{:S(2)}) async-start(f32[32,8,128]{2,1,0:T(8,128)} %bitcast), calls=%async_computation | async-start | bytes 262144 | tf_op jit(solution)/shard_map/all_to_all | solution.py:674
  12.6 0.7 copy-done.14
  13.3 0.1 copy.23.band1_ref
  13.4 0.6 copy-done.15
  14.0 0.1 copy.22.band0_ref
  14.1 0.7 copy-done.10
  14.7 6.4 %shard_map.114 = (f32[640,320]{1,0:T(8,128)S(1)}, f32[640,320]{1,0:T(8,128)S(1)}, f32[640,320]{1,0:T(8,128)S(1)}, f32[128,128]{1,0:T(8,128)S(1)}) custom-call(s32[1]{0:T(128)} %bitcast.2.group_ref, s32[32]{0:T(128)S(1)} %copy-done.10, f32[32,4]{1,0:T(8,128)S(1)} %copy.22.band0_ref, s32[10]{0:T(128)S(1)} %copy-done.11, f32[10,4]{1,0:T(8,128)S(1)} %copy.23.band1_ref), custom_call_target="tpu_custom_call" | custom-call | tf_op jit(solution)/shard_map/pallas_call | solution.py:661
  21.2 0.6 copy-done.6
  21.8 1.4 %shard_map.115 = (f32[128,128]{1,0:T(8,128)S(1)}, f32[320,128]{1,0:T(8,128)S(1)}, f32[320,128]{1,0:T(8,128)S(1)}) custom-call(f32[256,128]{1,0:T(8,128)S(1)} %bitcast.17, f32[640,320]{1,0:T(8,128)S(1)} %get-tuple-element.25.gram_ref), custom_call_target="tpu_custom_call" | custom-call | tf_op jit(solution)/shard_map/pallas_call | solution.py:661
  23.1 13.0 %all_to_all.35 = f32[32,4,128]{2,1,0:T(4,128)S(1)} all-to-all(f32[32,4,128]{2,1,0:T(4,128)S(1)} %bitcast.26), channel_id=1, replica_groups=mesh['slab'=16,'grp'=2] {'slab','grp'}, dimensions={0} | all-to-all | bytes 131072 | tf_op jit(solution)/shard_map/all_to_all | solution.py:674
  36.2 1.7 %shard_map.116 = (f32[256,128]{1,0:T(8,128)S(1)}, f32[8,128]{1,0:T(8,128)S(1)}) custom-call(f32[128,128]{1,0:T(8,128)S(1)} %bitcast.22, f32[256,256]{1,0:T(8,128)S(1)} %get-tuple-element.27.wide_ref, f32[256,128]{1,0:T(8,128)S(1)} %get-tuple-element.28.kron_ref, f32[64,32]{1,0:T(8,128)S(1)} %get-tuple-element.29.second_ref, ...), custom_call_target="tpu_custom_call" | custom-call | tf_op jit(solution)/shard_map/pallas_call | solution.py:661
  37.9 9.9 %all_to_all.36 = f32[32,8,128]{2,1,0:T(8,128)S(1)} all-to-all(f32[32,8,128]{2,1,0:T(8,128)S(1)} %bitcast.25), channel_id=1, replica_groups=mesh['slab'=16,'grp'=2] {'slab','grp'}, dimensions={0} | all-to-all | bytes 262144 | tf_op jit(solution)/shard_map/all_to_all | solution.py:674
  47.8 1.4 %shard_map.117 = (f32[128,128]{1,0:T(8,128)}, f32[320,128]{1,0:T(8,128)S(1)}, f32[8,128]{1,0:T(8,128)S(1)}) custom-call(f32[256,128]{1,0:T(8,128)S(1)} %bitcast.18, f32[640,320]{1,0:T(8,128)S(1)} %get-tuple-element.25.gram_ref, f32[320,128]{1,0:T(8,128)S(1)} %get-tuple-element.32.fields_ref, f32[320,128]{1,0:T(8,128)S(1)} %get-tuple-element.33.images_ref, ...), custom_call_target="tpu_custom_call" | custom-call | tf_op jit(solution)/shard_map/pallas_call | solution.py:661
  49.2 0.7 copy-done.4
  49.9 2.6 %all-to-all-start.4 = ((f32[32,4,128]{2,1,0:T(4,128)}), f32[32,4,128]{2,1,0:T(4,128)S(1)}, u32[]{:S(2)}, u32[]{:S(2)}) async-start(f32[32,4,128]{2,1,0:T(4,128)} %bitcast.9), calls=%async_computation.4 | async-start | bytes 131072 | tf_op jit(solution)/shard_map/all_to_all | solution.py:674
  52.5 0.9 copy-done.5
  53.4 3.4 %shard_map.118 = (f32[960,128]{1,0:T(8,128)S(1)}, f32[640,128]{1,0:T(8,128)S(1)}, f32[8,128]{1,0:T(8,128)S(1)}) custom-call(f32[320,128]{1,0:T(8,128)S(1)} %copy-done.5, f32[640,320]{1,0:T(8,128)S(1)} %get-tuple-element.25.gram_ref, f32[640,320]{1,0:T(8,128)S(1)} %get-tuple-element.36.high_ref, f32[640,320]{1,0:T(8,128)S(1)} %get-tuple-element.37.lift_ref, ...), custom_call_target="tpu_custom_call" | custom-call | tf_op jit(solution)/shard_map/pallas_call | solution.py:661
  56.7 0.8 copy-done
  57.5 0.7 copy-done.2
  58.2 1.6 %all-to-all-done.4 = f32[32,4,128]{2,1,0:T(4,128)S(1)} async-done(((f32[32,4,128]{2,1,0:T(4,128)}), f32[32,4,128]{2,1,0:T(4,128)S(1)}, u32[]{:S(2)}, u32[]{:S(2)}) %all-to-all-start.4) | async-done | bytes 65568 | tf_op jit(solution)/shard_map/all_to_all | solution.py:674
  59.9 1.6 %shard_map.119 = f32[128,128]{1,0:T(8,128)S(1)} custom-call(f32[128,128]{1,0:T(8,128)S(1)} %bitcast.20, f32[8,128]{1,0:T(8,128)S(1)} %get-tuple-element.41.sums_ref, f32[256,256]{1,0:T(8,128)S(1)} %get-tuple-element.27.wide_ref, f32[256,128]{1,0:T(8,128)S(1)} %get-tuple-element.28.kron_ref, f32[64,32]{1,0:T(8,128)S(1)} %get-tuple-element.29.second_ref, ...), custom_call_target="tpu_custom_call" | custom-call | tf_op jit(solution)/shard_map/pallas_call | solution.py:661
  61.5 11.6 %all_to_all.37 = f32[32,4,128]{2,1,0:T(4,128)S(1)} all-to-all(f32[32,4,128]{2,1,0:T(4,128)S(1)} %bitcast.21), channel_id=1, replica_groups=mesh['slab'=16,'grp'=2] {'slab','grp'}, dimensions={0} | all-to-all | bytes 131072 | tf_op jit(solution)/shard_map/all_to_all | solution.py:674
  73.1 1.2 %shard_map.120 = (f32[320,128]{1,0:T(8,128)S(1)}, f32[8,128]{1,0:T(8,128)S(1)}) custom-call(f32[128,128]{1,0:T(8,128)S(1)} %bitcast.23, f32[640,320]{1,0:T(8,128)S(1)} %get-tuple-element.37.lift_ref, f32[640,128]{1,0:T(8,128)S(1)} %copy-done.3, f32[8,128]{1,0:T(8,128)S(1)} %get-tuple-element.38.scalar_ref), custom_call_target="tpu_custom_call" | custom-call | tf_op jit(solution)/shard_map/pallas_call | solution.py:661
  74.3 10.3 %all_to_all.38 = f32[32,1,1280]{2,1,0:T(1,128)S(1)} all-to-all(f32[32,1,1280]{2,1,0:T(1,128)S(1)} %bitcast.24), channel_id=1, replica_groups=mesh['slab'=16,'grp'=2] {'slab','grp'}, dimensions={0} | all-to-all | bytes 327680 | tf_op jit(solution)/shard_map/all_to_all | solution.py:674
  84.6 17.0 %all_to_all.39 = f32[32,1,3840]{2,1,0:T(1,128)S(1)} all-to-all(f32[32,1,3840]{2,1,0:T(1,128)S(1)} %bitcast.19), channel_id=1, replica_groups=mesh['slab'=16,'grp'=2] {'slab','grp'}, dimensions={0} | all-to-all | bytes 983040 | tf_op jit(solution)/shard_map/all_to_all | solution.py:674
  101.5 2.5 %shard_map.121 = (f32[4,32,1024]{2,1,0:T(8,128)}, f32[4,32,1024]{2,1,0:T(8,128)}) custom-call(f32[960,128]{1,0:T(8,128)S(1)} %bitcast.15, f32[320,128]{1,0:T(8,128)S(1)} %bitcast.16, f32[128,128]{1,0:T(8,128)S(1)} %copy-done.7, f32[8,128]{1,0:T(8,128)S(1)} %get-tuple-element.45.scalar_ref), custom_call_target="tpu_custom_call" | custom-call | tf_op jit(solution)/shard_map/pallas_call | solution.py:661
  (24 shorter events, 0.1 us)
Async XLA Ops:
  0.6 0.8 copy-start.13
  1.5 1.0 copy-start.12
  2.5 0.7 copy-start.8
  2.5 0.7 copy-start.9
  5.3 16.5 %all-to-all-start = ((f32[32,8,128]{2,1,0:T(8,128)}), f32[32,8,128]{2,1,0:T(8,128)S(1)}, u32[]{:S(2)}, u32[]{:S(2)}) async-start(f32[32,8,128]{2,1,0:T(8,128)} %bitcast), calls=%async_computation | async-start | bytes 262144 | tf_op jit(solution)/shard_map/all_to_all | solution.py:674
  12.6 0.7 copy-start.14
  13.3 0.7 copy-start.15
  14.1 0.7 copy-start.10
  14.1 0.7 copy-start.11
  21.1 0.6 copy-start.6
  49.2 0.7 copy-start.4
  49.9 10.0 %all-to-all-start.4 = ((f32[32,4,128]{2,1,0:T(4,128)}), f32[32,4,128]{2,1,0:T(4,128)S(1)}, u32[]{:S(2)}, u32[]{:S(2)}) async-start(f32[32,4,128]{2,1,0:T(4,128)} %bitcast.9), calls=%async_computation.4 | async-start | bytes 131072 | tf_op jit(solution)/shard_map/all_to_all | solution.py:674
  52.4 0.9 copy-start.5
  56.7 0.8 copy-start
  57.5 0.7 copy-start.2
  59.9 13.2 %copy-start.3 = (f32[640,128]{1,0:T(8,128)S(1)}, f32[640,128]{1,0:T(8,128)}, u32[]{:S(2)}) copy-start(f32[640,128]{1,0:T(8,128)} %copy-done.2) | copy-start | bytes 983044
  73.1 11.5 %copy-start.1 = (f32[960,128]{1,0:T(8,128)S(1)}, f32[960,128]{1,0:T(8,128)}, u32[]{:S(2)}) copy-start(f32[960,128]{1,0:T(8,128)} %copy-done) | copy-start | bytes 1474564
  84.6 17.0 %copy-start.7 = (f32[128,128]{1,0:T(8,128)S(1)}, f32[128,128]{1,0:T(8,128)}, u32[]{:S(2)}) copy-start(f32[128,128]{1,0:T(8,128)} %copy-done.6) | copy-start | bytes 196612
where the time goes:
time: 104 us
  blocking collectives  61.8 us (59%)
  Pallas kernels  21.6 us (21%)
  starting transfers between devices  9.85 us (9%)
  local copies, waits for them, and re-layouts  8.33 us (8%)
  waiting for transfers between devices  1.62 us (2%)
    all_to_all x5, blocking collectives, exchange(): moved = lax.all_to_all(shaped, ('slab', 'grp'), 0, 0, tiled=True)  61.8 us
    pallas_call x9, Pallas kernels, call(): pl.pallas_call(kernel, out_shape=[jax.ShapeDtypeStruct(shape, f32) for sh...  21.6 us
    all_to_all x2, starting transfers between devices, exchange(): moved = lax.all_to_all(shaped, ('slab', 'grp'), 0, 0, tiled=True)  9.85 us
    unnamed x38, local copies, waits for them, and re-layouts  8.33 us
  transfers between devices with their start and end apart: 2, of which 1 were waited for; matrix products, arithmetic and copies ran while one was open for 0% of the time, Pallas kernels for 9%

commit v1 on v0

--- a/solution.py
+++ b/solution.py
@@ -156,6 +156,7 @@
 N0, N1 = 32, 10
 HI = lax.Precision.HIGHEST
 f32 = jnp.float32
+JOINT = 19
 
 
 def iota(shape, dim):
@@ -186,33 +187,29 @@
 
 
 def slot(r):
-    return 8 * (r // L1) + r % L1
-
-
-def banded(start_ref, band_ref, width, wrap):
+    return L0 * (r % L1) + r // L1
+
+
+def banded_t(start_ref, band_ref, width, wrap):
     n = start_ref.shape[0]
-    row = start_ref[...].reshape(1, n)
-    eye = iota((n, n), 0) == iota((n, n), 1)
-    start = jnp.sum(jnp.where(eye, row.astype(f32), 0.0), axis=1, keepdims=True)
-    relative = (iota((n, width), 1) % wrap) - start.astype(jnp.int32)
-    band = band_ref[...]
-    out = jnp.zeros((n, width), f32)
+    relative = (iota((width, n), 0) % wrap) - start_ref[...].reshape(1, n)
+    out = jnp.zeros((width, n), f32)
     for offset in range(4):
-        out = out + jnp.where(relative == offset, band[:, offset : offset + 1], 0.0)
+        out = out + jnp.where(relative == offset, band_ref[offset : offset + 1, :], 0.0)
     return out
 
 
-def expand(ref, a, p):
+def expand(ref, p):
     first = 200 * p
     tile, off = first // 128, first % 128
-    lane = iota((L1, 128), 1)
+    lane = iota((16, 128), 1)
 
     def window(t):
-        low = ref[a, :, t * 128 : (t + 1) * 128]
+        low = ref[:, t * 128 : (t + 1) * 128]
         if off == 0:
             return low
         t1 = min(t + 1, 24)
-        high = ref[a, :, t1 * 128 : (t1 + 1) * 128]
+        high = ref[:, t1 * 128 : (t1 + 1) * 128]
         return jnp.where(
             lane < 128 - off, pltpu.roll(low, 128 - off, 1), pltpu.roll(high, 128 - off, 1)
         )
@@ -301,32 +298,32 @@
 
 def start_kernel(
     table_ref, weight_ref, start2_ref, band2_ref, start3_ref, band3_ref,
-    send_ref, wide_ref, kron_ref, second_ref, second_t_ref, field_ref, rows_ref, stack_ref,
-):
-    fourth = banded(start3_ref, band3_ref, 128, 32)
+    send_ref, wide_ref, kron_ref, second_ref, second_t_ref,
+    product_ref, packed_ref, field_ref, rows_ref, stack_ref,
+):
+    fourth_t = banded_t(start3_ref, band3_ref, 128, 32)
     pick_bin = (iota((256, N3), 0) % N3 == iota((256, N3), 1)) & (iota((256, N3), 0) < 4 * N3)
-    kron = mm(jnp.where(pick_bin, 1.0, 0.0), fourth)
+    kron = mm_t(jnp.where(pick_bin, 1.0, 0.0), fourth_t)
     same = iota((256, 128), 0) // N3 == iota((256, 128), 1) // 32
     kron = jnp.where(same, kron, 0.0)
     kron_ref[...] = kron
-    third = banded(start2_ref, band2_ref, 32, 32)
-    order = iota((N2, N2), 0)
-    permute = (order % 16) * 4 + order // 16 == iota((N2, N2), 1)
-    second = mm(jnp.where(permute, 1.0, 0.0), third)
-    second_ref[...] = second
-    second_t = second.T
+    third_t = banded_t(start2_ref, band2_ref, 32, 32)
+    order = iota((N2, N2), 1)
+    permute = (order % 16) * 4 + order // 16 == iota((N2, N2), 0)
+    second_t = mm(third_t, jnp.where(permute, 1.0, 0.0))
     second_t_ref[...] = second_t
-    wide_ref[...] = jnp.zeros((256, 256), f32)
-    field_ref[...] = jnp.zeros((256, 256), f32)
+    second_ref[...] = second_t.T
+    packed_ref[8:16, :] = jnp.zeros((8, N2 * N3), f32)
+    product_ref[8:16, :] = jnp.zeros((8, N2 * N3), f32)
+    for b in range(L1):
+        weight = weight_ref[b]
+        packed_ref[L0 * b : L0 * b + L0, :] = weight
+        product_ref[L0 * b : L0 * b + L0, :] = weight * table_ref[b]
     for p in range(16):
-        for a in range(L0):
-            base = 16 * p + 8 * a
-            low, high = expand(weight_ref, a, p)
-            wide_ref[base : base + L1, 0:128] = low
-            wide_ref[base : base + L1, 128:256] = high
-            t_low, t_high = expand(table_ref, a, p)
-            field_ref[base : base + L1, 0:128] = t_low * low
-            field_ref[base : base + L1, 128:256] = t_high * high
+        for source, target in ((packed_ref, wide_ref), (product_ref, field_ref)):
+            low, high = expand(source, p)
+            target[16 * p : 16 * p + 16, 0:128] = low
+            target[16 * p : 16 * p + 16, 128:256] = high
     mixed = table_to_mixed(field_ref[...], kron, second_t, rows_ref, stack_ref)
     once = inner_penalty(mixed)
     twice = inner_penalty(once)
@@ -359,69 +356,105 @@
     return out
 
 
-def matrix_kernel(
-    group_ref, start0_ref, band0_ref, start1_ref, band1_ref,
-    gram_ref, high_ref, lift_ref, side_ref, rows0_ref, rows1_ref,
-):
-    first = banded(start0_ref, band0_ref, K0, K0)
-    second = banded(start1_ref, band1_ref, K1, K1)
-    penalty_matrix = pentadiagonal(K0)
-
-    def powers(basis):
-        out = [basis]
-        for _ in range(3):
-            out.append(mm(out[-1], penalty_matrix))
-        return out
-
+def powers(basis_t, count):
+    penalty_matrix = pentadiagonal(basis_t.shape[0])
+    out = [basis_t]
+    for _ in range(count - 1):
+        out.append(mm(penalty_matrix, out[-1]))
+    return out
+
+
+def select_first():
+    column = iota((N0, DEVICES * ROWS), 1)
+    chosen = L0 * (column % 32 // GRPS) + column // 32 // L1 == iota((N0, DEVICES * ROWS), 0)
+    return jnp.where(chosen, 1.0, 0.0).astype(jnp.bfloat16)
+
+
+def gram_rows(start0_ref, band0_ref, start1_ref, band1_ref, rows0_ref, rows1_ref, count):
     total = DEVICES * ROWS
+    powers0 = powers(banded_t(start0_ref, band0_ref, K0, K0), count)
+    powers1 = powers(banded_t(start1_ref, band1_ref, K1, K1), count)
     row0 = iota((total, N0), 0)
-    pick0 = 2 * (row0 % 32 // 2) + row0 // 32 // L1 == iota((total, N0), 1)
+    pick0 = L0 * (row0 % 32 // GRPS) + row0 // 32 // L1 == iota((total, N0), 1)
     row1 = iota((total, N1), 0)
-    pick1 = L1 * (row1 % 2) + row1 // 32 % L1 == iota((total, N1), 1)
-    powers0, powers1 = powers(first), powers(second)
-    wide0 = mm(jnp.where(pick0, 1.0, 0.0), first)
-    wide1 = mm(jnp.where(pick1, 1.0, 0.0), second)
-    for k in range(4):
-        rows0_ref[:, 32 * k : 32 * k + 32] = mm_t(wide0, powers0[k])
-        rows1_ref[:, 16 * k : 16 * k + N1] = mm_t(wide1, powers1[k])
-    col0 = iota((N0, total), 1)
-    select0 = jnp.where(
-        2 * (col0 % 32 // 2) + col0 // 32 // L1 == iota((N0, total), 0), 1.0, 0.0
-    ).astype(jnp.bfloat16)
-    col1 = iota((N1, total), 1)
-    select1 = jnp.where(
-        L1 * (col1 % 2) + col1 // 32 % L1 == iota((N1, total), 0), 1.0, 0.0
-    ).astype(jnp.bfloat16)
+    pick1 = L1 * (row1 % GRPS) + row1 // 32 % L1 == iota((total, N1), 1)
+    wide0 = mm_t(jnp.where(pick0, 1.0, 0.0), powers0[0])
+    wide1 = mm_t(jnp.where(pick1, 1.0, 0.0), powers1[0])
+    for k in range(count):
+        rows0_ref[:, 32 * k : 32 * k + 32] = mm(wide0, powers0[k])
+        rows1_ref[:, 16 * k : 16 * k + N1] = mm(wide1, powers1[k])
+    column = iota((N1, total), 1)
+    chosen = L1 * (column % GRPS) + column // 32 % L1 == iota((N1, total), 0)
+    select0, select1 = select_first(), jnp.where(chosen, 1.0, 0.0).astype(jnp.bfloat16)
+
+    def block(base):
+        block0 = rows0_ref[pl.ds(base, 32), :]
+        block1 = rows1_ref[pl.ds(base, 32), :]
+        g = [choose(three_terms(block0[:, 32 * k : 32 * k + 32]), select0) for k in range(count)]
+        h = [choose(three_terms(block1[:, 16 * k : 16 * k + N1]), select1) for k in range(count)]
+        return g, h
+
+    return block
+
+
+def gram_kernel(start0_ref, band0_ref, start1_ref, band1_ref, gram_ref, rows0_ref, rows1_ref):
+    total = DEVICES * ROWS
+    block = gram_rows(start0_ref, band0_ref, start1_ref, band1_ref, rows0_ref, rows1_ref, 2)
 
     @pl.loop(0, ROWS)
     def _(step):
         base = pl.multiple_of(step * 32, 32)
-        block0 = rows0_ref[pl.ds(base, 32), :]
-        block1 = rows1_ref[pl.ds(base, 32), :]
-        g = [choose(three_terms(block0[:, 32 * k : 32 * k + 32]), select0) for k in range(4)]
-        h = [choose(three_terms(block1[:, 16 * k : 16 * k + N1]), select1) for k in range(4)]
+        g, h = block(base)
         gram_ref[pl.ds(base, 32), :] = g[0] * h[0]
         gram_ref[pl.ds(base + total, 32), :] = g[1] * h[0] + g[0] * h[1]
+
+
+def high_kernel(
+    after_ref, start0_ref, band0_ref, start1_ref, band1_ref, high_ref, rows0_ref, rows1_ref
+):
+    total = DEVICES * ROWS
+    block = gram_rows(start0_ref, band0_ref, start1_ref, band1_ref, rows0_ref, rows1_ref, 4)
+
+    @pl.loop(0, ROWS)
+    def _(step):
+        base = pl.multiple_of(step * 32, 32)
+        g, h = block(base)
         high_ref[pl.ds(base, 32), :] = g[2] * h[0] + 2.0 * g[1] * h[1] + g[0] * h[2]
         high_ref[pl.ds(base + total, 32), :] = (
             g[3] * h[0] + 3.0 * (g[2] * h[1] + g[1] * h[2]) + g[0] * h[3]
         )
 
-    lifted = choose(three_terms(first.T), select0)
+
+def lift_kernel(
+    after_ref, group_ref, start0_ref, band0_ref, start1_ref, band1_ref, lift_ref, side_ref
+):
+    total = DEVICES * ROWS
+    lifted = choose(three_terms(banded_t(start0_ref, band0_ref, K0, K0)), select_first())
     column = iota((K0, total), 1)
-    owner = L1 * (column % 2) + column // 32 % L1
+    owner = L1 * (column % GRPS) + column // 32 % L1
     for n in range(N1):
         lift_ref[K0 * n : K0 * n + K0, :] = jnp.where(owner == n, lifted, 0.0)
-
-    coef = iota((128, K1), 0) % 32 + 32 * group_ref[0]
+    group = group_ref[0]
+    coef = iota((128, K1), 0) % 32 + 32 * group
     pick_coef = jnp.where(coef == iota((128, K1), 1), 1.0, 0.0)
-    side_ref[...] = jnp.zeros((128, 128), f32)
-    spot = iota((N1, 128), 1)
-    for k in range(3):
-        own = mm_t(pick_coef, powers1[k])
+    half = iota((N1, N1), 1) // L1
+    wanted = L1 * jnp.where(half == group, 0, 1) + iota((N1, N1), 1) % L1
+    reorder = jnp.where(iota((N1, N1), 0) == wanted, 1.0, 0.0)
+    side_ref[...] = jnp.zeros((128, 256), f32)
+    for k, value in enumerate(powers(banded_t(start1_ref, band1_ref, K1, K1), 3)):
+        own = mm(pick_coef, value)
+        halves = mm(own, reorder)
         for alpha in range(4):
             rows = slice(32 * alpha, 32 * alpha + 32)
-            side_ref[rows, 40 * k + 10 * alpha : 40 * k + 10 * alpha + 10] = own[rows, :]
+            if k == 0:
+                side_ref[rows, 10 * alpha : 10 * alpha + 10] = own[rows, :]
+            for h in range(2):
+                piece = halves[rows, L1 * h : L1 * h + L1]
+                place = 40 * k + 20 * h + L1 * alpha
+                if k > 0:
+                    side_ref[rows, place : place + L1] = piece
+                if k < 2:
+                    side_ref[rows, 128 + place : 128 + place + L1] = piece
 
 
 def unpack(ref, row, count, r, source, target):
@@ -541,6 +574,17 @@
         merged = merge(parts)
         for g in range(GRPS):
             send_ref[pl.ds(g * count + base + j, 16, stride=2 * count), :] = merged
+
+
+def send_halves(send_ref, count, base, value_ref, block):
+    for g in range(GRPS):
+        for j in range(5):
+            parts = []
+            for q in range(4):
+                alpha, b = divmod(4 * j + q, L1)
+                row = K0 * (L1 * g + b) + alpha
+                parts.append(move(value_ref[pl.ds(row, 16, stride=4), :], block, q))
+            send_ref[pl.ds(g * count + base + j, 16, stride=2 * count), :] = merge(parts)
 
 
 def middle_kernel(blend_ref, gram_ref, high_ref, lift_ref, scalar_ref, send_ref, keep_ref, sums_ref):
@@ -576,11 +620,11 @@
     )
     keep_ref[...] = keep
     for block in range(3):
-        send_blocks(send_ref, 30, 10 * block, keep_ref, block)
+        send_halves(send_ref, JOINT, 4 + 5 * block, keep_ref, block)
 
 
 def second_row_kernel(
-    recv_ref, sums_ref, wide_ref, kron_ref, second_ref, second_t_ref,
+    early_ref, recv_ref, sums_ref, wide_ref, kron_ref, second_ref, second_t_ref,
     send_ref, rows_ref, stack_ref,
 ):
     kron = kron_ref[...]
@@ -589,8 +633,8 @@
     energy = jnp.sum(field * weighted)
     mixed = table_to_mixed(weighted, kron, second_t_ref[...], rows_ref, stack_ref)
     for j in range(3):
-        put(send_ref, j, 4, tile_of(mixed, j))
-    spread(send_ref, 3, 4, (energy, pick(sums_ref, 0), pick(sums_ref, 1)))
+        put(send_ref, j, JOINT, tile_of(mixed, j))
+    spread(send_ref, 3, JOINT, (energy, pick(sums_ref, 0), pick(sums_ref, 1)))
 
 
 def third_column_kernel(
@@ -599,8 +643,8 @@
     zero = jnp.zeros((32, 128), f32)
     for r in range(ROWS):
         j, q = r // 4, r % 4
-        last_ref[32 * r : 32 * r + 32, :] = unpack(recv_ref, j, 4, r, q, 0)
-    energy, norm_next, bend = totals(recv_ref, 3, 4, 3)
+        last_ref[32 * r : 32 * r + 32, :] = unpack(recv_ref, j, JOINT, r, q, 0)
+    energy, norm_next, bend = totals(recv_ref, 3, JOINT, 3)
     norm, step = pick(scalar_ref, 0), pick(scalar_ref, 1)
     ratio = norm_next / norm
     curve = energy + 0.1 * bend - ratio * norm_next / step
@@ -615,19 +659,22 @@
     send_blocks(send_ref, 10, 0, mixed_ref, 0)
 
 
-def gather_blocks(ref, count, base, out_ref, row):
-    for j in range(10):
-        rows = [ref[pl.ds(rho * count + base + j, 8, stride=4 * count), :] for rho in range(4)]
+def gather_blocks(ref, count, base, rows, out_ref, first):
+    for j in range(rows):
+        taken = [ref[pl.ds(rho * count + base + j, 8, stride=4 * count), :] for rho in range(4)]
         for q in range(4):
-            m = row + 4 * j + q
-            merged = merge([move(rows[rho], q, rho) for rho in range(4)])
+            m = first + 4 * j + q
+            merged = merge([move(taken[rho], q, rho) for rho in range(4)])
             out_ref[pl.ds(m // 8 * 64 + m % 8, 8, stride=8), :] = merged
 
 
-def final_kernel(early_ref, late_ref, side_ref, scalar_ref, solution_ref, residual_ref, early, late):
+def final_kernel(
+    own_ref, partner_ref, late_ref, side_ref, scalar_ref, solution_ref, residual_ref, early, late
+):
     for block in range(3):
-        gather_blocks(early_ref, 30, 10 * block, early, 40 * block)
-    gather_blocks(late_ref, 10, 0, late, 0)
+        for h, ref in enumerate((own_ref, partner_ref)):
+            gather_blocks(ref, JOINT, 4 + 5 * block, 5, early, 40 * block + 20 * h)
+    gather_blocks(late_ref, 10, 0, 10, late, 0)
     step, ratio, step_next = pick(scalar_ref, 1), pick(scalar_ref, 2), pick(scalar_ref, 3)
     small = 0.1 * step
     side = side_ref[...]
@@ -641,7 +688,7 @@
             [(step + step_next * ratio) * h_0 + step_next * h_a, (-step_next * small) * h_0], axis=0
         )
         columns = slice(128 * tile, 128 * tile + 128)
-        solution_ref[:, :, columns] = mm(side[:, 0:80], right).reshape(4, 32, 128)
+        solution_ref[:, :, columns] = mm(side[:, 128:208], right).reshape(4, 32, 128)
         right = jnp.concatenate(
             [
                 h_r,
@@ -654,24 +701,28 @@
         residual_ref[:, :, columns] = mm(side[:, 0:120], right).reshape(4, 32, 128)
 
 
-def call(kernel, outputs, scratch, *operands):
-    smem = [pl.BlockSpec(memory_space=pltpu.VMEM)] * len(operands)
-    if kernel is matrix_kernel:
-        smem[0] = pl.BlockSpec(memory_space=pltpu.SMEM)
+def call(kernel, outputs, scratch, *operands, aliases={}):
+    specs = [pl.BlockSpec(memory_space=pltpu.VMEM)] * len(operands)
+    if kernel in (high_kernel, lift_kernel):
+        specs[0] = pl.BlockSpec(memory_space=pl.ANY)
+    if kernel is lift_kernel:
+        specs[1] = pl.BlockSpec(memory_space=pltpu.SMEM)
     return pl.pallas_call(
         kernel,
         out_shape=[jax.ShapeDtypeStruct(shape, f32) for shape in outputs],
-        in_specs=smem,
+        in_specs=specs,
         out_specs=[pl.BlockSpec(memory_space=pltpu.VMEM)] * len(outputs),
         scratch_shapes=[pltpu.VMEM(shape, f32) for shape in scratch],
+        input_output_aliases=aliases,
         compiler_params=pltpu.CompilerParams(vmem_limit_bytes=32 * 2**20),
     )(*operands)
 
 
 def exchange(buffer):
     count = buffer.shape[0] // DEVICES
-    shaped = buffer.reshape(DEVICES, count, 128) if count % 4 == 0 else buffer.reshape(DEVICES, 1, count * 128)
-    moved = lax.all_to_all(shaped, ("slab", "grp"), 0, 0, tiled=True)
+    tiled = count == 4 or count % 8 == 0
+    shape = (DEVICES, count, 128) if tiled else (DEVICES, 1, count * 128)
+    moved = lax.all_to_all(buffer.reshape(shape), ("slab", "grp"), 0, 0, tiled=True)
     return moved.reshape(buffer.shape)
 
 
@@ -689,31 +740,32 @@
 ):
     total = DEVICES * ROWS
     work = [(256, 128), (64, 384)]
+    outer = (first_start, first_band.T, second_start, second_band.T)
     send, wide, kron, second, second_t = call(
         start_kernel,
         [(256, 128), (256, 256), (256, 128), (64, 32), (32, 64)],
-        [(256, 256)] + work,
-        photon_table, bin_weights, third_start, third_band, fourth_start, fourth_band,
+        [(16, N2 * N3), (16, N2 * N3), (256, 256)] + work,
+        photon_table.transpose(1, 0, 2),
+        bin_weights.transpose(1, 0, 2),
+        third_start, third_band.T, fourth_start, fourth_band.T,
+    )
+    recv = exchange(send)
+    (gram,) = call(gram_kernel, [(2 * total, total)], [(total, 64), (total, 32)], *outer)
+    send, fields, images = call(
+        first_column_kernel, [(128, 128), (total, 128), (total, 128)], [], recv, gram
+    )
+    recv = exchange(send)
+    (high,) = call(
+        high_kernel, [(2 * total, total)], [(total, 128), (total, 64)], images, *outer
+    )
+    send, scalars = call(
+        first_row_kernel, [(256, 128), (8, 128)], work, recv, wide, kron, second, second_t
     )
     recv = exchange(send)
     group = lax.axis_index("grp").reshape(1)
-    gram, high, lift, side = call(
-        matrix_kernel,
-        [(2 * total, total), (2 * total, total), (K0 * N1, total), (128, 128)],
-        [(total, 128), (total, 64)],
-        group, first_start, first_band, second_start, second_band,
-    )
-    send, fields, images = call(
-        first_column_kernel,
-        [(128, 128), (total, 128), (total, 128)],
-        [],
-        recv, gram,
-    )
-    recv = exchange(send)
-    send, scalars = call(
-        first_row_kernel, [(256, 128), (8, 128)], work, recv, wide, kron, second, second_t
-    )
-    recv = exchange(send)
+    lift, side = call(
+        lift_kernel, [(K0 * N1, total), (128, 256)], [], scalars, group, *outer
+    )
     send, blend, scalars = call(
         second_column_kernel,
         [(128, 128), (total, 128), (8, 128)],
@@ -721,17 +773,21 @@
         recv, gram, fields, images, scalars,
     )
     recv = exchange(send)
-    early_send, keep, sums = call(
+    send, keep, sums = call(
         middle_kernel,
-        [(DEVICES * 30, 128), (K0 * N1, 128), (8, 128)],
+        [(DEVICES * JOINT, 128), (K0 * N1, 128), (8, 128)],
         [],
         blend, gram, high, lift, scalars,
     )
     (send,) = call(
-        second_row_kernel, [(128, 128)], work, recv, sums, wide, kron, second, second_t
-    )
-    early = exchange(early_send)
+        second_row_kernel,
+        [(DEVICES * JOINT, 128)],
+        work,
+        send, recv, sums, wide, kron, second, second_t,
+        aliases={0: 0},
+    )
     recv = exchange(send)
+    partner = lax.ppermute(recv, "grp", [(0, 1), (1, 0)])
     send, scalars = call(
         third_column_kernel,
         [(DEVICES * 10, 128), (8, 128)],
@@ -743,7 +799,7 @@
         final_kernel,
         [(4, 32, 1024), (4, 32, 1024)],
         [(960, 128), (320, 128)],
-        early, late, side, scalars,
+        recv, partner, late, side, scalars,
     )
 
 

time: 104 us -> 92.5 us (0.89)
  blocking collectives: 61.8 us -> 36.7 us
  waiting for transfers between devices: 1.62 us -> 11.8 us
  Pallas kernels: 21.6 us -> 26.8 us
  local copies, waits for them, and re-layouts: 8.33 us -> 3.14 us
  starting transfers between devices: 9.85 us -> 12.8 us
    all_to_all x5 -> x3, blocking collectives: 61.8 us -> 36.7 us  [exchange(): lax.all_to_all(buffer.reshape(shape), ('slab', 'grp'), 0, 0, tiled=True)]
    all_to_all x2 -> x3, waiting for transfers between devices: 1.62 us -> 10.3 us  [exchange(): lax.all_to_all(buffer.reshape(shape), ('slab', 'grp'), 0, 0, tiled=True)]
    pallas_call x9 -> x11, Pallas kernels: 21.6 us -> 26.8 us  [call(): pl.pallas_call(kernel, out_shape=[jax.ShapeDtypeStruct(shape, f32) for sh...]
    unnamed x38 -> x20, local copies, waits for them, and re-layouts: 8.33 us -> 3.14 us
    all_to_all x2 -> x3, starting transfers between devices: 9.85 us -> 12.6 us  [exchange(): lax.all_to_all(buffer.reshape(shape), ('slab', 'grp'), 0, 0, tiled=True)]
    ppermute x0 -> x1, waiting for transfers between devices: none -> 1.49 us  [fast_program(): partner = lax.ppermute(recv, 'grp', [(0, 1), (1, 0)])]
  transfers between devices with their start and end apart: 2 -> 4, of which waited for: 1 -> 3; matrix products, arithmetic and copies ran while one was open for 0% -> 0% of each run, Pallas kernels for 9% -> 16%
where the time goes in v1:
time: 92.5 us; the launch traced here: 92.1 us
  blocking collectives  36.7 us (40%)
  Pallas kernels  26.8 us (29%)
  starting transfers between devices  12.8 us (14%)
  waiting for transfers between devices  11.8 us (13%)
  local copies, waits for them, and re-layouts  3.14 us (3%)
    all_to_all x3, blocking collectives, exchange(): lax.all_to_all(buffer.reshape(shape), ('slab', 'grp'), 0, 0, tiled=True)  36.7 us
    pallas_call x11, Pallas kernels, call(): pl.pallas_call(kernel, out_shape=[jax.ShapeDtypeStruct(shape, f32) for sh...  26.8 us
    all_to_all x3, starting transfers between devices, exchange(): lax.all_to_all(buffer.reshape(shape), ('slab', 'grp'), 0, 0, tiled=True)  12.6 us
    all_to_all x3, waiting for transfers between devices, exchange(): lax.all_to_all(buffer.reshape(shape), ('slab', 'grp'), 0, 0, tiled=True)  10.3 us
    unnamed x20, local copies, waits for them, and re-layouts  3.14 us
  transfers between devices with their start and end apart: 4, of which 3 were waited for; matrix products, arithmetic and copies ran while one was open for 0% of the time, Pallas kernels for 16%

profile of v1, /device:TPU:0, one launch (start us, length us, event | category | flops | bytes accessed | tf_op | source)
XLA Modules:
  0.0 92.1 jit_solution(5140114384912087726)
XLA Ops:
  0.6 0.0 copy-start.7
  0.7 0.6 copy-done.7
  1.3 0.0 copy-done.6
  1.3 0.9 copy-done
  2.2 0.9 copy-done.1
  3.1 2.1 %shard_map.113 = (f32[256,128]{1,0:T(8,128)}, f32[256,256]{1,0:T(8,128)S(1)}, f32[256,128]{1,0:T(8,128)S(1)}, f32[64,32]{1,0:T(8,128)S(1)}, f32[32,64]{1,0:T(8,128)S(1)}) custom-call(f32[5,2,3200]{2,1,0:T(2,128)S(1)} %bitcast.29, f32[5,2,3200]{2,1,0:T(2,128)S(1)} %bitcast.30, s32[64]{0:T(128)S(1)} %copy-done.8, f32[4,64]{1,0:T(4,128)S(1)} %bitcast.38, ...), custom_call_target="tpu_custom_call" | custom-call | tf_op jit(solution)/shard_map/pallas_call | solution.py:710
  5.2 7.3 %all-to-all-start = ((f32[32,8,128]{2,1,0:T(8,128)}), f32[32,8,128]{2,1,0:T(8,128)S(1)}, u32[]{:S(2)}, u32[]{:S(2)}) async-start(f32[32,8,128]{2,1,0:T(8,128)} %bitcast.4), calls=%async_computation | async-start | bytes 262144 | tf_op jit(solution)/shard_map/all_to_all | solution.py:725
  12.5 0.0 copy-start.2
  12.6 0.0 copy-start.4
  12.6 0.0 copy-start.5
  12.6 0.6 copy-done.2
  13.2 0.0 copy-done.4
  13.2 4.1 %shard_map.114.gram_ref = f32[640,320]{1,0:T(8,128)S(1)} custom-call(s32[32]{0:T(128)S(1)} %copy-done.4, f32[4,32]{1,0:T(4,128)S(1)} %bitcast.32, s32[10]{0:T(128)S(1)} %copy-done.5, f32[4,10]{1,0:T(4,128)S(1)} %bitcast.35), custom_call_target="tpu_custom_call" | custom-call | tf_op jit(solution)/shard_map/pallas_call | solution.py:710
  17.4 3.4 %all-to-all-done = f32[32,8,128]{2,1,0:T(8,128)S(1)} async-done(((f32[32,8,128]{2,1,0:T(8,128)}), f32[32,8,128]{2,1,0:T(8,128)S(1)}, u32[]{:S(2)}, u32[]{:S(2)}) %all-to-all-start) | async-done | bytes 131104 | tf_op jit(solution)/shard_map/all_to_all | solution.py:725
  20.8 1.4 %shard_map.115 = (f32[128,128]{1,0:T(8,128)S(1)}, f32[320,128]{1,0:T(8,128)S(1)}, f32[320,128]{1,0:T(8,128)S(1)}) custom-call(f32[256,128]{1,0:T(8,128)S(1)} %bitcast.24, f32[640,320]{1,0:T(8,128)S(1)} %shard_map.114.gram_ref), custom_call_target="tpu_custom_call" | custom-call | tf_op jit(solution)/shard_map/pallas_call | solution.py:710
  22.1 9.6 %all_to_all.30 = f32[32,4,128]{2,1,0:T(4,128)S(1)} all-to-all(f32[32,4,128]{2,1,0:T(4,128)S(1)} %bitcast.31), channel_id=1, replica_groups=mesh['slab'=16,'grp'=2] {'slab','grp'}, dimensions={0} | all-to-all | bytes 131072 | tf_op jit(solution)/shard_map/all_to_all | solution.py:725
  31.8 1.7 %shard_map.116 = (f32[256,128]{1,0:T(8,128)S(1)}, f32[8,128]{1,0:T(8,128)S(1)}) custom-call(f32[128,128]{1,0:T(8,128)S(1)} %bitcast.27, f32[256,256]{1,0:T(8,128)S(1)} %get-tuple-element.24.wide_ref, f32[256,128]{1,0:T(8,128)S(1)} %get-tuple-element.25.kron_ref, f32[64,32]{1,0:T(8,128)S(1)} %get-tuple-element.26.second_ref, ...), custom_call_target="tpu_custom_call" | custom-call | tf_op jit(solution)/shard_map/pallas_call | solution.py:710
  33.5 9.9 %all_to_all.31 = f32[32,8,128]{2,1,0:T(8,128)S(1)} all-to-all(f32[32,8,128]{2,1,0:T(8,128)S(1)} %bitcast.28), channel_id=1, replica_groups=mesh['slab'=16,'grp'=2] {'slab','grp'}, dimensions={0} | all-to-all | bytes 262144 | tf_op jit(solution)/shard_map/all_to_all | solution.py:725
  43.4 1.4 %shard_map.117 = (f32[128,128]{1,0:T(8,128)}, f32[320,128]{1,0:T(8,128)S(1)}, f32[8,128]{1,0:T(8,128)S(1)}) custom-call(f32[256,128]{1,0:T(8,128)S(1)} %bitcast.25, f32[640,320]{1,0:T(8,128)S(1)} %shard_map.114.gram_ref, f32[320,128]{1,0:T(8,128)S(1)} %get-tuple-element.29.fields_ref, f32[320,128]{1,0:T(8,128)S(1)} %get-tuple-element.30.images_ref.after_ref, ...), custom_call_target="tpu_custom_call" | custom-call | tf_op jit(solution)/shard_map/pallas_call | solution.py:710
  44.8 2.8 %all-to-all-start.3 = ((f32[32,4,128]{2,1,0:T(4,128)}), f32[32,4,128]{2,1,0:T(4,128)S(1)}, u32[]{:S(2)}, u32[]{:S(2)}) async-start(f32[32,4,128]{2,1,0:T(4,128)} %bitcast.13), calls=%async_computation.3 | async-start | bytes 131072 | tf_op jit(solution)/shard_map/all_to_all | solution.py:725
  47.6 5.8 %shard_map.118.high_ref = f32[640,320]{1,0:T(8,128)S(1)} custom-call(f32[320,128]{1,0:T(8,128)S(1)} %get-tuple-element.30.images_ref.after_ref, s32[32]{0:T(128)S(1)} %copy-done.4, f32[4,32]{1,0:T(4,128)S(1)} %bitcast.33, s32[10]{0:T(128)S(1)} %copy-done.5, f32[4,10]{1,0:T(4,128)S(1)} %bitcast.36), custom_call_target="tpu_custom_call" | custom-call | tf_op jit(solution)/shard_map/pallas_call | solution.py:710
  53.4 1.0 %shard_map.119 = (f32[640,320]{1,0:T(8,128)S(1)}, f32[128,256]{1,0:T(8,128)S(1)}) custom-call(f32[8,128]{1,0:T(8,128)S(1)} %get-tuple-element.31.scalar_ref.after_ref, s32[1]{0:T(128)} %bitcast.12.group_ref, s32[32]{0:T(128)S(1)} %copy-done.4, f32[4,32]{1,0:T(4,128)S(1)} %bitcast.34, s32[10]{0:T(128)S(1)} %copy-done.5, f32[4,10]{1,0:T(4,128)S(1)} %bitcast.37), custom_call_target="tpu_custom_call" | custom-call | tf_op jit(solution)/shard_map/pallas_call | solution.py:710
  54.4 3.4 %shard_map.120 = (f32[608,128]{1,0:T(8,128)S(1)}, f32[640,128]{1,0:T(8,128)S(1)}, f32[8,128]{1,0:T(8,128)S(1)}) custom-call(f32[320,128]{1,0:T(8,128)S(1)} %get-tuple-element.32.blend_ref, f32[640,320]{1,0:T(8,128)S(1)} %shard_map.114.gram_ref, f32[640,320]{1,0:T(8,128)S(1)} %shard_map.118.high_ref, f32[640,320]{1,0:T(8,128)S(1)} %get-tuple-element.33.lift_ref, ...), custom_call_target="tpu_custom_call" | custom-call | tf_op jit(solution)/shard_map/pallas_call | solution.py:710
  57.8 0.0 all-to-all-done.3
  57.9 1.6 %shard_map.121 = f32[608,128]{1,0:T(8,128)S(1)} custom-call(f32[608,128]{1,0:T(8,128)S(1)} %get-tuple-element.35.early_ref, f32[128,128]{1,0:T(8,128)S(1)} %bitcast.26, f32[8,128]{1,0:T(8,128)S(1)} %get-tuple-element.37.sums_ref, f32[256,256]{1,0:T(8,128)S(1)} %get-tuple-element.24.wide_ref, ...), custom_call_target="tpu_custom_call", output_to_operand_aliasing={{}: (0, {})} | custom-call | tf_op jit(solution)/shard_map/pallas_call | solution.py:710
  59.5 17.2 %all_to_all.32 = f32[32,1,2432]{2,1,0:T(1,128)S(1)} all-to-all(f32[32,1,2432]{2,1,0:T(1,128)S(1)} %bitcast.22), channel_id=1, replica_groups=mesh['slab'=16,'grp'=2] {'slab','grp'}, dimensions={0} | all-to-all | bytes 622592 | tf_op jit(solution)/shard_map/all_to_all | solution.py:725
  76.6 1.8 %shard_map.122 = (f32[320,128]{1,0:T(8,128)}, f32[8,128]{1,0:T(8,128)S(1)}) custom-call(f32[608,128]{1,0:T(8,128)S(1)} %bitcast.19, f32[640,320]{1,0:T(8,128)S(1)} %get-tuple-element.33.lift_ref, f32[640,128]{1,0:T(8,128)S(1)} %get-tuple-element.38.keep_ref, f32[8,128]{1,0:T(8,128)S(1)} %get-tuple-element.34.scalar_ref), custom_call_target="tpu_custom_call" | custom-call | tf_op jit(solution)/shard_map/pallas_call | solution.py:710
  78.5 2.6 %all-to-all-start.5 = ((f32[32,1,1280]{2,1,0:T(1,128)}), f32[32,1,1280]{2,1,0:T(1,128)S(1)}, u32[]{:S(2)}, u32[]{:S(2)}) async-start(f32[32,1,1280]{2,1,0:T(1,128)} %bitcast.17), calls=%async_computation.5 | async-start | bytes 327680 | tf_op jit(solution)/shard_map/all_to_all | solution.py:725
  81.0 0.2 collective-permute-start
  81.2 1.5 %collective-permute-done.partner_ref = f32[608,128]{1,0:T(8,128)S(1)} collective-permute-done((f32[608,128]{1,0:T(8,128)S(1)}, f32[608,128]{1,0:T(8,128)S(1)}, u32[]{:S(2)}, u32[]{:S(2)}) %collective-permute-start) | collective-permute-done | bytes 311328 | tf_op jit(solution)/shard_map/ppermute | solution.py:790
  82.7 6.9 %all-to-all-done.5 = f32[32,1,1280]{2,1,0:T(1,128)S(1)} async-done(((f32[32,1,1280]{2,1,0:T(1,128)}), f32[32,1,1280]{2,1,0:T(1,128)S(1)}, u32[]{:S(2)}, u32[]{:S(2)}) %all-to-all-start.5) | async-done | bytes 163872 | tf_op jit(solution)/shard_map/all_to_all | solution.py:725
  89.6 2.5 %shard_map.123 = (f32[4,32,1024]{2,1,0:T(8,128)}, f32[4,32,1024]{2,1,0:T(8,128)}) custom-call(f32[608,128]{1,0:T(8,128)S(1)} %bitcast.21, f32[608,128]{1,0:T(8,128)S(1)} %collective-permute-done.partner_ref, f32[320,128]{1,0:T(8,128)S(1)} %bitcast.23, f32[128,256]{1,0:T(8,128)S(1)} %get-tuple-element.40.side_ref, f32[8,128]{1,0:T(8,128)S(1)} %get-tuple-element.41.scalar_ref), custom_call_target="tpu_custom_call" | custom-call | tf_op jit(solution)/shard_map/pallas_call | solution.py:710
  (10 shorter events, 0.0 us)
Async XLA Ops:
  0.6 0.7 copy-start.7
  0.6 0.7 copy-start.6
  0.7 0.7 copy-start.8
  0.7 0.7 copy-start.9
  1.3 0.9 copy-start
  2.2 0.9 copy-start.1
  5.2 7.3 %copy-start.3 = (f32[10,4]{0,1:T(4,128)S(1)}, f32[10,4]{0,1:T(4,128)}, u32[]{:S(2)}) copy-start(f32[10,4]{0,1:T(4,128)} %param.15) | copy-start | bytes 484
  5.2 15.5 %all-to-all-start = ((f32[32,8,128]{2,1,0:T(8,128)}), f32[32,8,128]{2,1,0:T(8,128)S(1)}, u32[]{:S(2)}, u32[]{:S(2)}) async-start(f32[32,8,128]{2,1,0:T(8,128)} %bitcast.4), calls=%async_computation | async-start | bytes 262144 | tf_op jit(solution)/shard_map/all_to_all | solution.py:725
  12.5 0.7 copy-start.2
  12.6 0.7 copy-start.4
  12.6 0.7 copy-start.5
  44.8 13.0 %all-to-all-start.3 = ((f32[32,4,128]{2,1,0:T(4,128)}), f32[32,4,128]{2,1,0:T(4,128)S(1)}, u32[]{:S(2)}, u32[]{:S(2)}) async-start(f32[32,4,128]{2,1,0:T(4,128)} %bitcast.13), calls=%async_computation.3 | async-start | bytes 131072 | tf_op jit(solution)/shard_map/all_to_all | solution.py:725
  78.5 11.2 %all-to-all-start.5 = ((f32[32,1,1280]{2,1,0:T(1,128)}), f32[32,1,1280]{2,1,0:T(1,128)S(1)}, u32[]{:S(2)}, u32[]{:S(2)}) async-start(f32[32,1,1280]{2,1,0:T(1,128)} %bitcast.17), calls=%async_computation.5 | async-start | bytes 327680 | tf_op jit(solution)/shard_map/all_to_all | solution.py:725
  81.0 1.7 %collective-permute-start = (f32[608,128]{1,0:T(8,128)S(1)}, f32[608,128]{1,0:T(8,128)S(1)}, u32[]{:S(2)}, u32[]{:S(2)}) collective-permute-start(f32[608,128]{1,0:T(8,128)S(1)} %bitcast.20), channel_id=1, source_target_pairs={{0,1},{1,0},{2,3},{3,2},{4,5},{5,4},{6,7},{7,6},{8,9},{9,8},{10,11... | collective-permute-start | bytes 933896 | tf_op jit(solution)/shard_map/ppermute | solution.py:790

commit v2 on v1

--- a/solution.py
+++ b/solution.py
@@ -157,6 +157,7 @@
 HI = lax.Precision.HIGHEST
 f32 = jnp.float32
 JOINT = 19
+LARGE = 60
 
 
 def iota(shape, dim):
@@ -171,6 +172,24 @@
     return lax.dot_general(
         a, b, (((1,), (1,)), ((), ())), precision=HI, preferred_element_type=f32
     )
+
+
+def split(value):
+    high = value.astype(jnp.bfloat16)
+    return high, (value - high.astype(f32)).astype(jnp.bfloat16)
+
+
+def product(a, b, transposed=False):
+    dims = (((1,), (1 if transposed else 0,)), ((), ()))
+
+    def one(x, y):
+        return lax.dot_general(x, y, dims, preferred_element_type=f32)
+
+    return one(a[0], b[0]) + (one(a[0], b[1]) + one(a[1], b[0]))
+
+
+def load(pair):
+    return pair[0][...], pair[1][...]
 
 
 def move(block, source, target):
@@ -218,7 +237,7 @@
 
 
 def table_to_mixed(field, kron_third, second_t, rows_ref, stack_ref):
-    rows_ref[...] = mm(field, kron_third)
+    rows_ref[...] = product(split(field), kron_third)
     for c in range(4):
         for j in range(3):
             parts = []
@@ -230,11 +249,11 @@
                 else:
                     parts.append(jnp.zeros((16, 128), f32))
             stack_ref[16 * c : 16 * c + 16, 128 * j : 128 * j + 128] = merge(parts)
-    return mm(second_t, stack_ref[...])
+    return product(second_t, split(stack_ref[...]))
 
 
 def mixed_to_table(value, kron_third, second, rows_ref, stack_ref):
-    stack_ref[...] = mm(second, value)
+    stack_ref[...] = product(second, split(value))
     rows_ref[...] = jnp.zeros((256, 128), f32)
     for r in range(ROWS):
         j, q = r // 4, r % 4
@@ -242,7 +261,7 @@
             move(stack_ref[16 * c : 16 * c + 16, 128 * j : 128 * j + 128], q, c) for c in range(4)
         ]
         rows_ref[pl.ds(slot(r), 16, stride=16), :] = merge(parts)
-    return mm_t(rows_ref[...], kron_third)
+    return product(split(rows_ref[...]), kron_third, True)
 
 
 def inner_penalty(value):
@@ -296,23 +315,56 @@
     return jnp.sum(jnp.where(lane == k, ref[0:1, :], 0.0))
 
 
+def constants(ref):
+    kron = ref[0:256, :], ref[256:512, :]
+    second = ref[512:576, 0:32], ref[576:640, 0:32]
+    return kron, second, (ref[640:672, 0:64], ref[672:704, 0:64])
+
+
 def start_kernel(
-    table_ref, weight_ref, start2_ref, band2_ref, start3_ref, band3_ref,
-    send_ref, wide_ref, kron_ref, second_ref, second_t_ref,
+    table_hbm, weight_hbm, start2_hbm, band2_hbm, start3_hbm, band3_hbm,
+    send_ref, wide_ref, inner_ref,
+    table_ref, weight_ref, start2_ref, band2_ref, start3_ref, band3_ref, sems,
     product_ref, packed_ref, field_ref, rows_ref, stack_ref,
 ):
-    fourth_t = banded_t(start3_ref, band3_ref, 128, 32)
+    copies = [
+        pltpu.make_async_copy(source, target, sems.at[k])
+        for k, (source, target) in enumerate(
+            (
+                (start3_hbm, start3_ref),
+                (band3_hbm, band3_ref),
+                (start2_hbm, start2_ref),
+                (band2_hbm, band2_ref),
+                (weight_hbm, weight_ref),
+                (table_hbm, table_ref),
+            )
+        )
+    ]
+    for copy in copies:
+        copy.start()
+    copies[0].wait()
+    copies[1].wait()
     pick_bin = (iota((256, N3), 0) % N3 == iota((256, N3), 1)) & (iota((256, N3), 0) < 4 * N3)
-    kron = mm_t(jnp.where(pick_bin, 1.0, 0.0), fourth_t)
     same = iota((256, 128), 0) // N3 == iota((256, 128), 1) // 32
-    kron = jnp.where(same, kron, 0.0)
-    kron_ref[...] = kron
-    third_t = banded_t(start2_ref, band2_ref, 32, 32)
-    order = iota((N2, N2), 1)
-    permute = (order % 16) * 4 + order // 16 == iota((N2, N2), 0)
-    second_t = mm(third_t, jnp.where(permute, 1.0, 0.0))
-    second_t_ref[...] = second_t
-    second_ref[...] = second_t.T
+    picker = jnp.where(pick_bin, 1.0, 0.0).astype(jnp.bfloat16)
+    for k, term in enumerate(split(banded_t(start3_ref, band3_ref, 128, 32))):
+        spread_out = lax.dot_general(
+            picker, term, (((1,), (1,)), ((), ())), preferred_element_type=f32
+        )
+        inner_ref[256 * k : 256 * k + 256, :] = jnp.where(same, spread_out, 0.0).astype(jnp.bfloat16)
+    copies[2].wait()
+    copies[3].wait()
+    order, other = iota((N2, N2), 1), iota((N2, N2), 0)
+    permute = jnp.where((order % 16) * 4 + order // 16 == other, 1.0, 0.0).astype(jnp.bfloat16)
+    back = jnp.where((other % 16) * 4 + other // 16 == order, 1.0, 0.0).astype(jnp.bfloat16)
+    for k, term in enumerate(split(banded_t(start2_ref, band2_ref, 32, 32))):
+        value = jnp.dot(term, permute, preferred_element_type=f32)
+        inner_ref[640 + 32 * k : 672 + 32 * k, 0:64] = value.astype(jnp.bfloat16)
+        value = lax.dot_general(back, term, (((1,), (1,)), ((), ())), preferred_element_type=f32)
+        inner_ref[512 + 64 * k : 576 + 64 * k, 0:32] = value.astype(jnp.bfloat16)
+    kron, _, turned = constants(inner_ref)
+    copies[4].wait()
+    copies[5].wait()
     packed_ref[8:16, :] = jnp.zeros((8, N2 * N3), f32)
     product_ref[8:16, :] = jnp.zeros((8, N2 * N3), f32)
     for b in range(L1):
@@ -324,7 +376,7 @@
             low, high = expand(source, p)
             target[16 * p : 16 * p + 16, 0:128] = low
             target[16 * p : 16 * p + 16, 128:256] = high
-    mixed = table_to_mixed(field_ref[...], kron, second_t, rows_ref, stack_ref)
+    mixed = table_to_mixed(field_ref[...], kron, turned, rows_ref, stack_ref)
     once = inner_penalty(mixed)
     twice = inner_penalty(once)
     for base, value in ((0, mixed), (3, once), (5, twice)):
@@ -397,7 +449,15 @@
     return block
 
 
-def gram_kernel(start0_ref, band0_ref, start1_ref, band1_ref, gram_ref, rows0_ref, rows1_ref):
+def store_split(high_ref, low_ref, rows, value):
+    high, low = split(value)
+    high_ref[rows, :] = high
+    low_ref[rows, :] = low
+
+
+def gram_kernel(
+    start0_ref, band0_ref, start1_ref, band1_ref, gram_h_ref, gram_l_ref, rows0_ref, rows1_ref
+):
     total = DEVICES * ROWS
     block = gram_rows(start0_ref, band0_ref, start1_ref, band1_ref, rows0_ref, rows1_ref, 2)
 
@@ -405,13 +465,17 @@
     def _(step):
         base = pl.multiple_of(step * 32, 32)
         g, h = block(base)
-        gram_ref[pl.ds(base, 32), :] = g[0] * h[0]
-        gram_ref[pl.ds(base + total, 32), :] = g[1] * h[0] + g[0] * h[1]
+        store_split(gram_h_ref, gram_l_ref, pl.ds(base, 32), g[0] * h[0])
+        store_split(
+            gram_h_ref, gram_l_ref, pl.ds(base + total, 32), g[1] * h[0] + g[0] * h[1]
+        )
 
 
 def high_kernel(
-    after_ref, start0_ref, band0_ref, start1_ref, band1_ref, high_ref, rows0_ref, rows1_ref
-):
+    after_ref, start0_ref, band0_ref, start1_ref, band1_ref, high_h_ref, high_l_ref, token_ref,
+    rows0_ref, rows1_ref,
+):
+    token_ref[...] = after_ref[...]
     total = DEVICES * ROWS
     block = gram_rows(start0_ref, band0_ref, start1_ref, band1_ref, rows0_ref, rows1_ref, 4)
 
@@ -419,21 +483,24 @@
     def _(step):
         base = pl.multiple_of(step * 32, 32)
         g, h = block(base)
-        high_ref[pl.ds(base, 32), :] = g[2] * h[0] + 2.0 * g[1] * h[1] + g[0] * h[2]
-        high_ref[pl.ds(base + total, 32), :] = (
-            g[3] * h[0] + 3.0 * (g[2] * h[1] + g[1] * h[2]) + g[0] * h[3]
-        )
+        squared = g[2] * h[0] + 2.0 * g[1] * h[1] + g[0] * h[2]
+        cubed = g[3] * h[0] + 3.0 * (g[2] * h[1] + g[1] * h[2]) + g[0] * h[3]
+        store_split(high_h_ref, high_l_ref, pl.ds(base, 32), squared)
+        store_split(high_h_ref, high_l_ref, pl.ds(base + total, 32), cubed)
 
 
 def lift_kernel(
-    after_ref, group_ref, start0_ref, band0_ref, start1_ref, band1_ref, lift_ref, side_ref
-):
+    after_ref, group_ref, start0_ref, band0_ref, start1_ref, band1_ref,
+    lift_h_ref, lift_l_ref, side_ref, token_ref,
+):
+    token_ref[...] = after_ref[...]
     total = DEVICES * ROWS
     lifted = choose(three_terms(banded_t(start0_ref, band0_ref, K0, K0)), select_first())
     column = iota((K0, total), 1)
     owner = L1 * (column % GRPS) + column // 32 % L1
     for n in range(N1):
-        lift_ref[K0 * n : K0 * n + K0, :] = jnp.where(owner == n, lifted, 0.0)
+        rows = slice(K0 * n, K0 * n + K0)
+        store_split(lift_h_ref, lift_l_ref, rows, jnp.where(owner == n, lifted, 0.0))
     group = group_ref[0]
     coef = iota((128, K1), 0) % 32 + 32 * group
     pick_coef = jnp.where(coef == iota((128, K1), 1), 1.0, 0.0)
@@ -461,7 +528,7 @@
     return move(ref[pl.ds(row, 32, stride=count), :], source, target)
 
 
-def first_column_kernel(recv_ref, gram_ref, send_ref, fields_ref, images_ref):
+def first_column_kernel(recv_ref, gram_h_ref, gram_l_ref, send_ref, fields_ref, images_ref, token_ref):
     total = DEVICES * ROWS
     zero = jnp.zeros((32, 128), f32)
     for r in range(ROWS):
@@ -475,16 +542,17 @@
         ]
         fields_ref[32 * r : 32 * r + 32, :] = merge(parts + [zero])
     fields = fields_ref[...]
-    product = mm(gram_ref[...], fields)
+    applied = product(load((gram_h_ref, gram_l_ref)), split(fields))
     lane = iota((total, 128), 1)
-    images = product[:total] + jnp.where(
-        (lane >= 32) & (lane < 64), pltpu.roll(product[total:], 32, 1), 0.0
+    images = applied[:total] + jnp.where(
+        (lane >= 32) & (lane < 64), pltpu.roll(applied[total:], 32, 1), 0.0
     )
     images_ref[...] = images
     norm = jnp.sum(jnp.where(lane < 32, fields * images, 0.0))
     bend = jnp.sum(jnp.where(lane < 32, fields * pltpu.roll(images, 96, 1), 0.0))
     send_rows(send_ref, images_ref)
     spread(send_ref, 3, 4, (norm, bend))
+    token_ref[...] = lanes((norm, bend))
 
 
 def send_rows(send_ref, value_ref):
@@ -504,16 +572,15 @@
 
 
 def first_row_kernel(
-    recv_ref, wide_ref, kron_ref, second_ref, second_t_ref,
-    send_ref, scalar_ref, rows_ref, stack_ref,
+    recv_ref, wide_ref, inner_ref, after_ref, send_ref, scalar_ref, rows_ref, stack_ref,
 ):
     norm, bend = totals(recv_ref, 3, 4, 2)
     scalar_ref[...] = lanes((norm, bend))
-    kron = kron_ref[...]
-    field = mixed_to_table(received_rows(recv_ref), kron, second_ref[...], rows_ref, stack_ref)
+    kron, second, turned = constants(inner_ref)
+    field = mixed_to_table(received_rows(recv_ref), kron, second, rows_ref, stack_ref)
     weighted = wide_ref[...] * field
     energy = jnp.sum(field * weighted)
-    mixed = table_to_mixed(weighted, kron, second_t_ref[...], rows_ref, stack_ref)
+    mixed = table_to_mixed(weighted, kron, turned, rows_ref, stack_ref)
     once = inner_penalty(mixed)
     for base, value in ((0, mixed), (3, once)):
         put(send_ref, base, 8, tile_of(value, 0))
@@ -526,7 +593,7 @@
 
 
 def second_column_kernel(
-    recv_ref, gram_ref, fields_ref, images_ref, scalar_ref,
+    recv_ref, gram_h_ref, gram_l_ref, fields_ref, images_ref, scalar_ref, after_ref,
     send_ref, blend_ref, out_scalar_ref, next_ref, image_ref,
 ):
     zero = jnp.zeros((32, 128), f32)
@@ -543,7 +610,8 @@
     step = norm / (energy + 0.1 * bend)
     out_scalar_ref[...] = lanes((norm, step))
     fields, images, following = fields_ref[...], images_ref[...], next_ref[...]
-    image = mm(gram_ref[0 : DEVICES * ROWS, :], following)
+    gram = gram_h_ref[0 : DEVICES * ROWS, :], gram_l_ref[0 : DEVICES * ROWS, :]
+    image = product(gram, split(following))
     image_ref[...] = images - step * (image + 0.1 * pltpu.roll(images, 96, 1))
     send_rows(send_ref, image_ref)
     put(send_ref, 3, 4, zero)
@@ -587,14 +655,19 @@
             send_ref[pl.ds(g * count + base + j, 16, stride=2 * count), :] = merge(parts)
 
 
-def middle_kernel(blend_ref, gram_ref, high_ref, lift_ref, scalar_ref, send_ref, keep_ref, sums_ref):
+def middle_kernel(
+    blend_ref, gram_h_ref, gram_l_ref, high_h_ref, high_l_ref, lift_h_ref, lift_l_ref, scalar_ref,
+    send_ref, keep_ref, sums_ref,
+):
     total = DEVICES * ROWS
     step = pick(scalar_ref, 1)
     small = 0.1 * step
     blend = blend_ref[...]
     lane = iota(blend.shape, 1)
-    product, higher = mm(gram_ref[...], blend), mm(high_ref[...], blend)
-    g0, g1, g2, g3 = product[:total], product[total:], higher[:total], higher[total:]
+    pair = split(blend)
+    lower = product(load((gram_h_ref, gram_l_ref)), pair)
+    higher = product(load((high_h_ref, high_l_ref)), pair)
+    g0, g1, g2, g3 = lower[:total], lower[total:], higher[:total], higher[total:]
     head = g0 - small * pltpu.roll(g1, 64, 1)
     tail = g1 - small * pltpu.roll(g2, 64, 1)
     end = g2 - small * pltpu.roll(g3, 64, 1)
@@ -605,7 +678,7 @@
     tail_p = end + pltpu.roll(tail, 96, 1)
     bend = jnp.sum(jnp.where(low, blend * head_p - small * scaled * tail_p, 0.0))
     sums_ref[...] = lanes((norm, bend))
-    lifted = mm(lift_ref[...], blend)
+    lifted = product(load((lift_h_ref, lift_l_ref)), pair)
     once = coefficient_penalty(lifted)
     twice = coefficient_penalty(once)
     h_a = lifted - small * pltpu.roll(once, 64, 1)
@@ -624,21 +697,21 @@
 
 
 def second_row_kernel(
-    early_ref, recv_ref, sums_ref, wide_ref, kron_ref, second_ref, second_t_ref,
+    early_ref, recv_ref, sums_ref, wide_ref, inner_ref,
     send_ref, rows_ref, stack_ref,
 ):
-    kron = kron_ref[...]
-    field = mixed_to_table(received_rows(recv_ref), kron, second_ref[...], rows_ref, stack_ref)
+    kron, second, turned = constants(inner_ref)
+    field = mixed_to_table(received_rows(recv_ref), kron, second, rows_ref, stack_ref)
     weighted = wide_ref[...] * field
     energy = jnp.sum(field * weighted)
-    mixed = table_to_mixed(weighted, kron, second_t_ref[...], rows_ref, stack_ref)
+    mixed = table_to_mixed(weighted, kron, turned, rows_ref, stack_ref)
     for j in range(3):
         put(send_ref, j, JOINT, tile_of(mixed, j))
     spread(send_ref, 3, JOINT, (energy, pick(sums_ref, 0), pick(sums_ref, 1)))
 
 
 def third_column_kernel(
-    recv_ref, lift_ref, keep_ref, scalar_ref, send_ref, out_scalar_ref, last_ref, mixed_ref
+    recv_ref, lift_h_ref, lift_l_ref, keep_ref, scalar_ref, send_ref, out_scalar_ref, last_ref, mixed_ref
 ):
     zero = jnp.zeros((32, 128), f32)
     for r in range(ROWS):
@@ -650,7 +723,7 @@
     curve = energy + 0.1 * bend - ratio * norm_next / step
     step_next = norm_next / curve
     out_scalar_ref[...] = lanes((norm, step, ratio, step_next))
-    lifted = mm(lift_ref[...], last_ref[...])
+    lifted = product(load((lift_h_ref, lift_l_ref)), split(last_ref[...]))
     keep = keep_ref[...]
     h_a, x_a = pltpu.roll(keep, 96, 1), pltpu.roll(keep, 32, 1)
     mixed_ref[...] = (
@@ -668,54 +741,72 @@
             out_ref[pl.ds(m // 8 * 64 + m % 8, 8, stride=8), :] = merged
 
 
-def final_kernel(
-    own_ref, partner_ref, late_ref, side_ref, scalar_ref, solution_ref, residual_ref, early, late
-):
+def take(ref, block, tile):
+    return jnp.concatenate(
+        [ref[pl.ds((5 * block + t) * 64 + 8 * tile, 8), :] for t in range(5)], axis=0
+    )
+
+
+def settle_kernel(own_ref, partner_ref, side_ref, scalar_ref, solution_ref, part_ref, early):
     for block in range(3):
         for h, ref in enumerate((own_ref, partner_ref)):
             gather_blocks(ref, JOINT, 4 + 5 * block, 5, early, 40 * block + 20 * h)
-    gather_blocks(late_ref, 10, 0, 10, late, 0)
     step, ratio, step_next = pick(scalar_ref, 1), pick(scalar_ref, 2), pick(scalar_ref, 3)
     small = 0.1 * step
-    side = side_ref[...]
+    value = split(side_ref[:, 128:208])
+    slope = split(side_ref[:, 40:120])
     for tile in range(8):
-        def take(ref, block):
-            return jnp.concatenate(
-                [ref[pl.ds((5 * block + t) * 64 + 8 * tile, 8), :] for t in range(5)], axis=0
-            )
-        h_0, h_a, y_1, h_r = take(early, 0), take(early, 1), take(early, 2), take(late, 0)
+        h_0, h_a, y_1 = take(early, 0, tile), take(early, 1, tile), take(early, 2, tile)
         right = jnp.concatenate(
             [(step + step_next * ratio) * h_0 + step_next * h_a, (-step_next * small) * h_0], axis=0
         )
         columns = slice(128 * tile, 128 * tile + 128)
-        solution_ref[:, :, columns] = mm(side[:, 128:208], right).reshape(4, 32, 128)
+        solution_ref[:, :, columns] = product(value, split(right)).reshape(4, 32, 128)
         right = jnp.concatenate(
             [
-                h_r,
                 (-small * (1.0 + step_next * ratio / step)) * h_0
                 - (0.1 * step_next) * (h_a - small * y_1),
                 (0.1 * step_next * small) * h_0,
             ],
             axis=0,
         )
-        residual_ref[:, :, columns] = mm(side[:, 0:120], right).reshape(4, 32, 128)
-
-
-def call(kernel, outputs, scratch, *operands, aliases={}):
-    specs = [pl.BlockSpec(memory_space=pltpu.VMEM)] * len(operands)
-    if kernel in (high_kernel, lift_kernel):
-        specs[0] = pl.BlockSpec(memory_space=pl.ANY)
-    if kernel is lift_kernel:
-        specs[1] = pl.BlockSpec(memory_space=pltpu.SMEM)
+        part_ref[:, columns] = product(slope, split(right))
+
+
+def final_kernel(late_ref, side_ref, part_ref, residual_ref, late):
+    gather_blocks(late_ref, 10, 0, 10, late, 0)
+    value = split(side_ref[:, 0:40])
+    for tile in range(8):
+        columns = slice(128 * tile, 128 * tile + 128)
+        whole = part_ref[:, columns] + product(value, split(take(late, 0, tile)))
+        residual_ref[:, :, columns] = whole.reshape(4, 32, 128)
+
+
+def call(kernel, outputs, scratch, *operands, aliases={}, left=(), scalars=(), limit=16):
+    vmem = pl.BlockSpec(memory_space=pltpu.VMEM)
+    specs = [vmem] * len(operands)
+    for k in left:
+        specs[k] = pl.BlockSpec(memory_space=pltpu.HBM)
+    for k in scalars:
+        specs[k] = pl.BlockSpec(memory_space=pltpu.SMEM)
     return pl.pallas_call(
         kernel,
-        out_shape=[jax.ShapeDtypeStruct(shape, f32) for shape in outputs],
+        out_shape=[
+            shape if isinstance(shape, jax.ShapeDtypeStruct) else jax.ShapeDtypeStruct(shape, f32)
+            for shape in outputs
+        ],
         in_specs=specs,
-        out_specs=[pl.BlockSpec(memory_space=pltpu.VMEM)] * len(outputs),
-        scratch_shapes=[pltpu.VMEM(shape, f32) for shape in scratch],
+        out_specs=[vmem] * len(outputs),
+        scratch_shapes=[
+            pltpu.VMEM(shape, f32) if isinstance(shape, tuple) else shape for shape in scratch
+        ],
         input_output_aliases=aliases,
-        compiler_params=pltpu.CompilerParams(vmem_limit_bytes=32 * 2**20),
+        compiler_params=pltpu.CompilerParams(vmem_limit_bytes=limit * 2**20),
     )(*operands)
+
+
+def pair_of(*shape):
+    return [jax.ShapeDtypeStruct(shape, jnp.bfloat16)] * 2
 
 
 def exchange(buffer):
@@ -741,49 +832,67 @@
     total = DEVICES * ROWS
     work = [(256, 128), (64, 384)]
     outer = (first_start, first_band.T, second_start, second_band.T)
-    send, wide, kron, second, second_t = call(
-        start_kernel,
-        [(256, 128), (256, 256), (256, 128), (64, 32), (32, 64)],
-        [(16, N2 * N3), (16, N2 * N3), (256, 256)] + work,
+    inputs = (
         photon_table.transpose(1, 0, 2),
         bin_weights.transpose(1, 0, 2),
-        third_start, third_band.T, fourth_start, fourth_band.T,
+        third_start,
+        third_band.T,
+        fourth_start,
+        fourth_band.T,
+    )
+    send, wide, inner = call(
+        start_kernel,
+        [(256, 128), (256, 256), jax.ShapeDtypeStruct((704, 128), jnp.bfloat16)],
+        [pltpu.VMEM(value.shape, value.dtype) for value in inputs]
+        + [pltpu.SemaphoreType.DMA((len(inputs),))]
+        + [(16, N2 * N3), (16, N2 * N3), (256, 256)]
+        + work,
+        *inputs,
+        left=range(len(inputs)),
+        limit=LARGE,
     )
     recv = exchange(send)
-    (gram,) = call(gram_kernel, [(2 * total, total)], [(total, 64), (total, 32)], *outer)
-    send, fields, images = call(
-        first_column_kernel, [(128, 128), (total, 128), (total, 128)], [], recv, gram
+    gram = call(gram_kernel, pair_of(2 * total, total), [(total, 64), (total, 32)], *outer)
+    send, fields, images, token = call(
+        first_column_kernel, [(128, 128), (total, 128), (total, 128), (8, 128)], [], recv, *gram
     )
     recv = exchange(send)
-    (high,) = call(
-        high_kernel, [(2 * total, total)], [(total, 128), (total, 64)], images, *outer
+    *high, token = call(
+        high_kernel,
+        pair_of(2 * total, total) + [(8, 128)],
+        [(total, 128), (total, 64)],
+        token, *outer,
     )
     send, scalars = call(
-        first_row_kernel, [(256, 128), (8, 128)], work, recv, wide, kron, second, second_t
+        first_row_kernel, [(256, 128), (8, 128)], work, recv, wide, inner, token
     )
     recv = exchange(send)
     group = lax.axis_index("grp").reshape(1)
-    lift, side = call(
-        lift_kernel, [(K0 * N1, total), (128, 256)], [], scalars, group, *outer
+    *lift, side, token = call(
+        lift_kernel,
+        pair_of(K0 * N1, total) + [(128, 256), (8, 128)],
+        [],
+        scalars, group, *outer,
+        scalars=(1,),
     )
     send, blend, scalars = call(
         second_column_kernel,
         [(128, 128), (total, 128), (8, 128)],
         [(total, 128), (total, 128)],
-        recv, gram, fields, images, scalars,
+        recv, *gram, fields, images, scalars, token,
     )
     recv = exchange(send)
     send, keep, sums = call(
         middle_kernel,
         [(DEVICES * JOINT, 128), (K0 * N1, 128), (8, 128)],
         [],
-        blend, gram, high, lift, scalars,
+        blend, *gram, *high, *lift, scalars,
     )
     (send,) = call(
         second_row_kernel,
         [(DEVICES * JOINT, 128)],
         work,
-        send, recv, sums, wide, kron, second, second_t,
+        send, recv, sums, wide, inner,
         aliases={0: 0},
     )
     recv = exchange(send)
@@ -792,15 +901,17 @@
         third_column_kernel,
         [(DEVICES * 10, 128), (8, 128)],
         [(total, 128), (K0 * N1, 128)],
-        recv, lift, keep, scalars,
+        recv, *lift, keep, scalars,
     )
     late = exchange(send)
-    return call(
-        final_kernel,
-        [(4, 32, 1024), (4, 32, 1024)],
-        [(960, 128), (320, 128)],
-        recv, partner, late, side, scalars,
-    )
+    solution_part, part = call(
+        settle_kernel,
+        [(4, 32, 1024), (128, 1024)],
+        [(960, 128)],
+        recv, partner, side, scalars,
+    )
+    (residual,) = call(final_kernel, [(4, 32, 1024)], [(320, 128)], late, side, part)
+    return solution_part, residual
 
 
 def fits(mesh):

time: 92.5 us -> 87.8 us (0.949)
  blocking collectives: 36.7 us -> 14.8 us
  waiting for transfers between devices: 11.8 us -> 20.4 us
  starting transfers between devices: 12.8 us -> 20.2 us
  local copies, waits for them, and re-layouts: 3.14 us -> 5.38 us
  Pallas kernels: 26.8 us -> 25.7 us
    all_to_all x3 -> x1, blocking collectives: 36.7 us -> 14.8 us  [exchange(): lax.all_to_all(buffer.reshape(shape), ('slab', 'grp'), 0, 0, tiled=True)]
    all_to_all x3 -> x5, waiting for transfers between devices: 10.3 us -> 18.9 us  [exchange(): lax.all_to_all(buffer.reshape(shape), ('slab', 'grp'), 0, 0, tiled=True)]
    all_to_all x3 -> x5, starting transfers between devices: 12.6 us -> 20.1 us  [exchange(): lax.all_to_all(buffer.reshape(shape), ('slab', 'grp'), 0, 0, tiled=True)]
    unnamed x20 -> x26, local copies, waits for them, and re-layouts: 3.14 us -> 5.38 us
    pallas_call x11 -> x12, Pallas kernels: 26.8 us -> 25.7 us  [call(): pl.pallas_call(kernel, out_shape=[shape if isinstance(shape, jax.ShapeDty...]
  transfers between devices with their start and end apart: 4 -> 6, of which waited for: 3 -> 6; matrix products, arithmetic and copies ran while one was open for 0% -> 0% of each run, Pallas kernels for 16% -> 17%
where the time goes in v2:
time: 87.8 us; the launch traced here: 87.3 us
  Pallas kernels  25.7 us (29%)
  waiting for transfers between devices  20.4 us (23%)
  starting transfers between devices  20.2 us (23%)
  blocking collectives  14.8 us (17%)
  local copies, waits for them, and re-layouts  5.38 us (6%)
    pallas_call x12, Pallas kernels, call(): pl.pallas_call(kernel, out_shape=[shape if isinstance(shape, jax.ShapeDty...  25.7 us
    all_to_all x5, starting transfers between devices, exchange(): lax.all_to_all(buffer.reshape(shape), ('slab', 'grp'), 0, 0, tiled=True)  20.1 us
    all_to_all x5, waiting for transfers between devices, exchange(): lax.all_to_all(buffer.reshape(shape), ('slab', 'grp'), 0, 0, tiled=True)  18.9 us
    all_to_all x1, blocking collectives, exchange(): lax.all_to_all(buffer.reshape(shape), ('slab', 'grp'), 0, 0, tiled=True)  14.8 us
    unnamed x26, local copies, waits for them, and re-layouts  5.38 us
  transfers between devices with their start and end apart: 6, of which 6 were waited for; matrix products, arithmetic and copies ran while one was open for 0% of the time, Pallas kernels for 17%

profile of v2, /device:TPU:0, one launch (start us, length us, event | category | flops | bytes accessed | tf_op | source)
XLA Modules:
  0.0 87.3 jit_solution(3773534015404359656)
XLA Ops:
  0.6 2.7 %shard_map.113 = (f32[256,128]{1,0:T(8,128)}, f32[256,256]{1,0:T(8,128)}, bf16[704,128]{1,0:T(8,128)(2,1)}) custom-call(f32[5,2,3200]{2,1,0:T(2,128)} %bitcast.36, f32[5,2,3200]{2,1,0:T(2,128)} %bitcast.37, s32[64]{0:T(128)} %start2_hbm.1, f32[4,64]{1,0:T(4,128)} %bitcast.38, s32[50]{0:T(128)} %start3_hbm.1, f32[4,50]{1,0:T(4,128)} %bitcast.39), custom_call_target="tpu_custom_call" | custom-call | tf_op jit(solution)/shard_map/pallas_call | solution.py:792
  3.3 7.3 %all-to-all-start = ((f32[32,8,128]{2,1,0:T(8,128)}), f32[32,8,128]{2,1,0:T(8,128)S(1)}, u32[]{:S(2)}, u32[]{:S(2)}) async-start(f32[32,8,128]{2,1,0:T(8,128)} %bitcast.35), calls=%async_computation | async-start | bytes 262144 | tf_op jit(solution)/shard_map/all_to_all | solution.py:816
  10.7 0.6 copy-done.9
  11.3 4.2 %shard_map.114 = (bf16[640,320]{1,0:T(8,128)(2,1)S(1)}, bf16[640,320]{1,0:T(8,128)(2,1)S(1)}) custom-call(s32[32]{0:T(128)S(1)} %copy-done.11, f32[4,32]{1,0:T(4,128)S(1)} %bitcast.29, s32[10]{0:T(128)S(1)} %copy-done.12, f32[4,10]{1,0:T(4,128)S(1)} %bitcast.32), custom_call_target="tpu_custom_call" | custom-call | tf_op jit(solution)/shard_map/pallas_call | solution.py:792
  15.5 3.4 %all-to-all-done = f32[32,8,128]{2,1,0:T(8,128)S(1)} async-done(((f32[32,8,128]{2,1,0:T(8,128)}), f32[32,8,128]{2,1,0:T(8,128)S(1)}, u32[]{:S(2)}, u32[]{:S(2)}) %all-to-all-start) | async-done | bytes 131104 | tf_op jit(solution)/shard_map/all_to_all | solution.py:816
  18.9 1.6 %shard_map.115 = (f32[128,128]{1,0:T(8,128)}, f32[320,128]{1,0:T(8,128)S(1)}, f32[320,128]{1,0:T(8,128)S(1)}, f32[8,128]{1,0:T(8,128)S(1)}) custom-call(f32[256,128]{1,0:T(8,128)S(1)} %bitcast.24, bf16[640,320]{1,0:T(8,128)(2,1)S(1)} %get-tuple-element.31.gram_h_ref, bf16[640,320]{1,0:T(8,128)(2,1)S(1)} %get-tuple-element.32.gram_l_ref), custom_call_target="tpu_custom_call" | custom-call | tf_op jit(solution)/shard_map/pallas_call | solution.py:792
  20.5 2.6 %all-to-all-start.1 = ((f32[32,4,128]{2,1,0:T(4,128)}), f32[32,4,128]{2,1,0:T(4,128)S(1)}, u32[]{:S(2)}, u32[]{:S(2)}) async-start(f32[32,4,128]{2,1,0:T(4,128)} %bitcast.8), calls=%async_computation.1 | async-start | bytes 131072 | tf_op jit(solution)/shard_map/all_to_all | solution.py:816
  23.0 5.9 %shard_map.116 = (bf16[640,320]{1,0:T(8,128)(2,1)S(1)}, bf16[640,320]{1,0:T(8,128)(2,1)S(1)}, f32[8,128]{1,0:T(8,128)S(1)}) custom-call(f32[8,128]{1,0:T(8,128)S(1)} %get-tuple-element.36.after_ref, s32[32]{0:T(128)S(1)} %copy-done.11, f32[4,32]{1,0:T(4,128)S(1)} %bitcast.30, s32[10]{0:T(128)S(1)} %copy-done.12, f32[4,10]{1,0:T(4,128)S(1)} %bitcast.33), custom_call_target="tpu_custom_call" | custom-call | tf_op jit(solution)/shard_map/pallas_call | solution.py:792
  28.9 0.8 copy-done.2
  29.7 0.8 all-to-all-done.1
  30.4 1.9 %shard_map.117 = (f32[256,128]{1,0:T(8,128)}, f32[8,128]{1,0:T(8,128)S(1)}) custom-call(f32[128,128]{1,0:T(8,128)S(1)} %bitcast.27, f32[256,256]{1,0:T(8,128)S(1)} %copy-done, bf16[704,128]{1,0:T(8,128)(2,1)S(1)} %copy-done.1, f32[8,128]{1,0:T(8,128)S(1)} %get-tuple-element.37.after_ref), custom_call_target="tpu_custom_call" | custom-call | tf_op jit(solution)/shard_map/pallas_call | solution.py:792
  32.4 5.1 %all-to-all-start.2 = ((f32[32,8,128]{2,1,0:T(8,128)}), f32[32,8,128]{2,1,0:T(8,128)S(1)}, u32[]{:S(2)}, u32[]{:S(2)}) async-start(f32[32,8,128]{2,1,0:T(8,128)} %bitcast.10), calls=%async_computation.2 | async-start | bytes 262144 | tf_op jit(solution)/shard_map/all_to_all | solution.py:816
  37.5 1.1 %shard_map.118 = (bf16[640,320]{1,0:T(8,128)(2,1)S(1)}, bf16[640,320]{1,0:T(8,128)(2,1)S(1)}, f32[128,256]{1,0:T(8,128)S(1)}, f32[8,128]{1,0:T(8,128)S(1)}) custom-call(f32[8,128]{1,0:T(8,128)S(1)} %get-tuple-element.41.after_ref.scalar_ref, s32[1]{0:T(128)} %bitcast.12.group_ref, s32[32]{0:T(128)S(1)} %copy-done.11, f32[4,32]{1,0:T(4,128)S(1)} %bitcast.31, ...), custom_call_target="tpu_custom_call" | custom-call | tf_op jit(solution)/shard_map/pallas_call | solution.py:792
  38.5 7.1 %all-to-all-done.2 = f32[32,8,128]{2,1,0:T(8,128)S(1)} async-done(((f32[32,8,128]{2,1,0:T(8,128)}), f32[32,8,128]{2,1,0:T(8,128)S(1)}, u32[]{:S(2)}, u32[]{:S(2)}) %all-to-all-start.2) | async-done | bytes 131104 | tf_op jit(solution)/shard_map/all_to_all | solution.py:816
  45.7 0.5 shard_map.119
  46.2 0.7 copy-done.6
  46.9 0.6 copy-done.8
  47.5 2.6 %all-to-all-start.3 = ((f32[32,4,128]{2,1,0:T(4,128)}), f32[32,4,128]{2,1,0:T(4,128)S(1)}, u32[]{:S(2)}, u32[]{:S(2)}) async-start(f32[32,4,128]{2,1,0:T(4,128)} %bitcast.28), calls=%async_computation.3 | async-start | bytes 131072 | tf_op jit(solution)/shard_map/all_to_all | solution.py:816
  50.1 1.0 %copy-done.3 = bf16[640,320]{1,0:T(8,128)(2,1)S(1)} copy-done((bf16[640,320]{1,0:T(8,128)(2,1)S(1)}, bf16[640,320]{1,0:T(8,128)(2,1)}, u32[]{:S(2)}) %copy-start.3) | copy-done | bytes 409624
  51.1 0.9 %copy-done.7 = f32[320,128]{1,0:T(8,128)S(1)} copy-done((f32[320,128]{1,0:T(8,128)S(1)}, f32[320,128]{1,0:T(8,128)}, u32[]{:S(2)}) %copy-start.7) | copy-done | bytes 163864
  52.0 2.2 %shard_map.120 = (f32[608,128]{1,0:T(8,128)S(1)}, f32[640,128]{1,0:T(8,128)S(1)}, f32[8,128]{1,0:T(8,128)S(1)}) custom-call(f32[320,128]{1,0:T(8,128)S(1)} %copy-done.7, bf16[640,320]{1,0:T(8,128)(2,1)S(1)} %get-tuple-element.31.gram_h_ref, bf16[640,320]{1,0:T(8,128)(2,1)S(1)} %get-tuple-element.32.gram_l_ref, ...), custom_call_target="tpu_custom_call" | custom-call | tf_op jit(solution)/shard_map/pallas_call | solution.py:792
  54.2 0.7 copy-done.4
  54.9 2.6 %all-to-all-done.3 = f32[32,4,128]{2,1,0:T(4,128)S(1)} async-done(((f32[32,4,128]{2,1,0:T(4,128)}), f32[32,4,128]{2,1,0:T(4,128)S(1)}, u32[]{:S(2)}, u32[]{:S(2)}) %all-to-all-start.3) | async-done | bytes 65568 | tf_op jit(solution)/shard_map/all_to_all | solution.py:816
  57.5 1.1 %shard_map.121 = f32[608,128]{1,0:T(8,128)S(1)} custom-call(f32[608,128]{1,0:T(8,128)S(1)} %get-tuple-element.49.early_ref, f32[128,128]{1,0:T(8,128)S(1)} %bitcast.26, f32[8,128]{1,0:T(8,128)S(1)} %get-tuple-element.51.sums_ref, f32[256,256]{1,0:T(8,128)S(1)} %copy-done, bf16[704,128]{1,0:T(8,128)(2,1)S(1)} %copy-done.1), custom_call_target="tpu_custom_call", output_to_operand_aliasing={{}: (0, {})} | custom-call | tf_op jit(solution)/shard_map/pallas_call | solution.py:792
  58.6 14.8 %all_to_all.30 = f32[32,1,2432]{2,1,0:T(1,128)S(1)} all-to-all(f32[32,1,2432]{2,1,0:T(1,128)S(1)} %bitcast.22), channel_id=1, replica_groups=mesh['slab'=16,'grp'=2] {'slab','grp'}, dimensions={0} | all-to-all | bytes 622592 | tf_op jit(solution)/shard_map/all_to_all | solution.py:816
  73.4 1.4 %shard_map.122 = (f32[320,128]{1,0:T(8,128)}, f32[8,128]{1,0:T(8,128)S(1)}) custom-call(f32[608,128]{1,0:T(8,128)S(1)} %bitcast.19, bf16[640,320]{1,0:T(8,128)(2,1)S(1)} %get-tuple-element.46.lift_h_ref, bf16[640,320]{1,0:T(8,128)(2,1)S(1)} %get-tuple-element.47.lift_l_ref, f32[640,128]{1,0:T(8,128)S(1)} %copy-done.5, f32[8,128]{1,0:T(8,128)S(1)} %get-tuple-element.48.scalar_ref), custom_call_target="tpu_custom_call" | custom-call | tf_op jit(solution)/shard_map/pallas_call | solution.py:792
  74.8 2.6 %all-to-all-start.5 = ((f32[32,1,1280]{2,1,0:T(1,128)}), f32[32,1,1280]{2,1,0:T(1,128)S(1)}, u32[]{:S(2)}, u32[]{:S(2)}) async-start(f32[32,1,1280]{2,1,0:T(1,128)} %bitcast.17), calls=%async_computation.5 | async-start | bytes 327680 | tf_op jit(solution)/shard_map/all_to_all | solution.py:816
  77.4 0.2 collective-permute-start
  77.6 1.5 %collective-permute-done.partner_ref = f32[608,128]{1,0:T(8,128)S(1)} collective-permute-done((f32[608,128]{1,0:T(8,128)S(1)}, f32[608,128]{1,0:T(8,128)S(1)}, u32[]{:S(2)}, u32[]{:S(2)}) %collective-permute-start) | collective-permute-done | bytes 311328 | tf_op jit(solution)/shard_map/ppermute | solution.py:899
  79.1 1.9 %shard_map.123 = (f32[4,32,1024]{2,1,0:T(8,128)}, f32[128,1024]{1,0:T(8,128)S(1)}) custom-call(f32[608,128]{1,0:T(8,128)S(1)} %bitcast.21, f32[608,128]{1,0:T(8,128)S(1)} %collective-permute-done.partner_ref, f32[128,256]{1,0:T(8,128)S(1)} %get-tuple-element.52.side_ref, f32[8,128]{1,0:T(8,128)S(1)} %get-tuple-element.54.scalar_ref), custom_call_target="tpu_custom_call" | custom-call | tf_op jit(solution)/shard_map/pallas_call | solution.py:792
  80.9 5.0 %all-to-all-done.5 = f32[32,1,1280]{2,1,0:T(1,128)S(1)} async-done(((f32[32,1,1280]{2,1,0:T(1,128)}), f32[32,1,1280]{2,1,0:T(1,128)S(1)}, u32[]{:S(2)}, u32[]{:S(2)}) %all-to-all-start.5) | async-done | bytes 163872 | tf_op jit(solution)/shard_map/all_to_all | solution.py:816
  86.0 1.3 %shard_map.124 = f32[4,32,1024]{2,1,0:T(8,128)} custom-call(f32[320,128]{1,0:T(8,128)S(1)} %bitcast.23, f32[128,256]{1,0:T(8,128)S(1)} %get-tuple-element.52.side_ref, f32[128,1024]{1,0:T(8,128)S(1)} %get-tuple-element.57.part_ref), custom_call_target="tpu_custom_call" | custom-call | tf_op jit(solution)/shard_map/pallas_call | solution.py:792
  (19 shorter events, 0.1 us)
Async XLA Ops:
  3.3 7.4 %copy-start.10 = (f32[10,4]{0,1:T(4,128)S(1)}, f32[10,4]{0,1:T(4,128)}, u32[]{:S(2)}) copy-start(f32[10,4]{0,1:T(4,128)} %param.15) | copy-start | bytes 484
  3.3 15.5 %all-to-all-start = ((f32[32,8,128]{2,1,0:T(8,128)}), f32[32,8,128]{2,1,0:T(8,128)S(1)}, u32[]{:S(2)}, u32[]{:S(2)}) async-start(f32[32,8,128]{2,1,0:T(8,128)} %bitcast.35), calls=%async_computation | async-start | bytes 262144 | tf_op jit(solution)/shard_map/all_to_all | solution.py:816
  10.7 0.7 copy-start.9
  10.7 0.7 copy-start.11
  10.7 0.7 copy-start.12
  18.9 11.6 %copy-start = (f32[256,256]{1,0:T(8,128)S(1)}, f32[256,256]{1,0:T(8,128)}, u32[]{:S(2)}) copy-start(f32[256,256]{1,0:T(8,128)} %get-tuple-element.34.wide_ref) | copy-start | bytes 786436
  18.9 11.6 %copy-start.1 = (bf16[704,128]{1,0:T(8,128)(2,1)S(1)}, bf16[704,128]{1,0:T(8,128)(2,1)}, u32[]{:S(2)}) copy-start(bf16[704,128]{1,0:T(8,128)(2,1)} %get-tuple-element.35.inner_ref) | copy-start | bytes 540676
  20.5 10.0 %all-to-all-start.1 = ((f32[32,4,128]{2,1,0:T(4,128)}), f32[32,4,128]{2,1,0:T(4,128)S(1)}, u32[]{:S(2)}, u32[]{:S(2)}) async-start(f32[32,4,128]{2,1,0:T(4,128)} %bitcast.8), calls=%async_computation.1 | async-start | bytes 131072 | tf_op jit(solution)/shard_map/all_to_all | solution.py:816
  28.9 0.8 copy-start.2
  32.4 13.3 %all-to-all-start.2 = ((f32[32,8,128]{2,1,0:T(8,128)}), f32[32,8,128]{2,1,0:T(8,128)S(1)}, u32[]{:S(2)}, u32[]{:S(2)}) async-start(f32[32,8,128]{2,1,0:T(8,128)} %bitcast.10), calls=%async_computation.2 | async-start | bytes 262144 | tf_op jit(solution)/shard_map/all_to_all | solution.py:816
  46.2 0.7 copy-start.6
  46.9 0.6 copy-start.8
  47.5 10.0 %all-to-all-start.3 = ((f32[32,4,128]{2,1,0:T(4,128)}), f32[32,4,128]{2,1,0:T(4,128)S(1)}, u32[]{:S(2)}, u32[]{:S(2)}) async-start(f32[32,4,128]{2,1,0:T(4,128)} %bitcast.28), calls=%async_computation.3 | async-start | bytes 131072 | tf_op jit(solution)/shard_map/all_to_all | solution.py:816
  50.1 1.0 %copy-start.3 = (bf16[640,320]{1,0:T(8,128)(2,1)S(1)}, bf16[640,320]{1,0:T(8,128)(2,1)}, u32[]{:S(2)}) copy-start(bf16[640,320]{1,0:T(8,128)(2,1)} %copy-done.2) | copy-start | bytes 1228804
  51.1 0.9 %copy-start.7 = (f32[320,128]{1,0:T(8,128)S(1)}, f32[320,128]{1,0:T(8,128)}, u32[]{:S(2)}) copy-start(f32[320,128]{1,0:T(8,128)} %copy-done.6) | copy-start | bytes 491524
  54.2 0.7 copy-start.4
  58.6 14.8 %copy-start.5 = (f32[640,128]{1,0:T(8,128)S(1)}, f32[640,128]{1,0:T(8,128)}, u32[]{:S(2)}) copy-start(f32[640,128]{1,0:T(8,128)} %copy-done.4) | copy-start | bytes 983044
  74.8 11.2 %all-to-all-start.5 = ((f32[32,1,1280]{2,1,0:T(1,128)}), f32[32,1,1280]{2,1,0:T(1,128)S(1)}, u32[]{:S(2)}, u32[]{:S(2)}) async-start(f32[32,1,1280]{2,1,0:T(1,128)} %bitcast.17), calls=%async_computation.5 | async-start | bytes 327680 | tf_op jit(solution)/shard_map/all_to_all | solution.py:816
  77.4 1.7 %collective-permute-start = (f32[608,128]{1,0:T(8,128)S(1)}, f32[608,128]{1,0:T(8,128)S(1)}, u32[]{:S(2)}, u32[]{:S(2)}) collective-permute-start(f32[608,128]{1,0:T(8,128)S(1)} %bitcast.20), channel_id=1, source_target_pairs={{0,1},{1,0},{2,3},{3,2},{4,5},{5,4},{6,7},{7,6},{8,9},{9,8},{10,11... | collective-permute-start | bytes 933896 | tf_op jit(solution)/shard_map/ppermute | solution.py:899

commit v3 on v2

--- a/solution.py
+++ b/solution.py
@@ -392,14 +392,6 @@
     return jnp.where(gap == 0, 6.0, jnp.where(gap == 1, -4.0, jnp.where(gap == 2, 1.0, 0.0)))
 
 
-def three_terms(value):
-    high = value.astype(jnp.bfloat16)
-    rest = value - high.astype(f32)
-    middle = rest.astype(jnp.bfloat16)
-    low = (rest - middle.astype(f32)).astype(jnp.bfloat16)
-    return high, middle, low
-
-
 def choose(pieces, selector):
     out = None
     for piece in pieces:
@@ -416,91 +408,71 @@
     return out
 
 
-def select_first():
-    column = iota((N0, DEVICES * ROWS), 1)
-    chosen = L0 * (column % 32 // GRPS) + column // 32 // L1 == iota((N0, DEVICES * ROWS), 0)
-    return jnp.where(chosen, 1.0, 0.0).astype(jnp.bfloat16)
-
-
-def gram_rows(start0_ref, band0_ref, start1_ref, band1_ref, rows0_ref, rows1_ref, count):
-    total = DEVICES * ROWS
-    powers0 = powers(banded_t(start0_ref, band0_ref, K0, K0), count)
-    powers1 = powers(banded_t(start1_ref, band1_ref, K1, K1), count)
-    row0 = iota((total, N0), 0)
-    pick0 = L0 * (row0 % 32 // GRPS) + row0 // 32 // L1 == iota((total, N0), 1)
-    row1 = iota((total, N1), 0)
-    pick1 = L1 * (row1 % GRPS) + row1 // 32 % L1 == iota((total, N1), 1)
-    wide0 = mm_t(jnp.where(pick0, 1.0, 0.0), powers0[0])
-    wide1 = mm_t(jnp.where(pick1, 1.0, 0.0), powers1[0])
-    for k in range(count):
-        rows0_ref[:, 32 * k : 32 * k + 32] = mm(wide0, powers0[k])
-        rows1_ref[:, 16 * k : 16 * k + N1] = mm(wide1, powers1[k])
-    column = iota((N1, total), 1)
-    chosen = L1 * (column % GRPS) + column // 32 % L1 == iota((N1, total), 0)
-    select0, select1 = select_first(), jnp.where(chosen, 1.0, 0.0).astype(jnp.bfloat16)
-
-    def block(base):
-        block0 = rows0_ref[pl.ds(base, 32), :]
-        block1 = rows1_ref[pl.ds(base, 32), :]
-        g = [choose(three_terms(block0[:, 32 * k : 32 * k + 32]), select0) for k in range(count)]
-        h = [choose(three_terms(block1[:, 16 * k : 16 * k + N1]), select1) for k in range(count)]
-        return g, h
-
-    return block
-
-
 def store_split(high_ref, low_ref, rows, value):
     high, low = split(value)
     high_ref[rows, :] = high
     low_ref[rows, :] = low
 
 
-def gram_kernel(
-    start0_ref, band0_ref, start1_ref, band1_ref, gram_h_ref, gram_l_ref, rows0_ref, rows1_ref
+def matrix_kernel(
+    group_ref, start0_ref, band0_ref, start1_ref, band1_ref,
+    gram_h_ref, gram_l_ref, high_h_ref, high_l_ref, lift_h_ref, lift_l_ref, side_ref,
+    small_ref, rows0_h, rows0_l, rows1_h, rows1_l,
 ):
     total = DEVICES * ROWS
-    block = gram_rows(start0_ref, band0_ref, start1_ref, band1_ref, rows0_ref, rows1_ref, 2)
-
-    @pl.loop(0, ROWS)
+    powers0 = powers(banded_t(start0_ref, band0_ref, K0, K0), 4)
+    powers1 = powers(banded_t(start1_ref, band1_ref, K1, K1), 4)
+    small_ref[...] = jnp.zeros((48, 128), f32)
+    first, second = powers0[0].T, powers1[0].T
+    for k in range(4):
+        small_ref[0:N0, 32 * k : 32 * k + N0] = mm(first, powers0[k])
+        small_ref[N0 : N0 + N1, 32 * k : 32 * k + N1] = mm(second, powers1[k])
+    row0 = iota((total, N0), 0)
+    pick0 = L0 * (row0 % 32 // GRPS) + row0 // 32 // L1 == iota((total, N0), 1)
+    row1 = iota((total, 16), 0)
+    pick1 = L1 * (row1 % GRPS) + row1 // 32 % L1 == iota((total, 16), 1)
+    for pick, rows, targets in (
+        (pick0, slice(0, N0), (rows0_h, rows0_l)),
+        (pick1, slice(N0, N0 + 16), (rows1_h, rows1_l)),
+    ):
+        chooser = jnp.where(pick, 1.0, 0.0).astype(jnp.bfloat16)
+        for term, target in zip(split(small_ref[rows, :]), targets):
+            spread_out = jnp.dot(chooser, term, preferred_element_type=f32)
+            target[...] = spread_out.astype(jnp.bfloat16)
+    line, column = iota((128, total), 0), iota((128, total), 1)
+    match0 = line % 32 == L0 * (column % 32 // GRPS) + column // 32 // L1
+    match1 = line % 32 == L1 * (column % GRPS) + column // 32 % L1
+    select0 = [
+        jnp.where(match0 & (line // 32 == k), 1.0, 0.0).astype(jnp.bfloat16) for k in range(4)
+    ]
+    select1 = [
+        jnp.where(match1 & (line // 32 == k), 1.0, 0.0).astype(jnp.bfloat16) for k in range(4)
+    ]
+
+    @pl.loop(0, 5)
     def _(step):
-        base = pl.multiple_of(step * 32, 32)
-        g, h = block(base)
-        store_split(gram_h_ref, gram_l_ref, pl.ds(base, 32), g[0] * h[0])
-        store_split(
-            gram_h_ref, gram_l_ref, pl.ds(base + total, 32), g[1] * h[0] + g[0] * h[1]
-        )
-
-
-def high_kernel(
-    after_ref, start0_ref, band0_ref, start1_ref, band1_ref, high_h_ref, high_l_ref, token_ref,
-    rows0_ref, rows1_ref,
-):
-    token_ref[...] = after_ref[...]
-    total = DEVICES * ROWS
-    block = gram_rows(start0_ref, band0_ref, start1_ref, band1_ref, rows0_ref, rows1_ref, 4)
-
-    @pl.loop(0, ROWS)
-    def _(step):
-        base = pl.multiple_of(step * 32, 32)
-        g, h = block(base)
+        base = pl.multiple_of(step * 64, 64)
+        block0 = rows0_h[pl.ds(base, 64), :], rows0_l[pl.ds(base, 64), :]
+        block1 = rows1_h[pl.ds(base, 64), :], rows1_l[pl.ds(base, 64), :]
+        g = [choose(block0, selector) for selector in select0]
+        h = [choose(block1, selector) for selector in select1]
+        first_power = g[1] * h[0] + g[0] * h[1]
         squared = g[2] * h[0] + 2.0 * g[1] * h[1] + g[0] * h[2]
         cubed = g[3] * h[0] + 3.0 * (g[2] * h[1] + g[1] * h[2]) + g[0] * h[3]
-        store_split(high_h_ref, high_l_ref, pl.ds(base, 32), squared)
-        store_split(high_h_ref, high_l_ref, pl.ds(base + total, 32), cubed)
-
-
-def lift_kernel(
-    after_ref, group_ref, start0_ref, band0_ref, start1_ref, band1_ref,
-    lift_h_ref, lift_l_ref, side_ref, token_ref,
-):
-    token_ref[...] = after_ref[...]
-    total = DEVICES * ROWS
-    lifted = choose(three_terms(banded_t(start0_ref, band0_ref, K0, K0)), select_first())
-    column = iota((K0, total), 1)
-    owner = L1 * (column % GRPS) + column // 32 % L1
+        store_split(gram_h_ref, gram_l_ref, pl.ds(base, 64), g[0] * h[0])
+        store_split(gram_h_ref, gram_l_ref, pl.ds(base + total, 64), first_power)
+        store_split(high_h_ref, high_l_ref, pl.ds(base, 64), squared)
+        store_split(high_h_ref, high_l_ref, pl.ds(base + total, 64), cubed)
+
+    lifted = [
+        jnp.dot(term, select0[0][0:N0, :], preferred_element_type=f32)
+        for term in split(powers0[0])
+    ]
+    owner = L1 * (iota((K0, total), 1) % GRPS) + iota((K0, total), 1) // 32 % L1
     for n in range(N1):
         rows = slice(K0 * n, K0 * n + K0)
-        store_split(lift_h_ref, lift_l_ref, rows, jnp.where(owner == n, lifted, 0.0))
+        for term, target in zip(lifted, (lift_h_ref, lift_l_ref)):
+            target[rows, :] = jnp.where(owner == n, term, 0.0).astype(jnp.bfloat16)
     group = group_ref[0]
     coef = iota((128, K1), 0) % 32 + 32 * group
     pick_coef = jnp.where(coef == iota((128, K1), 1), 1.0, 0.0)
@@ -508,8 +480,8 @@
     wanted = L1 * jnp.where(half == group, 0, 1) + iota((N1, N1), 1) % L1
     reorder = jnp.where(iota((N1, N1), 0) == wanted, 1.0, 0.0)
     side_ref[...] = jnp.zeros((128, 256), f32)
-    for k, value in enumerate(powers(banded_t(start1_ref, band1_ref, K1, K1), 3)):
-        own = mm(pick_coef, value)
+    for k in range(3):
+        own = mm(pick_coef, powers1[k])
         halves = mm(own, reorder)
         for alpha in range(4):
             rows = slice(32 * alpha, 32 * alpha + 32)
@@ -528,7 +500,7 @@
     return move(ref[pl.ds(row, 32, stride=count), :], source, target)
 
 
-def first_column_kernel(recv_ref, gram_h_ref, gram_l_ref, send_ref, fields_ref, images_ref, token_ref):
+def first_column_kernel(recv_ref, gram_h_ref, gram_l_ref, send_ref, fields_ref, images_ref):
     total = DEVICES * ROWS
     zero = jnp.zeros((32, 128), f32)
     for r in range(ROWS):
@@ -552,7 +524,6 @@
     bend = jnp.sum(jnp.where(lane < 32, fields * pltpu.roll(images, 96, 1), 0.0))
     send_rows(send_ref, images_ref)
     spread(send_ref, 3, 4, (norm, bend))
-    token_ref[...] = lanes((norm, bend))
 
 
 def send_rows(send_ref, value_ref):
@@ -572,7 +543,7 @@
 
 
 def first_row_kernel(
-    recv_ref, wide_ref, inner_ref, after_ref, send_ref, scalar_ref, rows_ref, stack_ref,
+    recv_ref, wide_ref, inner_ref, send_ref, scalar_ref, rows_ref, stack_ref,
 ):
     norm, bend = totals(recv_ref, 3, 4, 2)
     scalar_ref[...] = lanes((norm, bend))
@@ -593,7 +564,7 @@
 
 
 def second_column_kernel(
-    recv_ref, gram_h_ref, gram_l_ref, fields_ref, images_ref, scalar_ref, after_ref,
+    recv_ref, gram_h_ref, gram_l_ref, fields_ref, images_ref, scalar_ref,
     send_ref, blend_ref, out_scalar_ref, next_ref, image_ref,
 ):
     zero = jnp.zeros((32, 128), f32)
@@ -852,34 +823,28 @@
         limit=LARGE,
     )
     recv = exchange(send)
-    gram = call(gram_kernel, pair_of(2 * total, total), [(total, 64), (total, 32)], *outer)
-    send, fields, images, token = call(
-        first_column_kernel, [(128, 128), (total, 128), (total, 128), (8, 128)], [], recv, *gram
+    group = lax.axis_index("grp").reshape(1)
+    *matrices, side = call(
+        matrix_kernel,
+        pair_of(2 * total, total) * 2 + pair_of(K0 * N1, total) + [(128, 256)],
+        [(48, 128)] + [pltpu.VMEM((total, 128), jnp.bfloat16)] * 4,
+        group, *outer,
+        scalars=(0,),
+    )
+    gram, high, lift = matrices[0:2], matrices[2:4], matrices[4:6]
+    send, fields, images = call(
+        first_column_kernel, [(128, 128), (total, 128), (total, 128)], [], recv, *gram
     )
     recv = exchange(send)
-    *high, token = call(
-        high_kernel,
-        pair_of(2 * total, total) + [(8, 128)],
-        [(total, 128), (total, 64)],
-        token, *outer,
-    )
     send, scalars = call(
-        first_row_kernel, [(256, 128), (8, 128)], work, recv, wide, inner, token
+        first_row_kernel, [(256, 128), (8, 128)], work, recv, wide, inner
     )
     recv = exchange(send)
-    group = lax.axis_index("grp").reshape(1)
-    *lift, side, token = call(
-        lift_kernel,
-        pair_of(K0 * N1, total) + [(128, 256), (8, 128)],
-        [],
-        scalars, group, *outer,
-        scalars=(1,),
-    )
     send, blend, scalars = call(
         second_column_kernel,
         [(128, 128), (total, 128), (8, 128)],
         [(total, 128), (total, 128)],
-        recv, *gram, fields, images, scalars, token,
+        recv, *gram, fields, images, scalars,
     )
     recv = exchange(send)
     send, keep, sums = call(

time: 87.8 us -> 83.3 us (0.949)
  blocking collectives: 14.8 us -> 34.9 us
  waiting for transfers between devices: 20.4 us -> 11.9 us
  Pallas kernels: 25.7 us -> 17.9 us
  starting transfers between devices: 20.2 us -> 12.6 us
    all_to_all x1 -> x3, blocking collectives: 14.8 us -> 34.9 us  [exchange(): lax.all_to_all(buffer.reshape(shape), ('slab', 'grp'), 0, 0, tiled=True)]
    all_to_all x5 -> x3, waiting for transfers between devices: 18.9 us -> 10.4 us  [exchange(): lax.all_to_all(buffer.reshape(shape), ('slab', 'grp'), 0, 0, tiled=True)]
    pallas_call x12 -> x10, Pallas kernels: 25.7 us -> 17.9 us  [call(): pl.pallas_call(kernel, out_shape=[shape if isinstance(shape, jax.ShapeDty...]
    all_to_all x5 -> x3, starting transfers between devices: 20.1 us -> 12.4 us  [exchange(): lax.all_to_all(buffer.reshape(shape), ('slab', 'grp'), 0, 0, tiled=True)]
    unnamed x26 -> x24, local copies, waits for them, and re-layouts: 5.38 us -> 4.78 us
  transfers between devices with their start and end apart: 6 -> 4, of which waited for: 6 -> 4; matrix products, arithmetic and copies ran while one was open for 0% -> 0% of each run, Pallas kernels for 17% -> 10%
where the time goes in v3:
time: 83.3 us; the launch traced here: 82.9 us
  blocking collectives  34.9 us (42%)
  Pallas kernels  17.9 us (21%)
  starting transfers between devices  12.6 us (15%)
  waiting for transfers between devices  11.9 us (14%)
  local copies, waits for them, and re-layouts  4.78 us (6%)
    all_to_all x3, blocking collectives, exchange(): lax.all_to_all(buffer.reshape(shape), ('slab', 'grp'), 0, 0, tiled=True)  34.9 us
    pallas_call x10, Pallas kernels, call(): pl.pallas_call(kernel, out_shape=[shape if isinstance(shape, jax.ShapeDty...  17.9 us
    all_to_all x3, starting transfers between devices, exchange(): lax.all_to_all(buffer.reshape(shape), ('slab', 'grp'), 0, 0, tiled=True)  12.4 us
    all_to_all x3, waiting for transfers between devices, exchange(): lax.all_to_all(buffer.reshape(shape), ('slab', 'grp'), 0, 0, tiled=True)  10.4 us
    unnamed x24, local copies, waits for them, and re-layouts  4.78 us
  transfers between devices with their start and end apart: 4, of which 4 were waited for; matrix products, arithmetic and copies ran while one was open for 0% of the time, Pallas kernels for 10%

profile of v3, /device:TPU:0, one launch (start us, length us, event | category | flops | bytes accessed | tf_op | source)
XLA Modules:
  0.0 82.9 jit_solution(3498514856929588753)
XLA Ops:
  0.6 2.7 %shard_map.113 = (f32[256,128]{1,0:T(8,128)}, f32[256,256]{1,0:T(8,128)}, bf16[704,128]{1,0:T(8,128)(2,1)}) custom-call(f32[5,2,3200]{2,1,0:T(2,128)} %bitcast.33, f32[5,2,3200]{2,1,0:T(2,128)} %bitcast.34, s32[64]{0:T(128)} %start2_hbm.1, f32[4,64]{1,0:T(4,128)} %bitcast.35, s32[50]{0:T(128)} %start3_hbm.1, f32[4,50]{1,0:T(4,128)} %bitcast.36), custom_call_target="tpu_custom_call" | custom-call | tf_op jit(solution)/shard_map/pallas_call | solution.py:763
  3.3 7.3 %all-to-all-start = ((f32[32,8,128]{2,1,0:T(8,128)}), f32[32,8,128]{2,1,0:T(8,128)S(1)}, u32[]{:S(2)}, u32[]{:S(2)}) async-start(f32[32,8,128]{2,1,0:T(8,128)} %bitcast.32), calls=%async_computation | async-start | bytes 262144 | tf_op jit(solution)/shard_map/all_to_all | solution.py:787
  10.6 0.0 copy-start.9
  10.7 0.0 copy-start.8
  10.7 0.6 copy-done.9
  11.3 0.0 copy-done.8
  11.3 3.9 %shard_map.114 = (bf16[640,320]{1,0:T(8,128)(2,1)S(1)}, bf16[640,320]{1,0:T(8,128)(2,1)S(1)}, bf16[640,320]{1,0:T(8,128)(2,1)S(1)}, bf16[640,320]{1,0:T(8,128)(2...) custom-call(s32[1]{0:T(128)} %bitcast.6.group_ref, s32[32]{0:T(128)S(1)} %copy-done.10, ...), custom_call_target="tpu_custom_call" | custom-call | tf_op jit(solution)/shard_map/pallas_call | solution.py:763
  15.3 0.8 copy-done.2
  16.1 2.8 %all-to-all-done = f32[32,8,128]{2,1,0:T(8,128)S(1)} async-done(((f32[32,8,128]{2,1,0:T(8,128)}), f32[32,8,128]{2,1,0:T(8,128)S(1)}, u32[]{:S(2)}, u32[]{:S(2)}) %all-to-all-start) | async-done | bytes 131104 | tf_op jit(solution)/shard_map/all_to_all | solution.py:787
  18.9 1.0 %shard_map.115 = (f32[128,128]{1,0:T(8,128)S(1)}, f32[320,128]{1,0:T(8,128)S(1)}, f32[320,128]{1,0:T(8,128)S(1)}) custom-call(f32[256,128]{1,0:T(8,128)S(1)} %bitcast.24, bf16[640,320]{1,0:T(8,128)(2,1)S(1)} %get-tuple-element.28.gram_h_ref, bf16[640,320]{1,0:T(8,128)(2,1)S(1)} %get-tuple-element.29.gram_l_ref), custom_call_target="tpu_custom_call" | custom-call | tf_op jit(solution)/shard_map/pallas_call | solution.py:763
  19.8 10.2 %all_to_all.30 = f32[32,4,128]{2,1,0:T(4,128)S(1)} all-to-all(f32[32,4,128]{2,1,0:T(4,128)S(1)} %bitcast.29), channel_id=1, replica_groups=mesh['slab'=16,'grp'=2] {'slab','grp'}, dimensions={0} | all-to-all | bytes 131072 | tf_op jit(solution)/shard_map/all_to_all | solution.py:787
  30.1 1.3 %shard_map.116 = (f32[256,128]{1,0:T(8,128)S(1)}, f32[8,128]{1,0:T(8,128)S(1)}) custom-call(f32[128,128]{1,0:T(8,128)S(1)} %bitcast.27, f32[256,256]{1,0:T(8,128)S(1)} %copy-done, bf16[704,128]{1,0:T(8,128)(2,1)S(1)} %copy-done.1), custom_call_target="tpu_custom_call" | custom-call | tf_op jit(solution)/shard_map/pallas_call | solution.py:763
  31.3 9.9 %all_to_all.31 = f32[32,8,128]{2,1,0:T(8,128)S(1)} all-to-all(f32[32,8,128]{2,1,0:T(8,128)S(1)} %bitcast.28), channel_id=1, replica_groups=mesh['slab'=16,'grp'=2] {'slab','grp'}, dimensions={0} | all-to-all | bytes 262144 | tf_op jit(solution)/shard_map/all_to_all | solution.py:787
  41.3 1.2 %shard_map.117 = (f32[128,128]{1,0:T(8,128)}, f32[320,128]{1,0:T(8,128)S(1)}, f32[8,128]{1,0:T(8,128)S(1)}) custom-call(f32[256,128]{1,0:T(8,128)S(1)} %bitcast.25, bf16[640,320]{1,0:T(8,128)(2,1)S(1)} %get-tuple-element.28.gram_h_ref, bf16[640,320]{1,0:T(8,128)(2,1)S(1)} %get-tuple-element.29.gram_l_ref, f32[320,128]{1,0:T(8,128)S(1)} %get-tuple-element.34.fields_ref, ...), custom_call_target="tpu_custom_call" | custom-call | tf_op jit(solution)/shard_map/pallas_call | solution.py:763
  42.4 0.7 copy-done.6
  43.1 2.5 %all-to-all-start.3 = ((f32[32,4,128]{2,1,0:T(4,128)}), f32[32,4,128]{2,1,0:T(4,128)S(1)}, u32[]{:S(2)}, u32[]{:S(2)}) async-start(f32[32,4,128]{2,1,0:T(4,128)} %bitcast.13), calls=%async_computation.3 | async-start | bytes 131072 | tf_op jit(solution)/shard_map/all_to_all | solution.py:787
  45.6 0.0 copy-start.3
  45.7 1.0 %copy-done.3 = bf16[640,320]{1,0:T(8,128)(2,1)S(1)} copy-done((bf16[640,320]{1,0:T(8,128)(2,1)S(1)}, bf16[640,320]{1,0:T(8,128)(2,1)}, u32[]{:S(2)}) %copy-start.3) | copy-done | bytes 409624
  46.7 0.9 %copy-done.7 = f32[320,128]{1,0:T(8,128)S(1)} copy-done((f32[320,128]{1,0:T(8,128)S(1)}, f32[320,128]{1,0:T(8,128)}, u32[]{:S(2)}) %copy-start.7) | copy-done | bytes 163864
  47.6 2.1 %shard_map.118 = (f32[608,128]{1,0:T(8,128)S(1)}, f32[640,128]{1,0:T(8,128)S(1)}, f32[8,128]{1,0:T(8,128)S(1)}) custom-call(f32[320,128]{1,0:T(8,128)S(1)} %copy-done.7, bf16[640,320]{1,0:T(8,128)(2,1)S(1)} %get-tuple-element.28.gram_h_ref, bf16[640,320]{1,0:T(8,128)(2,1)S(1)} %get-tuple-element.29.gram_l_ref, ...), custom_call_target="tpu_custom_call" | custom-call | tf_op jit(solution)/shard_map/pallas_call | solution.py:763
  49.8 0.0 copy-start.4
  49.8 0.7 copy-done.4
  50.5 2.6 %all-to-all-done.3 = f32[32,4,128]{2,1,0:T(4,128)S(1)} async-done(((f32[32,4,128]{2,1,0:T(4,128)}), f32[32,4,128]{2,1,0:T(4,128)S(1)}, u32[]{:S(2)}, u32[]{:S(2)}) %all-to-all-start.3) | async-done | bytes 65568 | tf_op jit(solution)/shard_map/all_to_all | solution.py:787
  53.1 1.1 %shard_map.119 = f32[608,128]{1,0:T(8,128)S(1)} custom-call(f32[608,128]{1,0:T(8,128)S(1)} %get-tuple-element.43.early_ref, f32[128,128]{1,0:T(8,128)S(1)} %bitcast.26, f32[8,128]{1,0:T(8,128)S(1)} %get-tuple-element.45.sums_ref, f32[256,256]{1,0:T(8,128)S(1)} %copy-done, bf16[704,128]{1,0:T(8,128)(2,1)S(1)} %copy-done.1), custom_call_target="tpu_custom_call", output_to_operand_aliasing={{}: (0, {})} | custom-call | tf_op jit(solution)/shard_map/pallas_call | solution.py:763
  54.2 14.8 %all_to_all.32 = f32[32,1,2432]{2,1,0:T(1,128)S(1)} all-to-all(f32[32,1,2432]{2,1,0:T(1,128)S(1)} %bitcast.22), channel_id=1, replica_groups=mesh['slab'=16,'grp'=2] {'slab','grp'}, dimensions={0} | all-to-all | bytes 622592 | tf_op jit(solution)/shard_map/all_to_all | solution.py:787
  69.0 1.4 %shard_map.120 = (f32[320,128]{1,0:T(8,128)}, f32[8,128]{1,0:T(8,128)S(1)}) custom-call(f32[608,128]{1,0:T(8,128)S(1)} %bitcast.19, bf16[640,320]{1,0:T(8,128)(2,1)S(1)} %get-tuple-element.40.lift_h_ref, bf16[640,320]{1,0:T(8,128)(2,1)S(1)} %get-tuple-element.41.lift_l_ref, f32[640,128]{1,0:T(8,128)S(1)} %copy-done.5, f32[8,128]{1,0:T(8,128)S(1)} %get-tuple-element.42.scalar_ref), custom_call_target="tpu_custom_call" | custom-call | tf_op jit(solution)/shard_map/pallas_call | solution.py:763
  70.4 2.6 %all-to-all-start.5 = ((f32[32,1,1280]{2,1,0:T(1,128)}), f32[32,1,1280]{2,1,0:T(1,128)S(1)}, u32[]{:S(2)}, u32[]{:S(2)}) async-start(f32[32,1,1280]{2,1,0:T(1,128)} %bitcast.17), calls=%async_computation.5 | async-start | bytes 327680 | tf_op jit(solution)/shard_map/all_to_all | solution.py:787
  73.0 0.2 collective-permute-start
  73.1 1.5 %collective-permute-done.partner_ref = f32[608,128]{1,0:T(8,128)S(1)} collective-permute-done((f32[608,128]{1,0:T(8,128)S(1)}, f32[608,128]{1,0:T(8,128)S(1)}, u32[]{:S(2)}, u32[]{:S(2)}) %collective-permute-start) | collective-permute-done | bytes 311328 | tf_op jit(solution)/shard_map/ppermute | solution.py:864
  74.6 1.9 %shard_map.121 = (f32[4,32,1024]{2,1,0:T(8,128)}, f32[128,1024]{1,0:T(8,128)S(1)}) custom-call(f32[608,128]{1,0:T(8,128)S(1)} %bitcast.21, f32[608,128]{1,0:T(8,128)S(1)} %collective-permute-done.partner_ref, f32[128,256]{1,0:T(8,128)S(1)} %get-tuple-element.46.side_ref, f32[8,128]{1,0:T(8,128)S(1)} %get-tuple-element.48.scalar_ref), custom_call_target="tpu_custom_call" | custom-call | tf_op jit(solution)/shard_map/pallas_call | solution.py:763
  76.5 5.0 %all-to-all-done.5 = f32[32,1,1280]{2,1,0:T(1,128)S(1)} async-done(((f32[32,1,1280]{2,1,0:T(1,128)}), f32[32,1,1280]{2,1,0:T(1,128)S(1)}, u32[]{:S(2)}, u32[]{:S(2)}) %all-to-all-start.5) | async-done | bytes 163872 | tf_op jit(solution)/shard_map/all_to_all | solution.py:787
  81.5 1.3 %shard_map.122 = f32[4,32,1024]{2,1,0:T(8,128)} custom-call(f32[320,128]{1,0:T(8,128)S(1)} %bitcast.23, f32[128,256]{1,0:T(8,128)S(1)} %get-tuple-element.46.side_ref, f32[128,1024]{1,0:T(8,128)S(1)} %get-tuple-element.51.part_ref), custom_call_target="tpu_custom_call" | custom-call | tf_op jit(solution)/shard_map/pallas_call | solution.py:763
  (13 shorter events, 0.0 us)
Async XLA Ops:
  3.3 15.5 %all-to-all-start = ((f32[32,8,128]{2,1,0:T(8,128)}), f32[32,8,128]{2,1,0:T(8,128)S(1)}, u32[]{:S(2)}, u32[]{:S(2)}) async-start(f32[32,8,128]{2,1,0:T(8,128)} %bitcast.32), calls=%async_computation | async-start | bytes 262144 | tf_op jit(solution)/shard_map/all_to_all | solution.py:787
  10.6 0.7 copy-start.9
  10.7 0.7 copy-start.8
  10.7 0.7 copy-start.10
  10.7 0.7 copy-start.11
  15.3 0.8 copy-start.2
  18.9 11.2 %copy-start = (f32[256,256]{1,0:T(8,128)S(1)}, f32[256,256]{1,0:T(8,128)}, u32[]{:S(2)}) copy-start(f32[256,256]{1,0:T(8,128)} %get-tuple-element.31.wide_ref) | copy-start | bytes 786436
  18.9 11.2 %copy-start.1 = (bf16[704,128]{1,0:T(8,128)(2,1)S(1)}, bf16[704,128]{1,0:T(8,128)(2,1)}, u32[]{:S(2)}) copy-start(bf16[704,128]{1,0:T(8,128)(2,1)} %get-tuple-element.32.inner_ref) | copy-start | bytes 540676
  42.4 0.7 copy-start.6
  43.1 10.0 %all-to-all-start.3 = ((f32[32,4,128]{2,1,0:T(4,128)}), f32[32,4,128]{2,1,0:T(4,128)S(1)}, u32[]{:S(2)}, u32[]{:S(2)}) async-start(f32[32,4,128]{2,1,0:T(4,128)} %bitcast.13), calls=%async_computation.3 | async-start | bytes 131072 | tf_op jit(solution)/shard_map/all_to_all | solution.py:787
  45.6 1.0 %copy-start.3 = (bf16[640,320]{1,0:T(8,128)(2,1)S(1)}, bf16[640,320]{1,0:T(8,128)(2,1)}, u32[]{:S(2)}) copy-start(bf16[640,320]{1,0:T(8,128)(2,1)} %copy-done.2) | copy-start | bytes 1228804
  46.7 0.9 %copy-start.7 = (f32[320,128]{1,0:T(8,128)S(1)}, f32[320,128]{1,0:T(8,128)}, u32[]{:S(2)}) copy-start(f32[320,128]{1,0:T(8,128)} %copy-done.6) | copy-start | bytes 491524
  49.8 0.7 copy-start.4
  54.2 14.8 %copy-start.5 = (f32[640,128]{1,0:T(8,128)S(1)}, f32[640,128]{1,0:T(8,128)}, u32[]{:S(2)}) copy-start(f32[640,128]{1,0:T(8,128)} %copy-done.4) | copy-start | bytes 983044
  70.4 11.2 %all-to-all-start.5 = ((f32[32,1,1280]{2,1,0:T(1,128)}), f32[32,1,1280]{2,1,0:T(1,128)S(1)}, u32[]{:S(2)}, u32[]{:S(2)}) async-start(f32[32,1,1280]{2,1,0:T(1,128)} %bitcast.17), calls=%async_computation.5 | async-start | bytes 327680 | tf_op jit(solution)/shard_map/all_to_all | solution.py:787
  73.0 1.7 %collective-permute-start = (f32[608,128]{1,0:T(8,128)S(1)}, f32[608,128]{1,0:T(8,128)S(1)}, u32[]{:S(2)}, u32[]{:S(2)}) collective-permute-start(f32[608,128]{1,0:T(8,128)S(1)} %bitcast.20), channel_id=1, source_target_pairs={{0,1},{1,0},{2,3},{3,2},{4,5},{5,4},{6,7},{7,6},{8,9},{9,8},{10,11... | collective-permute-start | bytes 933896 | tf_op jit(solution)/shard_map/ppermute | solution.py:864

commit v4 on v3

--- a/solution.py
+++ b/solution.py
@@ -323,7 +323,7 @@
 
 def start_kernel(
     table_hbm, weight_hbm, start2_hbm, band2_hbm, start3_hbm, band3_hbm,
-    send_ref, wide_ref, inner_ref,
+    send_ref, wide_ref, inner_ref, mixed_ref,
     table_ref, weight_ref, start2_ref, band2_ref, start3_ref, band3_ref, sems,
     product_ref, packed_ref, field_ref, rows_ref, stack_ref,
 ):
@@ -378,13 +378,13 @@
             target[16 * p : 16 * p + 16, 128:256] = high
     mixed = table_to_mixed(field_ref[...], kron, turned, rows_ref, stack_ref)
     once = inner_penalty(mixed)
-    twice = inner_penalty(once)
-    for base, value in ((0, mixed), (3, once), (5, twice)):
-        put(send_ref, base, 8, tile_of(value, 0))
-        put(send_ref, base + 1, 8, tile_of(value, 1))
+    mixed_ref[0:32, :] = mixed
+    mixed_ref[32:64, :] = once
+    for base, value in ((0, mixed), (3, once)):
+        put(send_ref, base, 5, tile_of(value, 0))
+        put(send_ref, base + 1, 5, tile_of(value, 1))
     lane = iota((32, 128), 1)
-    put(send_ref, 2, 8, jnp.where(lane < 64, tile_of(mixed, 2), pltpu.roll(tile_of(once, 2), 64, 1)))
-    put(send_ref, 7, 8, tile_of(twice, 2))
+    put(send_ref, 2, 5, jnp.where(lane < 64, tile_of(mixed, 2), pltpu.roll(tile_of(once, 2), 64, 1)))
 
 
 def pentadiagonal(n):
@@ -479,7 +479,7 @@
     half = iota((N1, N1), 1) // L1
     wanted = L1 * jnp.where(half == group, 0, 1) + iota((N1, N1), 1) % L1
     reorder = jnp.where(iota((N1, N1), 0) == wanted, 1.0, 0.0)
-    side_ref[...] = jnp.zeros((128, 256), f32)
+    side_ref[...] = jnp.zeros((128, 384), f32)
     for k in range(3):
         own = mm(pick_coef, powers1[k])
         halves = mm(own, reorder)
@@ -490,8 +490,7 @@
             for h in range(2):
                 piece = halves[rows, L1 * h : L1 * h + L1]
                 place = 40 * k + 20 * h + L1 * alpha
-                if k > 0:
-                    side_ref[rows, place : place + L1] = piece
+                side_ref[rows, 256 + place : 256 + place + L1] = piece
                 if k < 2:
                     side_ref[rows, 128 + place : 128 + place + L1] = piece
 
@@ -507,10 +506,8 @@
         j, q = r // 4, r % 4
         where0 = (j, q) if j < 2 else (2, q)
         where1 = (3 + j, q) if j < 2 else (2, q + 2)
-        where2 = (5 + j, q) if j < 2 else (7, q)
         parts = [
-            unpack(recv_ref, place[0], 8, r, place[1], k)
-            for k, place in enumerate((where0, where1, where2))
+            unpack(recv_ref, place[0], 5, r, place[1], k) for k, place in enumerate((where0, where1))
         ]
         fields_ref[32 * r : 32 * r + 32, :] = merge(parts + [zero])
     fields = fields_ref[...]
@@ -543,7 +540,7 @@
 
 
 def first_row_kernel(
-    recv_ref, wide_ref, inner_ref, send_ref, scalar_ref, rows_ref, stack_ref,
+    recv_ref, wide_ref, inner_ref, start_ref, send_ref, scalar_ref, mixed_ref, rows_ref, stack_ref,
 ):
     norm, bend = totals(recv_ref, 3, 4, 2)
     scalar_ref[...] = lanes((norm, bend))
@@ -552,15 +549,11 @@
     weighted = wide_ref[...] * field
     energy = jnp.sum(field * weighted)
     mixed = table_to_mixed(weighted, kron, turned, rows_ref, stack_ref)
-    once = inner_penalty(mixed)
-    for base, value in ((0, mixed), (3, once)):
-        put(send_ref, base, 8, tile_of(value, 0))
-        put(send_ref, base + 1, 8, tile_of(value, 1))
-    lane = iota((32, 128), 1)
-    put(send_ref, 2, 8, jnp.where(lane < 64, tile_of(mixed, 2), pltpu.roll(tile_of(once, 2), 64, 1)))
-    spread(send_ref, 5, 8, (energy,))
-    for row in (6, 7):
-        put(send_ref, row, 8, jnp.zeros((32, 128), f32))
+    mixed_ref[0:32, :] = mixed
+    mixed_ref[32:96, :] = start_ref[...]
+    for j in range(3):
+        put(send_ref, j, 4, tile_of(mixed, j))
+    spread(send_ref, 3, 4, (energy,))
 
 
 def second_column_kernel(
@@ -569,14 +562,9 @@
 ):
     zero = jnp.zeros((32, 128), f32)
     for r in range(ROWS):
-        j, q = r // 4, r % 4
-        where0 = (j, q) if j < 2 else (2, q)
-        where1 = (3 + j, q) if j < 2 else (2, q + 2)
-        parts = [
-            unpack(recv_ref, place[0], 8, r, place[1], k) for k, place in enumerate((where0, where1))
-        ]
-        next_ref[32 * r : 32 * r + 32, :] = merge(parts + [zero])
-    (energy,) = totals(recv_ref, 5, 8, 1)
+        part = unpack(recv_ref, r // 4, 4, r, r % 4, 0)
+        next_ref[32 * r : 32 * r + 32, :] = merge([part, zero])
+    (energy,) = totals(recv_ref, 3, 4, 1)
     norm, bend = pick(scalar_ref, 0), pick(scalar_ref, 1)
     step = norm / (energy + 0.1 * bend)
     out_scalar_ref[...] = lanes((norm, step))
@@ -588,7 +576,8 @@
     put(send_ref, 3, 4, zero)
     lane = iota(fields.shape, 1)
     reduced = fields - step * (following + 0.1 * pltpu.roll(fields, 96, 1))
-    blend_ref[...] = jnp.where(lane < 64, reduced, pltpu.roll(fields, 64, 1))
+    kept = jnp.where(lane < 64, 0.0, pltpu.roll(fields, 64, 1))
+    blend_ref[...] = jnp.where(lane < 32, reduced, kept)
 
 
 def coefficient_penalty(value):
@@ -654,9 +643,7 @@
     twice = coefficient_penalty(once)
     h_a = lifted - small * pltpu.roll(once, 64, 1)
     y_1 = once + pltpu.roll(lifted, 96, 1)
-    x_a = once + pltpu.roll(lifted, 96, 1) - small * (
-        pltpu.roll(twice, 64, 1) + pltpu.roll(once, 32, 1)
-    )
+    x_a = once - small * pltpu.roll(twice, 64, 1)
     h_0 = pltpu.roll(lifted, 64, 1)
     wide = iota(lifted.shape, 1)
     keep = jnp.where(
@@ -668,17 +655,21 @@
 
 
 def second_row_kernel(
-    early_ref, recv_ref, sums_ref, wide_ref, inner_ref,
+    early_ref, recv_ref, sums_ref, scalar_ref, mixed_ref, wide_ref, inner_ref,
     send_ref, rows_ref, stack_ref,
 ):
     kron, second, turned = constants(inner_ref)
-    field = mixed_to_table(received_rows(recv_ref), kron, second, rows_ref, stack_ref)
+    image = received_rows(recv_ref)
+    step = pick(scalar_ref, 1)
+    reduced = mixed_ref[32:64, :] - step * (mixed_ref[0:32, :] + 0.1 * mixed_ref[64:96, :])
+    inner = jnp.sum(reduced * inner_penalty(image))
+    field = mixed_to_table(image, kron, second, rows_ref, stack_ref)
     weighted = wide_ref[...] * field
     energy = jnp.sum(field * weighted)
     mixed = table_to_mixed(weighted, kron, turned, rows_ref, stack_ref)
     for j in range(3):
         put(send_ref, j, JOINT, tile_of(mixed, j))
-    spread(send_ref, 3, JOINT, (energy, pick(sums_ref, 0), pick(sums_ref, 1)))
+    spread(send_ref, 3, JOINT, (energy, pick(sums_ref, 0), pick(sums_ref, 1) + inner))
 
 
 def third_column_kernel(
@@ -718,6 +709,20 @@
     )
 
 
+def bent_rows(value):
+    lane = iota(value.shape, 1)
+    inside = lane % 32
+    total = 12.0 * value
+    for d, weight in ((1, -4.0), (2, 1.0)):
+        total = total + weight * (
+            jnp.where(lane >= 32 * d, pltpu.roll(value, 32 * d, 1), 0.0)
+            + jnp.where(lane < 1024 - 32 * d, pltpu.roll(value, 1024 - 32 * d, 1), 0.0)
+            + jnp.where(inside >= d, pltpu.roll(value, d, 1), 0.0)
+            + jnp.where(inside < 32 - d, pltpu.roll(value, 1024 - d, 1), 0.0)
+        )
+    return total
+
+
 def settle_kernel(own_ref, partner_ref, side_ref, scalar_ref, solution_ref, part_ref, early):
     for block in range(3):
         for h, ref in enumerate((own_ref, partner_ref)):
@@ -725,7 +730,8 @@
     step, ratio, step_next = pick(scalar_ref, 1), pick(scalar_ref, 2), pick(scalar_ref, 3)
     small = 0.1 * step
     value = split(side_ref[:, 128:208])
-    slope = split(side_ref[:, 40:120])
+    slope = split(side_ref[:, 256:376])
+    bent = bent_rows(jnp.concatenate([take(early, 1, tile) for tile in range(8)], axis=1))
     for tile in range(8):
         h_0, h_a, y_1 = take(early, 0, tile), take(early, 1, tile), take(early, 2, tile)
         right = jnp.concatenate(
@@ -735,6 +741,7 @@
         solution_ref[:, :, columns] = product(value, split(right)).reshape(4, 32, 128)
         right = jnp.concatenate(
             [
+                (-0.1 * step_next) * bent[:, columns],
                 (-small * (1.0 + step_next * ratio / step)) * h_0
                 - (0.1 * step_next) * (h_a - small * y_1),
                 (0.1 * step_next * small) * h_0,
@@ -811,9 +818,9 @@
         fourth_start,
         fourth_band.T,
     )
-    send, wide, inner = call(
+    send, wide, inner, mixed0 = call(
         start_kernel,
-        [(256, 128), (256, 256), jax.ShapeDtypeStruct((704, 128), jnp.bfloat16)],
+        [(160, 128), (256, 256), jax.ShapeDtypeStruct((704, 128), jnp.bfloat16), (64, 384)],
         [pltpu.VMEM(value.shape, value.dtype) for value in inputs]
         + [pltpu.SemaphoreType.DMA((len(inputs),))]
         + [(16, N2 * N3), (16, N2 * N3), (256, 256)]
@@ -826,7 +833,7 @@
     group = lax.axis_index("grp").reshape(1)
     *matrices, side = call(
         matrix_kernel,
-        pair_of(2 * total, total) * 2 + pair_of(K0 * N1, total) + [(128, 256)],
+        pair_of(2 * total, total) * 2 + pair_of(K0 * N1, total) + [(128, 384)],
         [(48, 128)] + [pltpu.VMEM((total, 128), jnp.bfloat16)] * 4,
         group, *outer,
         scalars=(0,),
@@ -836,8 +843,8 @@
         first_column_kernel, [(128, 128), (total, 128), (total, 128)], [], recv, *gram
     )
     recv = exchange(send)
-    send, scalars = call(
-        first_row_kernel, [(256, 128), (8, 128)], work, recv, wide, inner
+    send, scalars, mixed1 = call(
+        first_row_kernel, [(128, 128), (8, 128), (96, 384)], work, recv, wide, inner, mixed0
     )
     recv = exchange(send)
     send, blend, scalars = call(
@@ -845,6 +852,7 @@
         [(128, 128), (total, 128), (8, 128)],
         [(total, 128), (total, 128)],
         recv, *gram, fields, images, scalars,
+        aliases={3: 1},
     )
     recv = exchange(send)
     send, keep, sums = call(
@@ -857,7 +865,7 @@
         second_row_kernel,
         [(DEVICES * JOINT, 128)],
         work,
-        send, recv, sums, wide, inner,
+        send, recv, sums, scalars, mixed1, wide, inner,
         aliases={0: 0},
     )
     recv = exchange(send)

time: 83.3 us -> 83 us (level)
    all_to_all x3, waiting for transfers between devices: 10.4 us -> 9.56 us  [exchange(): lax.all_to_all(buffer.reshape(shape), ('slab', 'grp'), 0, 0, tiled=True)]
    unnamed x24 -> x26, local copies, waits for them, and re-layouts: 4.78 us -> 5.2 us
where the time goes in v4:
time: 83 us; the launch traced here: 82.5 us
  blocking collectives  34.8 us (42%)
  Pallas kernels  18 us (22%)
  starting transfers between devices  12.6 us (15%)
  waiting for transfers between devices  11.1 us (13%)
  local copies, waits for them, and re-layouts  5.2 us (6%)
    all_to_all x3, blocking collectives, exchange(): lax.all_to_all(buffer.reshape(shape), ('slab', 'grp'), 0, 0, tiled=True)  34.8 us
    pallas_call x10, Pallas kernels, call(): pl.pallas_call(kernel, out_shape=[shape if isinstance(shape, jax.ShapeDty...  18 us
    all_to_all x3, starting transfers between devices, exchange(): lax.all_to_all(buffer.reshape(shape), ('slab', 'grp'), 0, 0, tiled=True)  12.4 us
    all_to_all x3, waiting for transfers between devices, exchange(): lax.all_to_all(buffer.reshape(shape), ('slab', 'grp'), 0, 0, tiled=True)  9.56 us
    unnamed x26, local copies, waits for them, and re-layouts  5.2 us
  transfers between devices with their start and end apart: 4, of which 4 were waited for; matrix products, arithmetic and copies ran while one was open for 0% of the time, Pallas kernels for 10%

profile of v4, /device:TPU:0, one launch (start us, length us, event | category | flops | bytes accessed | tf_op | source)
XLA Modules:
  0.0 82.5 jit_solution(13312414908976943427)
XLA Ops:
  0.6 2.8 %shard_map.113 = (f32[160,128]{1,0:T(8,128)}, f32[256,256]{1,0:T(8,128)}, bf16[704,128]{1,0:T(8,128)(2,1)}, f32[64,384]{1,0:T(8,128)}) custom-call(f32[5,2,3200]{2,1,0:T(2,128)} %bitcast.32, f32[5,2,3200]{2,1,0:T(2,128)} %bitcast.33, s32[64]{0:T(128)} %start2_hbm.1, f32[4,64]{1,0:T(4,128)} %bitcast.35, s32[50]{0:T(128)} %start3_hbm.1, f32[4,50]{1,0:T(4,128)} %bitcast.36), custom_call_target="tpu_custom_call" | custom-call | tf_op jit(solution)/shard_map/pallas_call | solution.py:770
  3.5 7.3 %all-to-all-start = ((f32[32,1,640]{2,1,0:T(1,128)}), f32[32,1,640]{2,1,0:T(1,128)S(1)}, u32[]{:S(2)}, u32[]{:S(2)}) async-start(f32[32,1,640]{2,1,0:T(1,128)} %bitcast.34), calls=%async_computation | async-start | bytes 163840 | tf_op jit(solution)/shard_map/all_to_all | solution.py:794
  10.8 0.0 copy-start.11
  10.8 0.0 copy-start.12
  10.8 0.6 copy-done.10
  11.5 0.0 copy-done.9
  11.5 3.9 %shard_map.114 = (bf16[640,320]{1,0:T(8,128)(2,1)S(1)}, bf16[640,320]{1,0:T(8,128)(2,1)S(1)}, bf16[640,320]{1,0:T(8,128)(2,1)S(1)}, bf16[640,320]{1,0:T(8,128)(2...) custom-call(s32[1]{0:T(128)} %bitcast.6.group_ref, s32[32]{0:T(128)S(1)} %copy-done.11, ...), custom_call_target="tpu_custom_call" | custom-call | tf_op jit(solution)/shard_map/pallas_call | solution.py:770
  15.4 0.0 copy-start.2
  15.4 0.8 copy-done.2
  16.2 0.8 copy-done.4
  17.0 1.4 %all-to-all-done = f32[32,1,640]{2,1,0:T(1,128)S(1)} async-done(((f32[32,1,640]{2,1,0:T(1,128)}), f32[32,1,640]{2,1,0:T(1,128)S(1)}, u32[]{:S(2)}, u32[]{:S(2)}) %all-to-all-start) | async-done | bytes 81952 | tf_op jit(solution)/shard_map/all_to_all | solution.py:794
  18.4 0.9 %shard_map.115 = (f32[128,128]{1,0:T(8,128)S(1)}, f32[320,128]{1,0:T(8,128)S(1)}, f32[320,128]{1,0:T(8,128)S(1)}) custom-call(f32[160,128]{1,0:T(8,128)S(1)} %bitcast.24, bf16[640,320]{1,0:T(8,128)(2,1)S(1)} %get-tuple-element.30.gram_h_ref, bf16[640,320]{1,0:T(8,128)(2,1)S(1)} %get-tuple-element.31.gram_l_ref), custom_call_target="tpu_custom_call" | custom-call | tf_op jit(solution)/shard_map/pallas_call | solution.py:770
  19.3 11.6 %all_to_all.30 = f32[32,4,128]{2,1,0:T(4,128)S(1)} all-to-all(f32[32,4,128]{2,1,0:T(4,128)S(1)} %bitcast.29), channel_id=1, replica_groups=mesh['slab'=16,'grp'=2] {'slab','grp'}, dimensions={0} | all-to-all | bytes 131072 | tf_op jit(solution)/shard_map/all_to_all | solution.py:794
  31.0 1.2 %shard_map.116 = (f32[128,128]{1,0:T(8,128)S(1)}, f32[8,128]{1,0:T(8,128)S(1)}, f32[96,384]{1,0:T(8,128)S(1)}) custom-call(f32[128,128]{1,0:T(8,128)S(1)} %bitcast.26, f32[256,256]{1,0:T(8,128)S(1)} %copy-done, bf16[704,128]{1,0:T(8,128)(2,1)S(1)} %copy-done.1, f32[64,384]{1,0:T(8,128)S(1)} %copy-done.8), custom_call_target="tpu_custom_call" | custom-call | tf_op jit(solution)/shard_map/pallas_call | solution.py:770
  32.1 9.1 %all_to_all.31 = f32[32,4,128]{2,1,0:T(4,128)S(1)} all-to-all(f32[32,4,128]{2,1,0:T(4,128)S(1)} %bitcast.28), channel_id=1, replica_groups=mesh['slab'=16,'grp'=2] {'slab','grp'}, dimensions={0} | all-to-all | bytes 131072 | tf_op jit(solution)/shard_map/all_to_all | solution.py:794
  41.2 1.2 %shard_map.117 = (f32[128,128]{1,0:T(8,128)}, f32[320,128]{1,0:T(8,128)S(1)}, f32[8,128]{1,0:T(8,128)S(1)}) custom-call(f32[128,128]{1,0:T(8,128)S(1)} %bitcast.27, bf16[640,320]{1,0:T(8,128)(2,1)S(1)} %get-tuple-element.30.gram_h_ref, bf16[640,320]{1,0:T(8,128)(2,1)S(1)} %get-tuple-element.31.gram_l_ref, ...), custom_call_target="tpu_custom_call", output_to_operand_aliasing={{1}: (3, {})} | custom-call | tf_op jit(solution)/shard_map/pallas_call | solution.py:770
  42.4 2.6 %all-to-all-start.3 = ((f32[32,4,128]{2,1,0:T(4,128)}), f32[32,4,128]{2,1,0:T(4,128)S(1)}, u32[]{:S(2)}, u32[]{:S(2)}) async-start(f32[32,4,128]{2,1,0:T(4,128)} %bitcast.13), calls=%async_computation.3 | async-start | bytes 131072 | tf_op jit(solution)/shard_map/all_to_all | solution.py:794
  45.0 0.0 copy-start.3
  45.0 1.0 %copy-done.3 = bf16[640,320]{1,0:T(8,128)(2,1)S(1)} copy-done((bf16[640,320]{1,0:T(8,128)(2,1)S(1)}, bf16[640,320]{1,0:T(8,128)(2,1)}, u32[]{:S(2)}) %copy-start.3) | copy-done | bytes 409624
  46.0 1.0 %copy-done.5 = bf16[640,320]{1,0:T(8,128)(2,1)S(1)} copy-done((bf16[640,320]{1,0:T(8,128)(2,1)S(1)}, bf16[640,320]{1,0:T(8,128)(2,1)}, u32[]{:S(2)}) %copy-start.5) | copy-done | bytes 409624
  47.0 2.1 %shard_map.118 = (f32[608,128]{1,0:T(8,128)S(1)}, f32[640,128]{1,0:T(8,128)S(1)}, f32[8,128]{1,0:T(8,128)S(1)}) custom-call(f32[320,128]{1,0:T(8,128)S(1)} %get-tuple-element.40.blend_ref, bf16[640,320]{1,0:T(8,128)(2,1)S(1)} %get-tuple-element.30.gram_h_ref, bf16[640,320]{1,0:T(8,128)(2,1)S(1)} %get-tuple-element.31.gram_l_ref, ...), custom_call_target="tpu_custom_call" | custom-call | tf_op jit(solution)/shard_map/pallas_call | solution.py:770
  49.1 3.2 %all-to-all-done.3 = f32[32,4,128]{2,1,0:T(4,128)S(1)} async-done(((f32[32,4,128]{2,1,0:T(4,128)}), f32[32,4,128]{2,1,0:T(4,128)S(1)}, u32[]{:S(2)}, u32[]{:S(2)}) %all-to-all-start.3) | async-done | bytes 65568 | tf_op jit(solution)/shard_map/all_to_all | solution.py:794
  52.4 0.9 %copy-done.7 = f32[96,384]{1,0:T(8,128)S(1)} copy-done((f32[96,384]{1,0:T(8,128)S(1)}, f32[96,384]{1,0:T(8,128)}, u32[]{:S(2)}) %copy-start.7) | copy-done | bytes 147480
  53.3 1.2 %shard_map.119 = f32[608,128]{1,0:T(8,128)S(1)} custom-call(f32[608,128]{1,0:T(8,128)S(1)} %get-tuple-element.46.early_ref, f32[128,128]{1,0:T(8,128)S(1)} %bitcast.25, f32[8,128]{1,0:T(8,128)S(1)} %get-tuple-element.48.sums_ref, f32[8,128]{1,0:T(8,128)S(1)} %get-tuple-element.45.scalar_ref, ...), custom_call_target="tpu_custom_call", output_to_operand_aliasing={{}: (0, {})} | custom-call | tf_op jit(solution)/shard_map/pallas_call | solution.py:770
  54.5 14.1 %all_to_all.32 = f32[32,1,2432]{2,1,0:T(1,128)S(1)} all-to-all(f32[32,1,2432]{2,1,0:T(1,128)S(1)} %bitcast.22), channel_id=1, replica_groups=mesh['slab'=16,'grp'=2] {'slab','grp'}, dimensions={0} | all-to-all | bytes 622592 | tf_op jit(solution)/shard_map/all_to_all | solution.py:794
  68.6 1.4 %shard_map.120 = (f32[320,128]{1,0:T(8,128)}, f32[8,128]{1,0:T(8,128)S(1)}) custom-call(f32[608,128]{1,0:T(8,128)S(1)} %bitcast.19, bf16[640,320]{1,0:T(8,128)(2,1)S(1)} %get-tuple-element.43.lift_h_ref, bf16[640,320]{1,0:T(8,128)(2,1)S(1)} %get-tuple-element.44.lift_l_ref, f32[640,128]{1,0:T(8,128)S(1)} %get-tuple-element.51.keep_ref, ...), custom_call_target="tpu_custom_call" | custom-call | tf_op jit(solution)/shard_map/pallas_call | solution.py:770
  70.0 2.6 %all-to-all-start.5 = ((f32[32,1,1280]{2,1,0:T(1,128)}), f32[32,1,1280]{2,1,0:T(1,128)S(1)}, u32[]{:S(2)}, u32[]{:S(2)}) async-start(f32[32,1,1280]{2,1,0:T(1,128)} %bitcast.17), calls=%async_computation.5 | async-start | bytes 327680 | tf_op jit(solution)/shard_map/all_to_all | solution.py:794
  72.6 0.2 collective-permute-start
  72.8 1.5 %collective-permute-done.partner_ref = f32[608,128]{1,0:T(8,128)S(1)} collective-permute-done((f32[608,128]{1,0:T(8,128)S(1)}, f32[608,128]{1,0:T(8,128)S(1)}, u32[]{:S(2)}, u32[]{:S(2)}) %collective-permute-start) | collective-permute-done | bytes 311328 | tf_op jit(solution)/shard_map/ppermute | solution.py:872
  74.3 2.0 %shard_map.121 = (f32[4,32,1024]{2,1,0:T(8,128)}, f32[128,1024]{1,0:T(8,128)S(1)}) custom-call(f32[608,128]{1,0:T(8,128)S(1)} %bitcast.21, f32[608,128]{1,0:T(8,128)S(1)} %collective-permute-done.partner_ref, f32[128,384]{1,0:T(8,128)S(1)} %get-tuple-element.50.side_ref, f32[8,128]{1,0:T(8,128)S(1)} %get-tuple-element.52.scalar_ref), custom_call_target="tpu_custom_call" | custom-call | tf_op jit(solution)/shard_map/pallas_call | solution.py:770
  76.3 4.9 %all-to-all-done.5 = f32[32,1,1280]{2,1,0:T(1,128)S(1)} async-done(((f32[32,1,1280]{2,1,0:T(1,128)}), f32[32,1,1280]{2,1,0:T(1,128)S(1)}, u32[]{:S(2)}, u32[]{:S(2)}) %all-to-all-start.5) | async-done | bytes 163872 | tf_op jit(solution)/shard_map/all_to_all | solution.py:794
  81.2 1.3 %shard_map.122 = f32[4,32,1024]{2,1,0:T(8,128)} custom-call(f32[320,128]{1,0:T(8,128)S(1)} %bitcast.23, f32[128,384]{1,0:T(8,128)S(1)} %get-tuple-element.50.side_ref, f32[128,1024]{1,0:T(8,128)S(1)} %get-tuple-element.55.part_ref), custom_call_target="tpu_custom_call" | custom-call | tf_op jit(solution)/shard_map/pallas_call | solution.py:770
  (15 shorter events, 0.0 us)
Async XLA Ops:
  3.5 14.9 %all-to-all-start = ((f32[32,1,640]{2,1,0:T(1,128)}), f32[32,1,640]{2,1,0:T(1,128)S(1)}, u32[]{:S(2)}, u32[]{:S(2)}) async-start(f32[32,1,640]{2,1,0:T(1,128)} %bitcast.34), calls=%async_computation | async-start | bytes 163840 | tf_op jit(solution)/shard_map/all_to_all | solution.py:794
  10.8 0.7 copy-start.10
  10.8 0.7 copy-start.9
  10.8 0.7 copy-start.11
  10.8 0.7 copy-start.12
  15.4 0.8 copy-start.2
  16.2 0.8 copy-start.4
  18.4 12.6 %copy-start = (f32[256,256]{1,0:T(8,128)S(1)}, f32[256,256]{1,0:T(8,128)}, u32[]{:S(2)}) copy-start(f32[256,256]{1,0:T(8,128)} %get-tuple-element.33.wide_ref) | copy-start | bytes 786436
  18.4 12.6 %copy-start.1 = (bf16[704,128]{1,0:T(8,128)(2,1)S(1)}, bf16[704,128]{1,0:T(8,128)(2,1)}, u32[]{:S(2)}) copy-start(bf16[704,128]{1,0:T(8,128)(2,1)} %get-tuple-element.34.inner_ref) | copy-start | bytes 540676
  19.3 11.7 %copy-start.8 = (f32[64,384]{1,0:T(8,128)S(1)}, f32[64,384]{1,0:T(8,128)}, u32[]{:S(2)}) copy-start(f32[64,384]{1,0:T(8,128)} %get-tuple-element.35.start_ref) | copy-start | bytes 294916
  32.1 10.3 %copy-start.6 = (f32[96,384]{1,0:T(8,128)}, f32[96,384]{1,0:T(8,128)S(1)}, u32[]{:S(2)}) copy-start(f32[96,384]{1,0:T(8,128)S(1)} %get-tuple-element.49.mixed_ref) | copy-start | bytes 442372
  42.4 10.0 %all-to-all-start.3 = ((f32[32,4,128]{2,1,0:T(4,128)}), f32[32,4,128]{2,1,0:T(4,128)S(1)}, u32[]{:S(2)}, u32[]{:S(2)}) async-start(f32[32,4,128]{2,1,0:T(4,128)} %bitcast.13), calls=%async_computation.3 | async-start | bytes 131072 | tf_op jit(solution)/shard_map/all_to_all | solution.py:794
  45.0 1.0 %copy-start.3 = (bf16[640,320]{1,0:T(8,128)(2,1)S(1)}, bf16[640,320]{1,0:T(8,128)(2,1)}, u32[]{:S(2)}) copy-start(bf16[640,320]{1,0:T(8,128)(2,1)} %copy-done.2) | copy-start | bytes 1228804
  46.0 1.0 %copy-start.5 = (bf16[640,320]{1,0:T(8,128)(2,1)S(1)}, bf16[640,320]{1,0:T(8,128)(2,1)}, u32[]{:S(2)}) copy-start(bf16[640,320]{1,0:T(8,128)(2,1)} %copy-done.4) | copy-start | bytes 1228804
  52.4 0.9 %copy-start.7 = (f32[96,384]{1,0:T(8,128)S(1)}, f32[96,384]{1,0:T(8,128)}, u32[]{:S(2)}) copy-start(f32[96,384]{1,0:T(8,128)} %copy-done.6) | copy-start | bytes 442372
  70.0 11.2 %all-to-all-start.5 = ((f32[32,1,1280]{2,1,0:T(1,128)}), f32[32,1,1280]{2,1,0:T(1,128)S(1)}, u32[]{:S(2)}, u32[]{:S(2)}) async-start(f32[32,1,1280]{2,1,0:T(1,128)} %bitcast.17), calls=%async_computation.5 | async-start | bytes 327680 | tf_op jit(solution)/shard_map/all_to_all | solution.py:794
  72.6 1.7 %collective-permute-start = (f32[608,128]{1,0:T(8,128)S(1)}, f32[608,128]{1,0:T(8,128)S(1)}, u32[]{:S(2)}, u32[]{:S(2)}) collective-permute-start(f32[608,128]{1,0:T(8,128)S(1)} %bitcast.20), channel_id=1, source_target_pairs={{0,1},{1,0},{2,3},{3,2},{4,5},{5,4},{6,7},{7,6},{8,9},{9,8},{10,11... | collective-permute-start | bytes 933896 | tf_op jit(solution)/shard_map/ppermute | solution.py:872

commit v5 on v4

--- a/solution.py
+++ b/solution.py
@@ -321,9 +321,24 @@
     return kron, second, (ref[640:672, 0:64], ref[672:704, 0:64])
 
 
+def row_tile(piece, j):
+    place = 3 * piece + j
+    first = 256 + 32 * (place // 2)
+    return slice(first, first + 32), slice(128 * (place % 2), 128 * (place % 2) + 128)
+
+
+def keep_rows(ref, piece, value):
+    for j in range(3):
+        ref[row_tile(piece, j)] = tile_of(value, j)
+
+
+def kept_rows(ref, piece):
+    return jnp.concatenate([ref[row_tile(piece, j)] for j in range(3)], axis=1)
+
+
 def start_kernel(
     table_hbm, weight_hbm, start2_hbm, band2_hbm, start3_hbm, band3_hbm,
-    send_ref, wide_ref, inner_ref, mixed_ref,
+    send_ref, wide_ref, inner_ref,
     table_ref, weight_ref, start2_ref, band2_ref, start3_ref, band3_ref, sems,
     product_ref, packed_ref, field_ref, rows_ref, stack_ref,
 ):
@@ -378,8 +393,8 @@
             target[16 * p : 16 * p + 16, 128:256] = high
     mixed = table_to_mixed(field_ref[...], kron, turned, rows_ref, stack_ref)
     once = inner_penalty(mixed)
-    mixed_ref[0:32, :] = mixed
-    mixed_ref[32:64, :] = once
+    keep_rows(wide_ref, 1, mixed)
+    keep_rows(wide_ref, 2, once)
     for base, value in ((0, mixed), (3, once)):
         put(send_ref, base, 5, tile_of(value, 0))
         put(send_ref, base + 1, 5, tile_of(value, 1))
@@ -414,17 +429,14 @@
     low_ref[rows, :] = low
 
 
-def matrix_kernel(
-    group_ref, start0_ref, band0_ref, start1_ref, band1_ref,
-    gram_h_ref, gram_l_ref, high_h_ref, high_l_ref, lift_h_ref, lift_l_ref, side_ref,
-    small_ref, rows0_h, rows0_l, rows1_h, rows1_l,
-):
+def gram_blocks(refs, count, small_ref, rows0_h, rows0_l, rows1_h, rows1_l):
+    start0_ref, band0_ref, start1_ref, band1_ref = refs
     total = DEVICES * ROWS
-    powers0 = powers(banded_t(start0_ref, band0_ref, K0, K0), 4)
-    powers1 = powers(banded_t(start1_ref, band1_ref, K1, K1), 4)
+    powers0 = powers(banded_t(start0_ref, band0_ref, K0, K0), count)
+    powers1 = powers(banded_t(start1_ref, band1_ref, K1, K1), max(count, 3))
     small_ref[...] = jnp.zeros((48, 128), f32)
     first, second = powers0[0].T, powers1[0].T
-    for k in range(4):
+    for k in range(count):
         small_ref[0:N0, 32 * k : 32 * k + N0] = mm(first, powers0[k])
         small_ref[N0 : N0 + N1, 32 * k : 32 * k + N1] = mm(second, powers1[k])
     row0 = iota((total, N0), 0)
@@ -442,30 +454,43 @@
     line, column = iota((128, total), 0), iota((128, total), 1)
     match0 = line % 32 == L0 * (column % 32 // GRPS) + column // 32 // L1
     match1 = line % 32 == L1 * (column % GRPS) + column // 32 % L1
-    select0 = [
-        jnp.where(match0 & (line // 32 == k), 1.0, 0.0).astype(jnp.bfloat16) for k in range(4)
+    select0, select1 = [
+        [
+            jnp.where(match & (line // 32 == k), 1.0, 0.0).astype(jnp.bfloat16)
+            for k in range(count)
+        ]
+        for match in (match0, match1)
     ]
-    select1 = [
-        jnp.where(match1 & (line // 32 == k), 1.0, 0.0).astype(jnp.bfloat16) for k in range(4)
-    ]
-
-    @pl.loop(0, 5)
-    def _(step):
-        base = pl.multiple_of(step * 64, 64)
+
+    def block(base):
         block0 = rows0_h[pl.ds(base, 64), :], rows0_l[pl.ds(base, 64), :]
         block1 = rows1_h[pl.ds(base, 64), :], rows1_l[pl.ds(base, 64), :]
         g = [choose(block0, selector) for selector in select0]
         h = [choose(block1, selector) for selector in select1]
-        first_power = g[1] * h[0] + g[0] * h[1]
-        squared = g[2] * h[0] + 2.0 * g[1] * h[1] + g[0] * h[2]
-        cubed = g[3] * h[0] + 3.0 * (g[2] * h[1] + g[1] * h[2]) + g[0] * h[3]
+        return g, h
+
+    return powers0, powers1, select0[0][0:N0, :], block
+
+
+def matrix_kernel(
+    group_ref, start0_ref, band0_ref, start1_ref, band1_ref,
+    gram_h_ref, gram_l_ref, lift_h_ref, lift_l_ref, side_ref, *scratch,
+):
+    total = DEVICES * ROWS
+    refs = (start0_ref, band0_ref, start1_ref, band1_ref)
+    powers0, powers1, chosen, block = gram_blocks(refs, 2, *scratch)
+
+    @pl.loop(0, 5)
+    def _(step):
+        base = pl.multiple_of(step * 64, 64)
+        g, h = block(base)
         store_split(gram_h_ref, gram_l_ref, pl.ds(base, 64), g[0] * h[0])
-        store_split(gram_h_ref, gram_l_ref, pl.ds(base + total, 64), first_power)
-        store_split(high_h_ref, high_l_ref, pl.ds(base, 64), squared)
-        store_split(high_h_ref, high_l_ref, pl.ds(base + total, 64), cubed)
+        store_split(
+            gram_h_ref, gram_l_ref, pl.ds(base + total, 64), g[1] * h[0] + g[0] * h[1]
+        )
 
     lifted = [
-        jnp.dot(term, select0[0][0:N0, :], preferred_element_type=f32)
+        jnp.dot(term, chosen, preferred_element_type=f32)
         for term in split(powers0[0])
     ]
     owner = L1 * (iota((K0, total), 1) % GRPS) + iota((K0, total), 1) // 32 % L1
@@ -540,17 +565,17 @@
 
 
 def first_row_kernel(
-    recv_ref, wide_ref, inner_ref, start_ref, send_ref, scalar_ref, mixed_ref, rows_ref, stack_ref,
+    recv_ref, wide_ref, inner_ref, send_ref, scalar_ref, carried_ref, rows_ref, stack_ref,
 ):
     norm, bend = totals(recv_ref, 3, 4, 2)
     scalar_ref[...] = lanes((norm, bend))
     kron, second, turned = constants(inner_ref)
     field = mixed_to_table(received_rows(recv_ref), kron, second, rows_ref, stack_ref)
-    weighted = wide_ref[...] * field
+    weighted = wide_ref[0:256, :] * field
     energy = jnp.sum(field * weighted)
     mixed = table_to_mixed(weighted, kron, turned, rows_ref, stack_ref)
-    mixed_ref[0:32, :] = mixed
-    mixed_ref[32:96, :] = start_ref[...]
+    carried_ref[...] = wide_ref[...]
+    keep_rows(carried_ref, 0, mixed)
     for j in range(3):
         put(send_ref, j, 4, tile_of(mixed, j))
     spread(send_ref, 3, 4, (energy,))
@@ -616,8 +641,9 @@
 
 
 def middle_kernel(
-    blend_ref, gram_h_ref, gram_l_ref, high_h_ref, high_l_ref, lift_h_ref, lift_l_ref, scalar_ref,
-    send_ref, keep_ref, sums_ref,
+    blend_ref, gram_h_ref, gram_l_ref, lift_h_ref, lift_l_ref, scalar_ref,
+    start0_ref, band0_ref, start1_ref, band1_ref,
+    send_ref, keep_ref, sums_ref, higher_ref, *scratch,
 ):
     total = DEVICES * ROWS
     step = pick(scalar_ref, 1)
@@ -626,8 +652,18 @@
     lane = iota(blend.shape, 1)
     pair = split(blend)
     lower = product(load((gram_h_ref, gram_l_ref)), pair)
-    higher = product(load((high_h_ref, high_l_ref)), pair)
-    g0, g1, g2, g3 = lower[:total], lower[total:], higher[:total], higher[total:]
+    *_, block = gram_blocks((start0_ref, band0_ref, start1_ref, band1_ref), 4, *scratch)
+
+    @pl.loop(0, 5)
+    def _(index):
+        base = pl.multiple_of(index * 64, 64)
+        g, h = block(base)
+        squared = g[2] * h[0] + 2.0 * g[1] * h[1] + g[0] * h[2]
+        cubed = g[3] * h[0] + 3.0 * (g[2] * h[1] + g[1] * h[2]) + g[0] * h[3]
+        higher_ref[pl.ds(base, 64), :] = product(split(squared), pair)
+        higher_ref[pl.ds(base + total, 64), :] = product(split(cubed), pair)
+
+    g0, g1, g2, g3 = lower[:total], lower[total:], higher_ref[0:total, :], higher_ref[total:, :]
     head = g0 - small * pltpu.roll(g1, 64, 1)
     tail = g1 - small * pltpu.roll(g2, 64, 1)
     end = g2 - small * pltpu.roll(g3, 64, 1)
@@ -655,16 +691,19 @@
 
 
 def second_row_kernel(
-    early_ref, recv_ref, sums_ref, scalar_ref, mixed_ref, wide_ref, inner_ref,
+    early_ref, recv_ref, sums_ref, scalar_ref, wide_ref, inner_ref,
     send_ref, rows_ref, stack_ref,
 ):
     kron, second, turned = constants(inner_ref)
+    send_ref[...] = early_ref[...]
     image = received_rows(recv_ref)
     step = pick(scalar_ref, 1)
-    reduced = mixed_ref[32:64, :] - step * (mixed_ref[0:32, :] + 0.1 * mixed_ref[64:96, :])
+    reduced = kept_rows(wide_ref, 1) - step * (
+        kept_rows(wide_ref, 0) + 0.1 * kept_rows(wide_ref, 2)
+    )
     inner = jnp.sum(reduced * inner_penalty(image))
     field = mixed_to_table(image, kron, second, rows_ref, stack_ref)
-    weighted = wide_ref[...] * field
+    weighted = wide_ref[0:256, :] * field
     energy = jnp.sum(field * weighted)
     mixed = table_to_mixed(weighted, kron, turned, rows_ref, stack_ref)
     for j in range(3):
@@ -818,9 +857,9 @@
         fourth_start,
         fourth_band.T,
     )
-    send, wide, inner, mixed0 = call(
+    send, wide, inner = call(
         start_kernel,
-        [(160, 128), (256, 256), jax.ShapeDtypeStruct((704, 128), jnp.bfloat16), (64, 384)],
+        [(160, 128), (416, 256), jax.ShapeDtypeStruct((704, 128), jnp.bfloat16)],
         [pltpu.VMEM(value.shape, value.dtype) for value in inputs]
         + [pltpu.SemaphoreType.DMA((len(inputs),))]
         + [(16, N2 * N3), (16, N2 * N3), (256, 256)]
@@ -830,21 +869,26 @@
         limit=LARGE,
     )
     recv = exchange(send)
+    grams = [(48, 128)] + [pltpu.VMEM((total, 128), jnp.bfloat16)] * 4
     group = lax.axis_index("grp").reshape(1)
     *matrices, side = call(
         matrix_kernel,
-        pair_of(2 * total, total) * 2 + pair_of(K0 * N1, total) + [(128, 384)],
-        [(48, 128)] + [pltpu.VMEM((total, 128), jnp.bfloat16)] * 4,
+        pair_of(2 * total, total) + pair_of(K0 * N1, total) + [(128, 384)],
+        grams,
         group, *outer,
         scalars=(0,),
     )
-    gram, high, lift = matrices[0:2], matrices[2:4], matrices[4:6]
+    gram, lift = matrices[0:2], matrices[2:4]
     send, fields, images = call(
         first_column_kernel, [(128, 128), (total, 128), (total, 128)], [], recv, *gram
     )
     recv = exchange(send)
-    send, scalars, mixed1 = call(
-        first_row_kernel, [(128, 128), (8, 128), (96, 384)], work, recv, wide, inner, mixed0
+    send, scalars, wide = call(
+        first_row_kernel,
+        [(128, 128), (8, 128), (416, 256)],
+        work,
+        recv, wide, inner,
+        aliases={1: 2},
     )
     recv = exchange(send)
     send, blend, scalars = call(
@@ -858,14 +902,14 @@
     send, keep, sums = call(
         middle_kernel,
         [(DEVICES * JOINT, 128), (K0 * N1, 128), (8, 128)],
-        [],
-        blend, *gram, *high, *lift, scalars,
+        [(2 * total, 128)] + grams,
+        blend, *gram, *lift, scalars, *outer,
     )
     (send,) = call(
         second_row_kernel,
         [(DEVICES * JOINT, 128)],
         work,
-        send, recv, sums, scalars, mixed1, wide, inner,
+        send, recv, sums, scalars, wide, inner,
         aliases={0: 0},
     )
     recv = exchange(send)

time: 83 us -> 81.8 us (0.986)
  local copies, waits for them, and re-layouts: 5.2 us -> 1.41 us
  Pallas kernels: 18 us -> 20.6 us
    unnamed x26 -> x16, local copies, waits for them, and re-layouts: 5.2 us -> 1.41 us
    pallas_call x10, Pallas kernels: 18 us -> 20.6 us  [call(): pl.pallas_call(kernel, out_shape=[shape if isinstance(shape, jax.ShapeDty...]
  transfers between devices with their start and end apart: 4 -> 4, of which waited for: 4 -> 4; matrix products, arithmetic and copies ran while one was open for 0% -> 0% of each run, Pallas kernels for 10% -> 13%
where the time goes in v5:
time: 81.8 us; the launch traced here: 81.4 us
  blocking collectives  34.7 us (42%)
  Pallas kernels  20.6 us (25%)
  starting transfers between devices  12.6 us (15%)
  waiting for transfers between devices  11.3 us (14%)
  local copies, waits for them, and re-layouts  1.41 us (2%)
    all_to_all x3, blocking collectives, exchange(): lax.all_to_all(buffer.reshape(shape), ('slab', 'grp'), 0, 0, tiled=True)  34.7 us
    pallas_call x10, Pallas kernels, call(): pl.pallas_call(kernel, out_shape=[shape if isinstance(shape, jax.ShapeDty...  20.6 us
    all_to_all x3, starting transfers between devices, exchange(): lax.all_to_all(buffer.reshape(shape), ('slab', 'grp'), 0, 0, tiled=True)  12.5 us
    all_to_all x3, waiting for transfers between devices, exchange(): lax.all_to_all(buffer.reshape(shape), ('slab', 'grp'), 0, 0, tiled=True)  9.82 us
  transfers between devices with their start and end apart: 4, of which 4 were waited for; matrix products, arithmetic and copies ran while one was open for 0% of the time, Pallas kernels for 13%

profile of v5, /device:TPU:0, one launch (start us, length us, event | category | flops | bytes accessed | tf_op | source)
XLA Modules:
  0.0 81.4 jit_solution(17767689637770411712)
XLA Ops:
  0.6 2.8 %shard_map.113 = (f32[160,128]{1,0:T(8,128)}, f32[416,256]{1,0:T(8,128)}, bf16[704,128]{1,0:T(8,128)(2,1)}) custom-call(f32[5,2,3200]{2,1,0:T(2,128)} %bitcast.34, f32[5,2,3200]{2,1,0:T(2,128)} %bitcast.35, s32[64]{0:T(128)} %start2_hbm.1, f32[4,64]{1,0:T(4,128)} %bitcast.37, s32[50]{0:T(128)} %start3_hbm.1, f32[4,50]{1,0:T(4,128)} %bitcast.38), custom_call_target="tpu_custom_call" | custom-call | tf_op jit(solution)/shard_map/pallas_call | solution.py:809
  3.4 7.3 %all-to-all-start = ((f32[32,1,640]{2,1,0:T(1,128)}), f32[32,1,640]{2,1,0:T(1,128)S(1)}, u32[]{:S(2)}, u32[]{:S(2)}) async-start(f32[32,1,640]{2,1,0:T(1,128)} %bitcast.36), calls=%async_computation | async-start | bytes 163840 | tf_op jit(solution)/shard_map/all_to_all | solution.py:833
  10.7 0.0 copy-start.5
  10.8 0.0 copy-start.4
  10.8 0.0 copy-start.6
  10.8 0.0 copy-start.7
  10.8 0.6 copy-done.5
  11.4 0.0 copy-done.4
  11.4 0.0 copy-done.6
  11.4 0.0 copy-done.7
  11.4 2.9 %shard_map.114 = (bf16[640,320]{1,0:T(8,128)(2,1)S(1)}, bf16[640,320]{1,0:T(8,128)(2,1)S(1)}, bf16[640,320]{1,0:T(8,128)(2,1)S(1)}, bf16[640,320]{1,0:T(8,128)(2,1)S(1)}, f32[128,384]{1,0:T(8,128)S(1)}) custom-call(s32[1]{0:T(128)} %bitcast.6.group_ref, s32[32]{0:T(128)S(1)} %copy-done.6, f32[4,32]{1,0:T(4,128)S(1)} %bitcast.30, s32[10]{0:T(128)S(1)} %copy-done.7, ...), custom_call_target="tpu_custom_call" | custom-call | tf_op jit(solution)/shard_map/pallas_call | solution.py:809
  14.3 4.0 %all-to-all-done = f32[32,1,640]{2,1,0:T(1,128)S(1)} async-done(((f32[32,1,640]{2,1,0:T(1,128)}), f32[32,1,640]{2,1,0:T(1,128)S(1)}, u32[]{:S(2)}, u32[]{:S(2)}) %all-to-all-start) | async-done | bytes 81952 | tf_op jit(solution)/shard_map/all_to_all | solution.py:833
  18.3 0.9 %shard_map.115 = (f32[128,128]{1,0:T(8,128)S(1)}, f32[320,128]{1,0:T(8,128)S(1)}, f32[320,128]{1,0:T(8,128)S(1)}) custom-call(f32[160,128]{1,0:T(8,128)S(1)} %bitcast.24, bf16[640,320]{1,0:T(8,128)(2,1)S(1)} %get-tuple-element.27.gram_h_ref, bf16[640,320]{1,0:T(8,128)(2,1)S(1)} %get-tuple-element.28.gram_l_ref), custom_call_target="tpu_custom_call" | custom-call | tf_op jit(solution)/shard_map/pallas_call | solution.py:809
  19.3 9.1 %all_to_all.30 = f32[32,4,128]{2,1,0:T(4,128)S(1)} all-to-all(f32[32,4,128]{2,1,0:T(4,128)S(1)} %bitcast.29), channel_id=1, replica_groups=mesh['slab'=16,'grp'=2] {'slab','grp'}, dimensions={0} | all-to-all | bytes 131072 | tf_op jit(solution)/shard_map/all_to_all | solution.py:833
  28.4 1.2 %shard_map.116 = (f32[128,128]{1,0:T(8,128)S(1)}, f32[8,128]{1,0:T(8,128)S(1)}, f32[416,256]{1,0:T(8,128)S(1)}) custom-call(f32[128,128]{1,0:T(8,128)S(1)} %bitcast.26, f32[416,256]{1,0:T(8,128)S(1)} %copy-done, bf16[704,128]{1,0:T(8,128)(2,1)S(1)} %copy-done.1), custom_call_target="tpu_custom_call", output_to_operand_aliasing={{2}: (1, {})} | custom-call | tf_op jit(solution)/shard_map/pallas_call | solution.py:809
  29.5 9.1 %all_to_all.31 = f32[32,4,128]{2,1,0:T(4,128)S(1)} all-to-all(f32[32,4,128]{2,1,0:T(4,128)S(1)} %bitcast.28), channel_id=1, replica_groups=mesh['slab'=16,'grp'=2] {'slab','grp'}, dimensions={0} | all-to-all | bytes 131072 | tf_op jit(solution)/shard_map/all_to_all | solution.py:833
  38.6 1.2 %shard_map.117 = (f32[128,128]{1,0:T(8,128)}, f32[320,128]{1,0:T(8,128)S(1)}, f32[8,128]{1,0:T(8,128)S(1)}) custom-call(f32[128,128]{1,0:T(8,128)S(1)} %bitcast.27, bf16[640,320]{1,0:T(8,128)(2,1)S(1)} %get-tuple-element.27.gram_h_ref, bf16[640,320]{1,0:T(8,128)(2,1)S(1)} %get-tuple-element.28.gram_l_ref, ...), custom_call_target="tpu_custom_call", output_to_operand_aliasing={{1}: (3, {})} | custom-call | tf_op jit(solution)/shard_map/pallas_call | solution.py:809
  39.8 2.6 %all-to-all-start.3 = ((f32[32,4,128]{2,1,0:T(4,128)}), f32[32,4,128]{2,1,0:T(4,128)S(1)}, u32[]{:S(2)}, u32[]{:S(2)}) async-start(f32[32,4,128]{2,1,0:T(4,128)} %bitcast.13), calls=%async_computation.3 | async-start | bytes 131072 | tf_op jit(solution)/shard_map/all_to_all | solution.py:833
  42.4 5.8 %shard_map.118 = (f32[608,128]{1,0:T(8,128)S(1)}, f32[640,128]{1,0:T(8,128)S(1)}, f32[8,128]{1,0:T(8,128)S(1)}) custom-call(f32[320,128]{1,0:T(8,128)S(1)} %get-tuple-element.36.blend_ref, bf16[640,320]{1,0:T(8,128)(2,1)S(1)} %get-tuple-element.27.gram_h_ref, bf16[640,320]{1,0:T(8,128)(2,1)S(1)} %get-tuple-element.28.gram_l_ref, ...), custom_call_target="tpu_custom_call" | custom-call | tf_op jit(solution)/shard_map/pallas_call | solution.py:809
  48.2 0.0 copy-start.2
  48.2 0.7 copy-done.2
  48.9 0.9 %all-to-all-done.3 = f32[32,4,128]{2,1,0:T(4,128)S(1)} async-done(((f32[32,4,128]{2,1,0:T(4,128)}), f32[32,4,128]{2,1,0:T(4,128)S(1)}, u32[]{:S(2)}, u32[]{:S(2)}) %all-to-all-start.3) | async-done | bytes 65568 | tf_op jit(solution)/shard_map/all_to_all | solution.py:833
  49.8 1.2 %shard_map.119 = f32[608,128]{1,0:T(8,128)S(1)} custom-call(f32[608,128]{1,0:T(8,128)S(1)} %get-tuple-element.40.early_ref, f32[128,128]{1,0:T(8,128)S(1)} %bitcast.25, f32[8,128]{1,0:T(8,128)S(1)} %get-tuple-element.42.sums_ref, f32[8,128]{1,0:T(8,128)S(1)} %get-tuple-element.39.scalar_ref, ...), custom_call_target="tpu_custom_call", output_to_operand_aliasing={{}: (0, {})} | custom-call | tf_op jit(solution)/shard_map/pallas_call | solution.py:809
  51.0 0.0 copy-start.3
  51.0 16.5 %all_to_all.32 = f32[32,1,2432]{2,1,0:T(1,128)S(1)} all-to-all(f32[32,1,2432]{2,1,0:T(1,128)S(1)} %bitcast.22), channel_id=1, replica_groups=mesh['slab'=16,'grp'=2] {'slab','grp'}, dimensions={0} | all-to-all | bytes 622592 | tf_op jit(solution)/shard_map/all_to_all | solution.py:833
  67.5 1.4 %shard_map.120 = (f32[320,128]{1,0:T(8,128)}, f32[8,128]{1,0:T(8,128)S(1)}) custom-call(f32[608,128]{1,0:T(8,128)S(1)} %bitcast.19, bf16[640,320]{1,0:T(8,128)(2,1)S(1)} %get-tuple-element.37.lift_h_ref, bf16[640,320]{1,0:T(8,128)(2,1)S(1)} %get-tuple-element.38.lift_l_ref, f32[640,128]{1,0:T(8,128)S(1)} %copy-done.3, f32[8,128]{1,0:T(8,128)S(1)} %get-tuple-element.39.scalar_ref), custom_call_target="tpu_custom_call" | custom-call | tf_op jit(solution)/shard_map/pallas_call | solution.py:809
  68.9 2.6 %all-to-all-start.5 = ((f32[32,1,1280]{2,1,0:T(1,128)}), f32[32,1,1280]{2,1,0:T(1,128)S(1)}, u32[]{:S(2)}, u32[]{:S(2)}) async-start(f32[32,1,1280]{2,1,0:T(1,128)} %bitcast.17), calls=%async_computation.5 | async-start | bytes 327680 | tf_op jit(solution)/shard_map/all_to_all | solution.py:833
  71.5 0.2 collective-permute-start
  71.7 1.5 %collective-permute-done.partner_ref = f32[608,128]{1,0:T(8,128)S(1)} collective-permute-done((f32[608,128]{1,0:T(8,128)S(1)}, f32[608,128]{1,0:T(8,128)S(1)}, u32[]{:S(2)}, u32[]{:S(2)}) %collective-permute-start) | collective-permute-done | bytes 311328 | tf_op jit(solution)/shard_map/ppermute | solution.py:916
  73.2 2.0 %shard_map.121 = (f32[4,32,1024]{2,1,0:T(8,128)}, f32[128,1024]{1,0:T(8,128)S(1)}) custom-call(f32[608,128]{1,0:T(8,128)S(1)} %bitcast.21, f32[608,128]{1,0:T(8,128)S(1)} %collective-permute-done.partner_ref, f32[128,384]{1,0:T(8,128)S(1)} %get-tuple-element.44.side_ref, f32[8,128]{1,0:T(8,128)S(1)} %get-tuple-element.46.scalar_ref), custom_call_target="tpu_custom_call" | custom-call | tf_op jit(solution)/shard_map/pallas_call | solution.py:809
  75.1 4.9 %all-to-all-done.5 = f32[32,1,1280]{2,1,0:T(1,128)S(1)} async-done(((f32[32,1,1280]{2,1,0:T(1,128)}), f32[32,1,1280]{2,1,0:T(1,128)S(1)}, u32[]{:S(2)}, u32[]{:S(2)}) %all-to-all-start.5) | async-done | bytes 163872 | tf_op jit(solution)/shard_map/all_to_all | solution.py:833
  80.1 1.3 %shard_map.122 = f32[4,32,1024]{2,1,0:T(8,128)} custom-call(f32[320,128]{1,0:T(8,128)S(1)} %bitcast.23, f32[128,384]{1,0:T(8,128)S(1)} %get-tuple-element.44.side_ref, f32[128,1024]{1,0:T(8,128)S(1)} %get-tuple-element.49.part_ref), custom_call_target="tpu_custom_call" | custom-call | tf_op jit(solution)/shard_map/pallas_call | solution.py:809
  (5 shorter events, 0.0 us)
Async XLA Ops:
  3.4 14.9 %all-to-all-start = ((f32[32,1,640]{2,1,0:T(1,128)}), f32[32,1,640]{2,1,0:T(1,128)S(1)}, u32[]{:S(2)}, u32[]{:S(2)}) async-start(f32[32,1,640]{2,1,0:T(1,128)} %bitcast.36), calls=%async_computation | async-start | bytes 163840 | tf_op jit(solution)/shard_map/all_to_all | solution.py:833
  10.7 0.7 copy-start.5
  10.8 0.7 copy-start.4
  10.8 0.7 copy-start.6
  10.8 0.7 copy-start.7
  18.3 10.0 %copy-start = (f32[416,256]{1,0:T(8,128)S(1)}, f32[416,256]{1,0:T(8,128)}, u32[]{:S(2)}) copy-start(f32[416,256]{1,0:T(8,128)} %get-tuple-element.30.wide_ref) | copy-start | bytes 1277956
  18.3 10.0 %copy-start.1 = (bf16[704,128]{1,0:T(8,128)(2,1)S(1)}, bf16[704,128]{1,0:T(8,128)(2,1)}, u32[]{:S(2)}) copy-start(bf16[704,128]{1,0:T(8,128)(2,1)} %get-tuple-element.31.inner_ref) | copy-start | bytes 540676
  39.8 10.0 %all-to-all-start.3 = ((f32[32,4,128]{2,1,0:T(4,128)}), f32[32,4,128]{2,1,0:T(4,128)S(1)}, u32[]{:S(2)}, u32[]{:S(2)}) async-start(f32[32,4,128]{2,1,0:T(4,128)} %bitcast.13), calls=%async_computation.3 | async-start | bytes 131072 | tf_op jit(solution)/shard_map/all_to_all | solution.py:833
  48.2 0.7 copy-start.2
  51.0 16.5 %copy-start.3 = (f32[640,128]{1,0:T(8,128)S(1)}, f32[640,128]{1,0:T(8,128)}, u32[]{:S(2)}) copy-start(f32[640,128]{1,0:T(8,128)} %copy-done.2) | copy-start | bytes 983044
  68.9 11.2 %all-to-all-start.5 = ((f32[32,1,1280]{2,1,0:T(1,128)}), f32[32,1,1280]{2,1,0:T(1,128)S(1)}, u32[]{:S(2)}, u32[]{:S(2)}) async-start(f32[32,1,1280]{2,1,0:T(1,128)} %bitcast.17), calls=%async_computation.5 | async-start | bytes 327680 | tf_op jit(solution)/shard_map/all_to_all | solution.py:833
  71.5 1.7 %collective-permute-start = (f32[608,128]{1,0:T(8,128)S(1)}, f32[608,128]{1,0:T(8,128)S(1)}, u32[]{:S(2)}, u32[]{:S(2)}) collective-permute-start(f32[608,128]{1,0:T(8,128)S(1)} %bitcast.20), channel_id=1, source_target_pairs={{0,1},{1,0},{2,3},{3,2},{4,5},{5,4},{6,7},{7,6},{8,9},{9,8},{10,11... | collective-permute-start | bytes 933896 | tf_op jit(solution)/shard_map/ppermute | solution.py:916

commit v6 on v5

--- a/solution.py
+++ b/solution.py
@@ -433,7 +433,7 @@
     start0_ref, band0_ref, start1_ref, band1_ref = refs
     total = DEVICES * ROWS
     powers0 = powers(banded_t(start0_ref, band0_ref, K0, K0), count)
-    powers1 = powers(banded_t(start1_ref, band1_ref, K1, K1), max(count, 3))
+    powers1 = powers(banded_t(start1_ref, band1_ref, K1, K1), 4)
     small_ref[...] = jnp.zeros((48, 128), f32)
     first, second = powers0[0].T, powers1[0].T
     for k in range(count):
@@ -504,7 +504,10 @@
     half = iota((N1, N1), 1) // L1
     wanted = L1 * jnp.where(half == group, 0, 1) + iota((N1, N1), 1) % L1
     reorder = jnp.where(iota((N1, N1), 0) == wanted, 1.0, 0.0)
-    side_ref[...] = jnp.zeros((128, 384), f32)
+    side_ref[...] = jnp.zeros((192, 384), f32)
+    across = powers1[0].T
+    for k in range(4):
+        side_ref[128 + 16 * k : 128 + 16 * k + N1, 0:N1] = mm(across, powers1[k])
     for k in range(3):
         own = mm(pick_coef, powers1[k])
         halves = mm(own, reorder)
@@ -641,51 +644,52 @@
 
 
 def middle_kernel(
-    blend_ref, gram_h_ref, gram_l_ref, lift_h_ref, lift_l_ref, scalar_ref,
-    start0_ref, band0_ref, start1_ref, band1_ref,
-    send_ref, keep_ref, sums_ref, higher_ref, *scratch,
+    blend_ref, lift_h_ref, lift_l_ref, scalar_ref, side_ref, send_ref, keep_ref, sums_ref, four_ref
 ):
-    total = DEVICES * ROWS
     step = pick(scalar_ref, 1)
     small = 0.1 * step
-    blend = blend_ref[...]
-    lane = iota(blend.shape, 1)
-    pair = split(blend)
-    lower = product(load((gram_h_ref, gram_l_ref)), pair)
-    *_, block = gram_blocks((start0_ref, band0_ref, start1_ref, band1_ref), 4, *scratch)
-
-    @pl.loop(0, 5)
-    def _(index):
-        base = pl.multiple_of(index * 64, 64)
-        g, h = block(base)
-        squared = g[2] * h[0] + 2.0 * g[1] * h[1] + g[0] * h[2]
-        cubed = g[3] * h[0] + 3.0 * (g[2] * h[1] + g[1] * h[2]) + g[0] * h[3]
-        higher_ref[pl.ds(base, 64), :] = product(split(squared), pair)
-        higher_ref[pl.ds(base + total, 64), :] = product(split(cubed), pair)
-
-    g0, g1, g2, g3 = lower[:total], lower[total:], higher_ref[0:total, :], higher_ref[total:, :]
-    head = g0 - small * pltpu.roll(g1, 64, 1)
-    tail = g1 - small * pltpu.roll(g2, 64, 1)
-    end = g2 - small * pltpu.roll(g3, 64, 1)
-    scaled = pltpu.roll(blend, 64, 1)
-    low = lane < 32
-    norm = jnp.sum(jnp.where(low, blend * head - small * scaled * tail, 0.0))
-    head_p = tail + pltpu.roll(head, 96, 1)
-    tail_p = end + pltpu.roll(tail, 96, 1)
-    bend = jnp.sum(jnp.where(low, blend * head_p - small * scaled * tail_p, 0.0))
-    sums_ref[...] = lanes((norm, bend))
-    lifted = product(load((lift_h_ref, lift_l_ref)), pair)
+    lifted = product(load((lift_h_ref, lift_l_ref)), split(blend_ref[...]))
     once = coefficient_penalty(lifted)
     twice = coefficient_penalty(once)
     h_a = lifted - small * pltpu.roll(once, 64, 1)
     y_1 = once + pltpu.roll(lifted, 96, 1)
     x_a = once - small * pltpu.roll(twice, 64, 1)
     h_0 = pltpu.roll(lifted, 64, 1)
-    wide = iota(lifted.shape, 1)
-    keep = jnp.where(
-        wide < 32, h_0, jnp.where(wide < 64, pltpu.roll(h_a, 32, 1), jnp.where(wide < 96, y_1, pltpu.roll(x_a, 96, 1)))
-    )
-    keep_ref[...] = keep
+    lane = iota(lifted.shape, 1)
+
+    def blocks(first, second, third, fourth):
+        return jnp.where(
+            lane < 32, first, jnp.where(lane < 64, second, jnp.where(lane < 96, third, fourth))
+        )
+
+    keep_ref[...] = blocks(h_0, pltpu.roll(h_a, 32, 1), y_1, pltpu.roll(x_a, 96, 1))
+    flat = x_a - small * pltpu.roll(once, 32, 1)
+    slope = h_a - small * pltpu.roll(y_1, 64, 1)
+    four_ref[...] = blocks(
+        h_a, -small * pltpu.roll(h_0, 32, 1), pltpu.roll(flat, 64, 1), pltpu.roll(slope, 96, 1)
+    )
+    grams = split(side_ref[128:192, 0:N1])
+    corner = iota((16, 128), 1) // 32
+    norm, bend = jnp.zeros((16, 128), f32), jnp.zeros((16, 128), f32)
+    filler = jnp.zeros((16 - N1, 128), f32)
+    for chunk in range(8):
+        tiles = [four_ref[pl.ds(8 * chunk + k, N1, stride=K0), :] for k in range(8)]
+        applied = product(grams, split(jnp.concatenate(tiles, axis=1)))
+        for k, tile in enumerate(tiles):
+            x = jnp.concatenate([tile, filler], axis=0)
+            r1, r2, r3 = [pltpu.roll(x, 32 * d, 1) for d in (1, 2, 3)]
+            y0, y1, y2, y3 = [applied[16 * d : 16 * d + 16, 128 * k : 128 * k + 128] for d in range(4)]
+            norm = norm + jnp.where(
+                corner == 0, x * y0, jnp.where(corner == 1, 2.0 * r1 * y1 + x * y2, 0.0)
+            )
+            bend = bend + jnp.where(
+                corner == 1,
+                r1 * y2 + x * y3,
+                jnp.where(
+                    corner == 2, r2 * y0 + r1 * y1, jnp.where(corner == 3, r3 * y1 + r2 * y2, 0.0)
+                ),
+            )
+    sums_ref[...] = lanes((jnp.sum(norm), jnp.sum(bend)))
     for block in range(3):
         send_halves(send_ref, JOINT, 4 + 5 * block, keep_ref, block)
 
@@ -768,8 +772,8 @@
             gather_blocks(ref, JOINT, 4 + 5 * block, 5, early, 40 * block + 20 * h)
     step, ratio, step_next = pick(scalar_ref, 1), pick(scalar_ref, 2), pick(scalar_ref, 3)
     small = 0.1 * step
-    value = split(side_ref[:, 128:208])
-    slope = split(side_ref[:, 256:376])
+    value = split(side_ref[0:128, 128:208])
+    slope = split(side_ref[0:128, 256:376])
     bent = bent_rows(jnp.concatenate([take(early, 1, tile) for tile in range(8)], axis=1))
     for tile in range(8):
         h_0, h_a, y_1 = take(early, 0, tile), take(early, 1, tile), take(early, 2, tile)
@@ -792,7 +796,7 @@
 
 def final_kernel(late_ref, side_ref, part_ref, residual_ref, late):
     gather_blocks(late_ref, 10, 0, 10, late, 0)
-    value = split(side_ref[:, 0:40])
+    value = split(side_ref[0:128, 0:40])
     for tile in range(8):
         columns = slice(128 * tile, 128 * tile + 128)
         whole = part_ref[:, columns] + product(value, split(take(late, 0, tile)))
@@ -873,7 +877,7 @@
     group = lax.axis_index("grp").reshape(1)
     *matrices, side = call(
         matrix_kernel,
-        pair_of(2 * total, total) + pair_of(K0 * N1, total) + [(128, 384)],
+        pair_of(2 * total, total) + pair_of(K0 * N1, total) + [(192, 384)],
         grams,
         group, *outer,
         scalars=(0,),
@@ -902,8 +906,8 @@
     send, keep, sums = call(
         middle_kernel,
         [(DEVICES * JOINT, 128), (K0 * N1, 128), (8, 128)],
-        [(2 * total, 128)] + grams,
-        blend, *gram, *lift, scalars, *outer,
+        [(K0 * N1, 128)],
+        blend, *lift, scalars, side,
     )
     (send,) = call(
         second_row_kernel,

time: 81.8 us -> 79 us (0.966)
  waiting for transfers between devices: 11.3 us -> 15 us
  Pallas kernels: 20.6 us -> 17.7 us
  blocking collectives: 34.7 us -> 31.9 us
    all_to_all x3, waiting for transfers between devices: 9.82 us -> 13.5 us  [exchange(): lax.all_to_all(buffer.reshape(shape), ('slab', 'grp'), 0, 0, tiled=True)]
    pallas_call x10, Pallas kernels: 20.6 us -> 17.7 us  [call(): pl.pallas_call(kernel, out_shape=[shape if isinstance(shape, jax.ShapeDty...]
    all_to_all x3, blocking collectives: 34.7 us -> 31.9 us  [exchange(): lax.all_to_all(buffer.reshape(shape), ('slab', 'grp'), 0, 0, tiled=True)]
  transfers between devices with their start and end apart: 4 -> 4, of which waited for: 4 -> 4; matrix products, arithmetic and copies ran while one was open for 0% -> 0% of each run, Pallas kernels for 13% -> 10%
where the time goes in v6:
time: 79 us; the launch traced here: 78.7 us
  blocking collectives  31.9 us (40%)
  Pallas kernels  17.7 us (22%)
  waiting for transfers between devices  15 us (19%)
  starting transfers between devices  12.6 us (16%)
    all_to_all x3, blocking collectives, exchange(): lax.all_to_all(buffer.reshape(shape), ('slab', 'grp'), 0, 0, tiled=True)  31.9 us
    pallas_call x10, Pallas kernels, call(): pl.pallas_call(kernel, out_shape=[shape if isinstance(shape, jax.ShapeDty...  17.7 us
    all_to_all x3, waiting for transfers between devices, exchange(): lax.all_to_all(buffer.reshape(shape), ('slab', 'grp'), 0, 0, tiled=True)  13.5 us
    all_to_all x3, starting transfers between devices, exchange(): lax.all_to_all(buffer.reshape(shape), ('slab', 'grp'), 0, 0, tiled=True)  12.5 us
  transfers between devices with their start and end apart: 4, of which 4 were waited for; matrix products, arithmetic and copies ran while one was open for 0% of the time, Pallas kernels for 10%

profile of v6, /device:TPU:0, one launch (start us, length us, event | category | flops | bytes accessed | tf_op | source)
XLA Modules:
  0.0 78.7 jit_solution(7270289071756953572)
XLA Ops:
  0.6 2.8 %shard_map.113 = (f32[160,128]{1,0:T(8,128)}, f32[416,256]{1,0:T(8,128)}, bf16[704,128]{1,0:T(8,128)(2,1)}) custom-call(f32[5,2,3200]{2,1,0:T(2,128)} %bitcast.32, f32[5,2,3200]{2,1,0:T(2,128)} %bitcast.33, s32[64]{0:T(128)} %start2_hbm.1, f32[4,64]{1,0:T(4,128)} %bitcast.35, s32[50]{0:T(128)} %start3_hbm.1, f32[4,50]{1,0:T(4,128)} %bitcast.36), custom_call_target="tpu_custom_call" | custom-call | tf_op jit(solution)/shard_map/pallas_call | solution.py:813
  3.4 7.3 %all-to-all-start = ((f32[32,1,640]{2,1,0:T(1,128)}), f32[32,1,640]{2,1,0:T(1,128)S(1)}, u32[]{:S(2)}, u32[]{:S(2)}) async-start(f32[32,1,640]{2,1,0:T(1,128)} %bitcast.34), calls=%async_computation | async-start | bytes 163840 | tf_op jit(solution)/shard_map/all_to_all | solution.py:837
  10.7 0.0 copy-start.3
  10.8 0.0 copy-start.2
  10.8 0.0 copy-start.4
  10.8 0.0 copy-start.5
  10.8 0.6 copy-done.3
  11.4 0.0 copy-done.2
  11.4 0.0 copy-done.4
  11.4 0.0 copy-done.5
  11.5 3.2 %shard_map.114 = (bf16[640,320]{1,0:T(8,128)(2,1)S(1)}, bf16[640,320]{1,0:T(8,128)(2,1)S(1)}, bf16[640,320]{1,0:T(8,128)(2,1)S(1)}, bf16[640,320]{1,0:T(8,128)(2,1)S(1)}, f32[192,384]{1,0:T(8,128)S(1)}) custom-call(s32[1]{0:T(128)} %bitcast.6.group_ref, s32[32]{0:T(128)S(1)} %copy-done.4, f32[4,32]{1,0:T(4,128)S(1)} %bitcast.30, s32[10]{0:T(128)S(1)} %copy-done.5, ...), custom_call_target="tpu_custom_call" | custom-call | tf_op jit(solution)/shard_map/pallas_call | solution.py:813
  14.7 3.7 %all-to-all-done = f32[32,1,640]{2,1,0:T(1,128)S(1)} async-done(((f32[32,1,640]{2,1,0:T(1,128)}), f32[32,1,640]{2,1,0:T(1,128)S(1)}, u32[]{:S(2)}, u32[]{:S(2)}) %all-to-all-start) | async-done | bytes 81952 | tf_op jit(solution)/shard_map/all_to_all | solution.py:837
  18.3 0.0 copy-start
  18.3 0.9 %shard_map.115 = (f32[128,128]{1,0:T(8,128)S(1)}, f32[320,128]{1,0:T(8,128)S(1)}, f32[320,128]{1,0:T(8,128)S(1)}) custom-call(f32[160,128]{1,0:T(8,128)S(1)} %bitcast.24, bf16[640,320]{1,0:T(8,128)(2,1)S(1)} %get-tuple-element.27.gram_h_ref, bf16[640,320]{1,0:T(8,128)(2,1)S(1)} %get-tuple-element.28.gram_l_ref), custom_call_target="tpu_custom_call" | custom-call | tf_op jit(solution)/shard_map/pallas_call | solution.py:813
  19.3 9.4 %all_to_all.30 = f32[32,4,128]{2,1,0:T(4,128)S(1)} all-to-all(f32[32,4,128]{2,1,0:T(4,128)S(1)} %bitcast.29), channel_id=1, replica_groups=mesh['slab'=16,'grp'=2] {'slab','grp'}, dimensions={0} | all-to-all | bytes 131072 | tf_op jit(solution)/shard_map/all_to_all | solution.py:837
  28.7 0.0 copy-done
  28.7 0.0 copy-done.1
  28.7 1.2 %shard_map.116 = (f32[128,128]{1,0:T(8,128)S(1)}, f32[8,128]{1,0:T(8,128)S(1)}, f32[416,256]{1,0:T(8,128)S(1)}) custom-call(f32[128,128]{1,0:T(8,128)S(1)} %bitcast.26, f32[416,256]{1,0:T(8,128)S(1)} %copy-done, bf16[704,128]{1,0:T(8,128)(2,1)S(1)} %copy-done.1), custom_call_target="tpu_custom_call", output_to_operand_aliasing={{2}: (1, {})} | custom-call | tf_op jit(solution)/shard_map/pallas_call | solution.py:813
  29.9 9.1 %all_to_all.31 = f32[32,4,128]{2,1,0:T(4,128)S(1)} all-to-all(f32[32,4,128]{2,1,0:T(4,128)S(1)} %bitcast.28), channel_id=1, replica_groups=mesh['slab'=16,'grp'=2] {'slab','grp'}, dimensions={0} | all-to-all | bytes 131072 | tf_op jit(solution)/shard_map/all_to_all | solution.py:837
  39.0 1.2 %shard_map.117 = (f32[128,128]{1,0:T(8,128)}, f32[320,128]{1,0:T(8,128)S(1)}, f32[8,128]{1,0:T(8,128)S(1)}) custom-call(f32[128,128]{1,0:T(8,128)S(1)} %bitcast.27, bf16[640,320]{1,0:T(8,128)(2,1)S(1)} %get-tuple-element.27.gram_h_ref, bf16[640,320]{1,0:T(8,128)(2,1)S(1)} %get-tuple-element.28.gram_l_ref, ...), custom_call_target="tpu_custom_call", output_to_operand_aliasing={{1}: (3, {})} | custom-call | tf_op jit(solution)/shard_map/pallas_call | solution.py:813
  40.1 2.6 %all-to-all-start.3 = ((f32[32,4,128]{2,1,0:T(4,128)}), f32[32,4,128]{2,1,0:T(4,128)S(1)}, u32[]{:S(2)}, u32[]{:S(2)}) async-start(f32[32,4,128]{2,1,0:T(4,128)} %bitcast.13), calls=%async_computation.3 | async-start | bytes 131072 | tf_op jit(solution)/shard_map/all_to_all | solution.py:837
  42.7 2.4 %shard_map.118 = (f32[608,128]{1,0:T(8,128)S(1)}, f32[640,128]{1,0:T(8,128)S(1)}, f32[8,128]{1,0:T(8,128)S(1)}) custom-call(f32[320,128]{1,0:T(8,128)S(1)} %get-tuple-element.36.blend_ref, bf16[640,320]{1,0:T(8,128)(2,1)S(1)} %get-tuple-element.37.lift_h_ref, bf16[640,320]{1,0:T(8,128)(2,1)S(1)} %get-tuple-element.38.lift_l_ref, ...), custom_call_target="tpu_custom_call" | custom-call | tf_op jit(solution)/shard_map/pallas_call | solution.py:813
  45.2 5.0 %all-to-all-done.3 = f32[32,4,128]{2,1,0:T(4,128)S(1)} async-done(((f32[32,4,128]{2,1,0:T(4,128)}), f32[32,4,128]{2,1,0:T(4,128)S(1)}, u32[]{:S(2)}, u32[]{:S(2)}) %all-to-all-start.3) | async-done | bytes 65568 | tf_op jit(solution)/shard_map/all_to_all | solution.py:837
  50.1 1.2 %shard_map.119 = f32[608,128]{1,0:T(8,128)S(1)} custom-call(f32[608,128]{1,0:T(8,128)S(1)} %get-tuple-element.41.early_ref, f32[128,128]{1,0:T(8,128)S(1)} %bitcast.25, f32[8,128]{1,0:T(8,128)S(1)} %get-tuple-element.43.sums_ref, f32[8,128]{1,0:T(8,128)S(1)} %get-tuple-element.39.scalar_ref, ...), custom_call_target="tpu_custom_call", output_to_operand_aliasing={{}: (0, {})} | custom-call | tf_op jit(solution)/shard_map/pallas_call | solution.py:813
  51.3 13.4 %all_to_all.32 = f32[32,1,2432]{2,1,0:T(1,128)S(1)} all-to-all(f32[32,1,2432]{2,1,0:T(1,128)S(1)} %bitcast.22), channel_id=1, replica_groups=mesh['slab'=16,'grp'=2] {'slab','grp'}, dimensions={0} | all-to-all | bytes 622592 | tf_op jit(solution)/shard_map/all_to_all | solution.py:837
  64.7 1.4 %shard_map.120 = (f32[320,128]{1,0:T(8,128)}, f32[8,128]{1,0:T(8,128)S(1)}) custom-call(f32[608,128]{1,0:T(8,128)S(1)} %bitcast.19, bf16[640,320]{1,0:T(8,128)(2,1)S(1)} %get-tuple-element.37.lift_h_ref, bf16[640,320]{1,0:T(8,128)(2,1)S(1)} %get-tuple-element.38.lift_l_ref, f32[640,128]{1,0:T(8,128)S(1)} %get-tuple-element.45.keep_ref, ...), custom_call_target="tpu_custom_call" | custom-call | tf_op jit(solution)/shard_map/pallas_call | solution.py:813
  66.2 2.6 %all-to-all-start.5 = ((f32[32,1,1280]{2,1,0:T(1,128)}), f32[32,1,1280]{2,1,0:T(1,128)S(1)}, u32[]{:S(2)}, u32[]{:S(2)}) async-start(f32[32,1,1280]{2,1,0:T(1,128)} %bitcast.17), calls=%async_computation.5 | async-start | bytes 327680 | tf_op jit(solution)/shard_map/all_to_all | solution.py:837
  68.8 0.2 collective-permute-start
  68.9 1.5 %collective-permute-done.partner_ref = f32[608,128]{1,0:T(8,128)S(1)} collective-permute-done((f32[608,128]{1,0:T(8,128)S(1)}, f32[608,128]{1,0:T(8,128)S(1)}, u32[]{:S(2)}, u32[]{:S(2)}) %collective-permute-start) | collective-permute-done | bytes 311328 | tf_op jit(solution)/shard_map/ppermute | solution.py:920
  70.4 2.0 %shard_map.121 = (f32[4,32,1024]{2,1,0:T(8,128)}, f32[128,1024]{1,0:T(8,128)S(1)}) custom-call(f32[608,128]{1,0:T(8,128)S(1)} %bitcast.21, f32[608,128]{1,0:T(8,128)S(1)} %collective-permute-done.partner_ref, f32[192,384]{1,0:T(8,128)S(1)} %get-tuple-element.40.side_ref, f32[8,128]{1,0:T(8,128)S(1)} %get-tuple-element.46.scalar_ref), custom_call_target="tpu_custom_call" | custom-call | tf_op jit(solution)/shard_map/pallas_call | solution.py:813
  72.4 4.9 %all-to-all-done.5 = f32[32,1,1280]{2,1,0:T(1,128)S(1)} async-done(((f32[32,1,1280]{2,1,0:T(1,128)}), f32[32,1,1280]{2,1,0:T(1,128)S(1)}, u32[]{:S(2)}, u32[]{:S(2)}) %all-to-all-start.5) | async-done | bytes 163872 | tf_op jit(solution)/shard_map/all_to_all | solution.py:837
  77.3 1.3 %shard_map.122 = f32[4,32,1024]{2,1,0:T(8,128)} custom-call(f32[320,128]{1,0:T(8,128)S(1)} %bitcast.23, f32[192,384]{1,0:T(8,128)S(1)} %get-tuple-element.40.side_ref, f32[128,1024]{1,0:T(8,128)S(1)} %get-tuple-element.49.part_ref), custom_call_target="tpu_custom_call" | custom-call | tf_op jit(solution)/shard_map/pallas_call | solution.py:813
  (1 shorter events, 0.0 us)
Async XLA Ops:
  3.4 14.9 %all-to-all-start = ((f32[32,1,640]{2,1,0:T(1,128)}), f32[32,1,640]{2,1,0:T(1,128)S(1)}, u32[]{:S(2)}, u32[]{:S(2)}) async-start(f32[32,1,640]{2,1,0:T(1,128)} %bitcast.34), calls=%async_computation | async-start | bytes 163840 | tf_op jit(solution)/shard_map/all_to_all | solution.py:837
  10.7 0.7 copy-start.3
  10.8 0.7 copy-start.2
  10.8 0.7 copy-start.4
  10.8 0.7 copy-start.5
  18.3 10.4 %copy-start = (f32[416,256]{1,0:T(8,128)S(1)}, f32[416,256]{1,0:T(8,128)}, u32[]{:S(2)}) copy-start(f32[416,256]{1,0:T(8,128)} %get-tuple-element.30.wide_ref) | copy-start | bytes 1277956
  18.3 10.4 %copy-start.1 = (bf16[704,128]{1,0:T(8,128)(2,1)S(1)}, bf16[704,128]{1,0:T(8,128)(2,1)}, u32[]{:S(2)}) copy-start(bf16[704,128]{1,0:T(8,128)(2,1)} %get-tuple-element.31.inner_ref) | copy-start | bytes 540676
  40.1 10.0 %all-to-all-start.3 = ((f32[32,4,128]{2,1,0:T(4,128)}), f32[32,4,128]{2,1,0:T(4,128)S(1)}, u32[]{:S(2)}, u32[]{:S(2)}) async-start(f32[32,4,128]{2,1,0:T(4,128)} %bitcast.13), calls=%async_computation.3 | async-start | bytes 131072 | tf_op jit(solution)/shard_map/all_to_all | solution.py:837
  66.2 11.2 %all-to-all-start.5 = ((f32[32,1,1280]{2,1,0:T(1,128)}), f32[32,1,1280]{2,1,0:T(1,128)S(1)}, u32[]{:S(2)}, u32[]{:S(2)}) async-start(f32[32,1,1280]{2,1,0:T(1,128)} %bitcast.17), calls=%async_computation.5 | async-start | bytes 327680 | tf_op jit(solution)/shard_map/all_to_all | solution.py:837
  68.8 1.7 %collective-permute-start = (f32[608,128]{1,0:T(8,128)S(1)}, f32[608,128]{1,0:T(8,128)S(1)}, u32[]{:S(2)}, u32[]{:S(2)}) collective-permute-start(f32[608,128]{1,0:T(8,128)S(1)} %bitcast.20), channel_id=1, source_target_pairs={{0,1},{1,0},{2,3},{3,2},{4,5},{5,4},{6,7},{7,6},{8,9},{9,8},{10,11... | collective-permute-start | bytes 933896 | tf_op jit(solution)/shard_map/ppermute | solution.py:920

commit v7 on v6

--- a/solution.py
+++ b/solution.py
@@ -355,8 +355,8 @@
             )
         )
     ]
-    for copy in copies:
-        copy.start()
+    for k in (4, 5, 1, 0, 3, 2):
+        copies[k].start()
     copies[0].wait()
     copies[1].wait()
     pick_bin = (iota((256, N3), 0) % N3 == iota((256, N3), 1)) & (iota((256, N3), 0) < 4 * N3)
@@ -474,7 +474,7 @@
 
 def matrix_kernel(
     group_ref, start0_ref, band0_ref, start1_ref, band1_ref,
-    gram_h_ref, gram_l_ref, lift_h_ref, lift_l_ref, side_ref, *scratch,
+    gram_h_ref, gram_l_ref, lift_h_ref, lift_l_ref, side_ref, small_h_ref, small_l_ref, *scratch,
 ):
     total = DEVICES * ROWS
     refs = (start0_ref, band0_ref, start1_ref, band1_ref)
@@ -493,6 +493,10 @@
         jnp.dot(term, chosen, preferred_element_type=f32)
         for term in split(powers0[0])
     ]
+    spot = iota((N0, N0), 1)
+    order = jnp.where(L0 * (spot % 16) + spot // 16 == iota((N0, N0), 0), 1.0, 0.0).astype(jnp.bfloat16)
+    for term, target in zip(split(powers0[0]), (small_h_ref, small_l_ref)):
+        target[...] = jnp.dot(term, order, preferred_element_type=f32).astype(jnp.bfloat16)
     owner = L1 * (iota((K0, total), 1) % GRPS) + iota((K0, total), 1) // 32 % L1
     for n in range(N1):
         rows = slice(K0 * n, K0 * n + K0)
@@ -716,19 +720,32 @@
 
 
 def third_column_kernel(
-    recv_ref, lift_h_ref, lift_l_ref, keep_ref, scalar_ref, send_ref, out_scalar_ref, last_ref, mixed_ref
+    recv_ref, small_h_ref, small_l_ref, keep_ref, scalar_ref,
+    send_ref, out_scalar_ref, packed_ref, lifted_ref, mixed_ref,
 ):
-    zero = jnp.zeros((32, 128), f32)
-    for r in range(ROWS):
-        j, q = r // 4, r % 4
-        last_ref[32 * r : 32 * r + 32, :] = unpack(recv_ref, j, JOINT, r, q, 0)
+    for a in range(L0):
+        for t in range(3):
+            parts = []
+            for block in range(4):
+                n = 4 * t + block
+                if n < N1:
+                    g, b = divmod(n, L1)
+                    j, q = divmod(L1 * a + b, 4)
+                    part = recv_ref[pl.ds(g * JOINT + j, 16, stride=2 * JOINT), :]
+                    parts.append(move(part, q, block))
+                else:
+                    parts.append(jnp.zeros((16, 128), f32))
+            packed_ref[16 * a : 16 * a + 16, 128 * t : 128 * t + 128] = merge(parts)
+    packed = product(load((small_h_ref, small_l_ref)), split(packed_ref[...]))
+    for n in range(N1):
+        lifted_ref[K0 * n : K0 * n + K0, :] = move(tile_of(packed, n // 4), n % 4, 0)
     energy, norm_next, bend = totals(recv_ref, 3, JOINT, 3)
     norm, step = pick(scalar_ref, 0), pick(scalar_ref, 1)
     ratio = norm_next / norm
     curve = energy + 0.1 * bend - ratio * norm_next / step
     step_next = norm_next / curve
     out_scalar_ref[...] = lanes((norm, step, ratio, step_next))
-    lifted = product(load((lift_h_ref, lift_l_ref)), split(last_ref[...]))
+    lifted = lifted_ref[...]
     keep = keep_ref[...]
     h_a, x_a = pltpu.roll(keep, 96, 1), pltpu.roll(keep, 32, 1)
     mixed_ref[...] = (
@@ -875,9 +892,9 @@
     recv = exchange(send)
     grams = [(48, 128)] + [pltpu.VMEM((total, 128), jnp.bfloat16)] * 4
     group = lax.axis_index("grp").reshape(1)
-    *matrices, side = call(
+    *matrices, side, small_h, small_l = call(
         matrix_kernel,
-        pair_of(2 * total, total) + pair_of(K0 * N1, total) + [(192, 384)],
+        pair_of(2 * total, total) + pair_of(K0 * N1, total) + [(192, 384)] + pair_of(K0, N0),
         grams,
         group, *outer,
         scalars=(0,),
@@ -921,8 +938,8 @@
     send, scalars = call(
         third_column_kernel,
         [(DEVICES * 10, 128), (8, 128)],
-        [(total, 128), (K0 * N1, 128)],
-        recv, *lift, keep, scalars,
+        [(32, 384), (K0 * N1, 128), (K0 * N1, 128)],
+        recv, small_h, small_l, keep, scalars,
     )
     late = exchange(send)
     solution_part, part = call(

time: 79 us -> 79 us (level)
  no operation moved by 1% of the time
where the time goes in v7:
time: 79 us; the launch traced here: 78.6 us
  blocking collectives  31.9 us (40%)
  Pallas kernels  17.6 us (22%)
  waiting for transfers between devices  15 us (19%)
  starting transfers between devices  12.6 us (16%)
    all_to_all x3, blocking collectives, exchange(): lax.all_to_all(buffer.reshape(shape), ('slab', 'grp'), 0, 0, tiled=True)  31.9 us
    pallas_call x10, Pallas kernels, call(): pl.pallas_call(kernel, out_shape=[shape if isinstance(shape, jax.ShapeDty...  17.6 us
    all_to_all x3, waiting for transfers between devices, exchange(): lax.all_to_all(buffer.reshape(shape), ('slab', 'grp'), 0, 0, tiled=True)  13.5 us
    all_to_all x3, starting transfers between devices, exchange(): lax.all_to_all(buffer.reshape(shape), ('slab', 'grp'), 0, 0, tiled=True)  12.5 us
  transfers between devices with their start and end apart: 4, of which 4 were waited for; matrix products, arithmetic and copies ran while one was open for 0% of the time, Pallas kernels for 10%

profile of v7, /device:TPU:0, one launch (start us, length us, event | category | flops | bytes accessed | tf_op | source)
XLA Modules:
  0.0 78.6 jit_solution(9938925508266415186)
XLA Ops:
  0.6 2.9 %shard_map.113 = (f32[160,128]{1,0:T(8,128)}, f32[416,256]{1,0:T(8,128)}, bf16[704,128]{1,0:T(8,128)(2,1)}) custom-call(f32[5,2,3200]{2,1,0:T(2,128)} %bitcast.32, f32[5,2,3200]{2,1,0:T(2,128)} %bitcast.33, s32[64]{0:T(128)} %start2_hbm.1, f32[4,64]{1,0:T(4,128)} %bitcast.35, s32[50]{0:T(128)} %start3_hbm.1, f32[4,50]{1,0:T(4,128)} %bitcast.36), custom_call_target="tpu_custom_call" | custom-call | tf_op jit(solution)/shard_map/pallas_call | solution.py:830
  3.5 7.3 %all-to-all-start = ((f32[32,1,640]{2,1,0:T(1,128)}), f32[32,1,640]{2,1,0:T(1,128)S(1)}, u32[]{:S(2)}, u32[]{:S(2)}) async-start(f32[32,1,640]{2,1,0:T(1,128)} %bitcast.34), calls=%async_computation | async-start | bytes 163840 | tf_op jit(solution)/shard_map/all_to_all | solution.py:854
  10.9 0.0 copy-start.3
  10.9 0.0 copy-start.2
  10.9 0.0 copy-start.4
  10.9 0.0 copy-start.5
  10.9 0.6 copy-done.3
  11.5 0.0 copy-done.2
  11.6 0.0 copy-done.4
  11.6 0.0 copy-done.5
  11.6 3.2 %shard_map.114 = (bf16[640,320]{1,0:T(8,128)(2,1)S(1)}, bf16[640,320]{1,0:T(8,128)(2,1)S(1)}, bf16[640,320]{1,0:T(8,128)(2,1)S(1)}, bf16[640,320]{1,0:T(8,128)(2...) custom-call(s32[1]{0:T(128)} %bitcast.6.group_ref, s32[32]{0:T(128)S(1)} %copy-done.4, ...), custom_call_target="tpu_custom_call" | custom-call | tf_op jit(solution)/shard_map/pallas_call | solution.py:830
  14.8 3.7 %all-to-all-done = f32[32,1,640]{2,1,0:T(1,128)S(1)} async-done(((f32[32,1,640]{2,1,0:T(1,128)}), f32[32,1,640]{2,1,0:T(1,128)S(1)}, u32[]{:S(2)}, u32[]{:S(2)}) %all-to-all-start) | async-done | bytes 81952 | tf_op jit(solution)/shard_map/all_to_all | solution.py:854
  18.5 0.0 copy-start
  18.5 0.9 %shard_map.115 = (f32[128,128]{1,0:T(8,128)S(1)}, f32[320,128]{1,0:T(8,128)S(1)}, f32[320,128]{1,0:T(8,128)S(1)}) custom-call(f32[160,128]{1,0:T(8,128)S(1)} %bitcast.24, bf16[640,320]{1,0:T(8,128)(2,1)S(1)} %get-tuple-element.29.gram_h_ref, bf16[640,320]{1,0:T(8,128)(2,1)S(1)} %get-tuple-element.30.gram_l_ref), custom_call_target="tpu_custom_call" | custom-call | tf_op jit(solution)/shard_map/pallas_call | solution.py:830
  19.4 9.4 %all_to_all.30 = f32[32,4,128]{2,1,0:T(4,128)S(1)} all-to-all(f32[32,4,128]{2,1,0:T(4,128)S(1)} %bitcast.29), channel_id=1, replica_groups=mesh['slab'=16,'grp'=2] {'slab','grp'}, dimensions={0} | all-to-all | bytes 131072 | tf_op jit(solution)/shard_map/all_to_all | solution.py:854
  28.8 0.0 copy-done
  28.8 0.0 copy-done.1
  28.8 1.2 %shard_map.116 = (f32[128,128]{1,0:T(8,128)S(1)}, f32[8,128]{1,0:T(8,128)S(1)}, f32[416,256]{1,0:T(8,128)S(1)}) custom-call(f32[128,128]{1,0:T(8,128)S(1)} %bitcast.26, f32[416,256]{1,0:T(8,128)S(1)} %copy-done, bf16[704,128]{1,0:T(8,128)(2,1)S(1)} %copy-done.1), custom_call_target="tpu_custom_call", output_to_operand_aliasing={{2}: (1, {})} | custom-call | tf_op jit(solution)/shard_map/pallas_call | solution.py:830
  30.0 9.1 %all_to_all.31 = f32[32,4,128]{2,1,0:T(4,128)S(1)} all-to-all(f32[32,4,128]{2,1,0:T(4,128)S(1)} %bitcast.28), channel_id=1, replica_groups=mesh['slab'=16,'grp'=2] {'slab','grp'}, dimensions={0} | all-to-all | bytes 131072 | tf_op jit(solution)/shard_map/all_to_all | solution.py:854
  39.1 1.2 %shard_map.117 = (f32[128,128]{1,0:T(8,128)}, f32[320,128]{1,0:T(8,128)S(1)}, f32[8,128]{1,0:T(8,128)S(1)}) custom-call(f32[128,128]{1,0:T(8,128)S(1)} %bitcast.27, bf16[640,320]{1,0:T(8,128)(2,1)S(1)} %get-tuple-element.29.gram_h_ref, bf16[640,320]{1,0:T(8,128)(2,1)S(1)} %get-tuple-element.30.gram_l_ref, ...), custom_call_target="tpu_custom_call", output_to_operand_aliasing={{1}: (3, {})} | custom-call | tf_op jit(solution)/shard_map/pallas_call | solution.py:830
  40.3 2.6 %all-to-all-start.3 = ((f32[32,4,128]{2,1,0:T(4,128)}), f32[32,4,128]{2,1,0:T(4,128)S(1)}, u32[]{:S(2)}, u32[]{:S(2)}) async-start(f32[32,4,128]{2,1,0:T(4,128)} %bitcast.13), calls=%async_computation.3 | async-start | bytes 131072 | tf_op jit(solution)/shard_map/all_to_all | solution.py:854
  42.8 2.4 %shard_map.118 = (f32[608,128]{1,0:T(8,128)S(1)}, f32[640,128]{1,0:T(8,128)S(1)}, f32[8,128]{1,0:T(8,128)S(1)}) custom-call(f32[320,128]{1,0:T(8,128)S(1)} %get-tuple-element.38.blend_ref, bf16[640,320]{1,0:T(8,128)(2,1)S(1)} %get-tuple-element.39.lift_h_ref, bf16[640,320]{1,0:T(8,128)(2,1)S(1)} %get-tuple-element.40.lift_l_ref, ...), custom_call_target="tpu_custom_call" | custom-call | tf_op jit(solution)/shard_map/pallas_call | solution.py:830
  45.3 5.0 %all-to-all-done.3 = f32[32,4,128]{2,1,0:T(4,128)S(1)} async-done(((f32[32,4,128]{2,1,0:T(4,128)}), f32[32,4,128]{2,1,0:T(4,128)S(1)}, u32[]{:S(2)}, u32[]{:S(2)}) %all-to-all-start.3) | async-done | bytes 65568 | tf_op jit(solution)/shard_map/all_to_all | solution.py:854
  50.2 1.2 %shard_map.119 = f32[608,128]{1,0:T(8,128)S(1)} custom-call(f32[608,128]{1,0:T(8,128)S(1)} %get-tuple-element.43.early_ref, f32[128,128]{1,0:T(8,128)S(1)} %bitcast.25, f32[8,128]{1,0:T(8,128)S(1)} %get-tuple-element.45.sums_ref, f32[8,128]{1,0:T(8,128)S(1)} %get-tuple-element.41.scalar_ref, ...), custom_call_target="tpu_custom_call", output_to_operand_aliasing={{}: (0, {})} | custom-call | tf_op jit(solution)/shard_map/pallas_call | solution.py:830
  51.5 13.4 %all_to_all.32 = f32[32,1,2432]{2,1,0:T(1,128)S(1)} all-to-all(f32[32,1,2432]{2,1,0:T(1,128)S(1)} %bitcast.22), channel_id=1, replica_groups=mesh['slab'=16,'grp'=2] {'slab','grp'}, dimensions={0} | all-to-all | bytes 622592 | tf_op jit(solution)/shard_map/all_to_all | solution.py:854
  64.9 1.2 %shard_map.120 = (f32[320,128]{1,0:T(8,128)}, f32[8,128]{1,0:T(8,128)S(1)}) custom-call(f32[608,128]{1,0:T(8,128)S(1)} %bitcast.19, bf16[64,32]{1,0:T(8,128)(2,1)S(1)} %get-tuple-element.47.small_h_ref, bf16[64,32]{1,0:T(8,128)(2,1)S(1)} %get-tuple-element.48.small_l_ref, f32[640,128]{1,0:T(8,128)S(1)} %get-tuple-element.49.keep_ref, ...), custom_call_target="tpu_custom_call" | custom-call | tf_op jit(solution)/shard_map/pallas_call | solution.py:830
  66.1 2.6 %all-to-all-start.5 = ((f32[32,1,1280]{2,1,0:T(1,128)}), f32[32,1,1280]{2,1,0:T(1,128)S(1)}, u32[]{:S(2)}, u32[]{:S(2)}) async-start(f32[32,1,1280]{2,1,0:T(1,128)} %bitcast.17), calls=%async_computation.5 | async-start | bytes 327680 | tf_op jit(solution)/shard_map/all_to_all | solution.py:854
  68.7 0.2 collective-permute-start
  68.9 1.5 %collective-permute-done.partner_ref = f32[608,128]{1,0:T(8,128)S(1)} collective-permute-done((f32[608,128]{1,0:T(8,128)S(1)}, f32[608,128]{1,0:T(8,128)S(1)}, u32[]{:S(2)}, u32[]{:S(2)}) %collective-permute-start) | collective-permute-done | bytes 311328 | tf_op jit(solution)/shard_map/ppermute | solution.py:937
  70.4 2.0 %shard_map.121 = (f32[4,32,1024]{2,1,0:T(8,128)}, f32[128,1024]{1,0:T(8,128)S(1)}) custom-call(f32[608,128]{1,0:T(8,128)S(1)} %bitcast.21, f32[608,128]{1,0:T(8,128)S(1)} %collective-permute-done.partner_ref, f32[192,384]{1,0:T(8,128)S(1)} %get-tuple-element.42.side_ref, f32[8,128]{1,0:T(8,128)S(1)} %get-tuple-element.50.scalar_ref), custom_call_target="tpu_custom_call" | custom-call | tf_op jit(solution)/shard_map/pallas_call | solution.py:830
  72.3 4.9 %all-to-all-done.5 = f32[32,1,1280]{2,1,0:T(1,128)S(1)} async-done(((f32[32,1,1280]{2,1,0:T(1,128)}), f32[32,1,1280]{2,1,0:T(1,128)S(1)}, u32[]{:S(2)}, u32[]{:S(2)}) %all-to-all-start.5) | async-done | bytes 163872 | tf_op jit(solution)/shard_map/all_to_all | solution.py:854
  77.3 1.3 %shard_map.122 = f32[4,32,1024]{2,1,0:T(8,128)} custom-call(f32[320,128]{1,0:T(8,128)S(1)} %bitcast.23, f32[192,384]{1,0:T(8,128)S(1)} %get-tuple-element.42.side_ref, f32[128,1024]{1,0:T(8,128)S(1)} %get-tuple-element.53.part_ref), custom_call_target="tpu_custom_call" | custom-call | tf_op jit(solution)/shard_map/pallas_call | solution.py:830
  (1 shorter events, 0.0 us)
Async XLA Ops:
  3.5 14.9 %all-to-all-start = ((f32[32,1,640]{2,1,0:T(1,128)}), f32[32,1,640]{2,1,0:T(1,128)S(1)}, u32[]{:S(2)}, u32[]{:S(2)}) async-start(f32[32,1,640]{2,1,0:T(1,128)} %bitcast.34), calls=%async_computation | async-start | bytes 163840 | tf_op jit(solution)/shard_map/all_to_all | solution.py:854
  10.9 0.7 copy-start.3
  10.9 0.7 copy-start.2
  10.9 0.7 copy-start.4
  10.9 0.7 copy-start.5
  18.5 10.4 %copy-start = (f32[416,256]{1,0:T(8,128)S(1)}, f32[416,256]{1,0:T(8,128)}, u32[]{:S(2)}) copy-start(f32[416,256]{1,0:T(8,128)} %get-tuple-element.32.wide_ref) | copy-start | bytes 1277956
  18.5 10.4 %copy-start.1 = (bf16[704,128]{1,0:T(8,128)(2,1)S(1)}, bf16[704,128]{1,0:T(8,128)(2,1)}, u32[]{:S(2)}) copy-start(bf16[704,128]{1,0:T(8,128)(2,1)} %get-tuple-element.33.inner_ref) | copy-start | bytes 540676
  40.3 10.0 %all-to-all-start.3 = ((f32[32,4,128]{2,1,0:T(4,128)}), f32[32,4,128]{2,1,0:T(4,128)S(1)}, u32[]{:S(2)}, u32[]{:S(2)}) async-start(f32[32,4,128]{2,1,0:T(4,128)} %bitcast.13), calls=%async_computation.3 | async-start | bytes 131072 | tf_op jit(solution)/shard_map/all_to_all | solution.py:854
  66.1 11.2 %all-to-all-start.5 = ((f32[32,1,1280]{2,1,0:T(1,128)}), f32[32,1,1280]{2,1,0:T(1,128)S(1)}, u32[]{:S(2)}, u32[]{:S(2)}) async-start(f32[32,1,1280]{2,1,0:T(1,128)} %bitcast.17), calls=%async_computation.5 | async-start | bytes 327680 | tf_op jit(solution)/shard_map/all_to_all | solution.py:854
  68.7 1.7 %collective-permute-start = (f32[608,128]{1,0:T(8,128)S(1)}, f32[608,128]{1,0:T(8,128)S(1)}, u32[]{:S(2)}, u32[]{:S(2)}) collective-permute-start(f32[608,128]{1,0:T(8,128)S(1)} %bitcast.20), channel_id=1, source_target_pairs={{0,1},{1,0},{2,3},{3,2},{4,5},{5,4},{6,7},{7,6},{8,9},{9,8},{10,11... | collective-permute-start | bytes 933896 | tf_op jit(solution)/shard_map/ppermute | solution.py:937

commit v8 on v7

--- a/solution.py
+++ b/solution.py
@@ -156,7 +156,8 @@
 N0, N1 = 32, 10
 HI = lax.Precision.HIGHEST
 f32 = jnp.float32
-JOINT = 19
+JOINT = 18
+PLAIN = 3
 LARGE = 60
 
 
@@ -299,15 +300,15 @@
     return out
 
 
-def spread(ref, row, count, values):
-    one = lanes(values)
-    put(ref, row, count, jnp.concatenate([one] * 4, axis=0))
-
-
-def totals(ref, row, count, number):
-    summed = jnp.sum(ref[pl.ds(row, 32, stride=count), :], axis=0, keepdims=True)
+def with_scalars(tile, values):
+    one = pltpu.roll(lanes(values), 64, 1)
+    return jnp.where(iota((32, 128), 1) < 64, tile, jnp.concatenate([one] * 4, axis=0))
+
+
+def totals(ref, count, number):
+    summed = jnp.sum(ref[pl.ds(2, 32, stride=count), :], axis=0, keepdims=True)
     lane = iota((1, 128), 1)
-    return [jnp.sum(jnp.where(lane == k, summed, 0.0)) for k in range(number)]
+    return [jnp.sum(jnp.where(lane == 64 + k, summed, 0.0)) for k in range(number)]
 
 
 def pick(ref, k):
@@ -355,8 +356,8 @@
             )
         )
     ]
-    for k in (4, 5, 1, 0, 3, 2):
-        copies[k].start()
+    for copy in copies:
+        copy.start()
     copies[0].wait()
     copies[1].wait()
     pick_bin = (iota((256, N3), 0) % N3 == iota((256, N3), 1)) & (iota((256, N3), 0) < 4 * N3)
@@ -551,11 +552,10 @@
     images_ref[...] = images
     norm = jnp.sum(jnp.where(lane < 32, fields * images, 0.0))
     bend = jnp.sum(jnp.where(lane < 32, fields * pltpu.roll(images, 96, 1), 0.0))
-    send_rows(send_ref, images_ref)
-    spread(send_ref, 3, 4, (norm, bend))
-
-
-def send_rows(send_ref, value_ref):
+    send_rows(send_ref, images_ref, (norm, bend))
+
+
+def send_rows(send_ref, value_ref, values=()):
     for j in range(3):
         parts = []
         for q in range(4):
@@ -564,17 +564,20 @@
                 parts.append(move(value_ref[32 * r : 32 * r + 32, :], 0, q))
             else:
                 parts.append(jnp.zeros((32, 128), f32))
-        put(send_ref, j, 4, merge(parts))
+        tile = merge(parts)
+        put(send_ref, j, PLAIN, with_scalars(tile, values) if j == 2 else tile)
 
 
 def received_rows(recv_ref):
-    return jnp.concatenate([recv_ref[pl.ds(j, 32, stride=4), :] for j in range(3)], axis=1)
+    tiles = [recv_ref[pl.ds(j, 32, stride=PLAIN), :] for j in range(3)]
+    tiles[2] = jnp.where(iota((32, 128), 1) < 64, tiles[2], 0.0)
+    return jnp.concatenate(tiles, axis=1)
 
 
 def first_row_kernel(
     recv_ref, wide_ref, inner_ref, send_ref, scalar_ref, carried_ref, rows_ref, stack_ref,
 ):
-    norm, bend = totals(recv_ref, 3, 4, 2)
+    norm, bend = totals(recv_ref, PLAIN, 2)
     scalar_ref[...] = lanes((norm, bend))
     kron, second, turned = constants(inner_ref)
     field = mixed_to_table(received_rows(recv_ref), kron, second, rows_ref, stack_ref)
@@ -583,9 +586,9 @@
     mixed = table_to_mixed(weighted, kron, turned, rows_ref, stack_ref)
     carried_ref[...] = wide_ref[...]
     keep_rows(carried_ref, 0, mixed)
-    for j in range(3):
-        put(send_ref, j, 4, tile_of(mixed, j))
-    spread(send_ref, 3, 4, (energy,))
+    for j in range(2):
+        put(send_ref, j, PLAIN, tile_of(mixed, j))
+    put(send_ref, 2, PLAIN, with_scalars(tile_of(mixed, 2), (energy,)))
 
 
 def second_column_kernel(
@@ -594,9 +597,9 @@
 ):
     zero = jnp.zeros((32, 128), f32)
     for r in range(ROWS):
-        part = unpack(recv_ref, r // 4, 4, r, r % 4, 0)
+        part = unpack(recv_ref, r // 4, PLAIN, r, r % 4, 0)
         next_ref[32 * r : 32 * r + 32, :] = merge([part, zero])
-    (energy,) = totals(recv_ref, 3, 4, 1)
+    (energy,) = totals(recv_ref, PLAIN, 1)
     norm, bend = pick(scalar_ref, 0), pick(scalar_ref, 1)
     step = norm / (energy + 0.1 * bend)
     out_scalar_ref[...] = lanes((norm, step))
@@ -605,7 +608,6 @@
     image = product(gram, split(following))
     image_ref[...] = images - step * (image + 0.1 * pltpu.roll(images, 96, 1))
     send_rows(send_ref, image_ref)
-    put(send_ref, 3, 4, zero)
     lane = iota(fields.shape, 1)
     reduced = fields - step * (following + 0.1 * pltpu.roll(fields, 96, 1))
     kept = jnp.where(lane < 64, 0.0, pltpu.roll(fields, 64, 1))
@@ -695,7 +697,7 @@
             )
     sums_ref[...] = lanes((jnp.sum(norm), jnp.sum(bend)))
     for block in range(3):
-        send_halves(send_ref, JOINT, 4 + 5 * block, keep_ref, block)
+        send_halves(send_ref, JOINT, PLAIN + 5 * block, keep_ref, block)
 
 
 def second_row_kernel(
@@ -714,9 +716,10 @@
     weighted = wide_ref[0:256, :] * field
     energy = jnp.sum(field * weighted)
     mixed = table_to_mixed(weighted, kron, turned, rows_ref, stack_ref)
-    for j in range(3):
+    for j in range(2):
         put(send_ref, j, JOINT, tile_of(mixed, j))
-    spread(send_ref, 3, JOINT, (energy, pick(sums_ref, 0), pick(sums_ref, 1) + inner))
+    values = (energy, pick(sums_ref, 0), pick(sums_ref, 1) + inner)
+    put(send_ref, 2, JOINT, with_scalars(tile_of(mixed, 2), values))
 
 
 def third_column_kernel(
@@ -739,7 +742,7 @@
     packed = product(load((small_h_ref, small_l_ref)), split(packed_ref[...]))
     for n in range(N1):
         lifted_ref[K0 * n : K0 * n + K0, :] = move(tile_of(packed, n // 4), n % 4, 0)
-    energy, norm_next, bend = totals(recv_ref, 3, JOINT, 3)
+    energy, norm_next, bend = totals(recv_ref, JOINT, 3)
     norm, step = pick(scalar_ref, 0), pick(scalar_ref, 1)
     ratio = norm_next / norm
     curve = energy + 0.1 * bend - ratio * norm_next / step
@@ -786,7 +789,7 @@
 def settle_kernel(own_ref, partner_ref, side_ref, scalar_ref, solution_ref, part_ref, early):
     for block in range(3):
         for h, ref in enumerate((own_ref, partner_ref)):
-            gather_blocks(ref, JOINT, 4 + 5 * block, 5, early, 40 * block + 20 * h)
+            gather_blocks(ref, JOINT, PLAIN + 5 * block, 5, early, 40 * block + 20 * h)
     step, ratio, step_next = pick(scalar_ref, 1), pick(scalar_ref, 2), pick(scalar_ref, 3)
     small = 0.1 * step
     value = split(side_ref[0:128, 128:208])
@@ -901,12 +904,12 @@
     )
     gram, lift = matrices[0:2], matrices[2:4]
     send, fields, images = call(
-        first_column_kernel, [(128, 128), (total, 128), (total, 128)], [], recv, *gram
+        first_column_kernel, [(32 * PLAIN, 128), (total, 128), (total, 128)], [], recv, *gram
     )
     recv = exchange(send)
     send, scalars, wide = call(
         first_row_kernel,
-        [(128, 128), (8, 128), (416, 256)],
+        [(32 * PLAIN, 128), (8, 128), (416, 256)],
         work,
         recv, wide, inner,
         aliases={1: 2},
@@ -914,7 +917,7 @@
     recv = exchange(send)
     send, blend, scalars = call(
         second_column_kernel,
-        [(128, 128), (total, 128), (8, 128)],
+        [(32 * PLAIN, 128), (total, 128), (8, 128)],
         [(total, 128), (total, 128)],
         recv, *gram, fields, images, scalars,
         aliases={3: 1},

time: 79 us -> 78.3 us (level)
  no operation moved by 1% of the time
where the time goes in v8:
time: 78.3 us; the launch traced here: 78 us
  blocking collectives  31.4 us (40%)
  Pallas kernels  17.6 us (22%)
  waiting for transfers between devices  14.9 us (19%)
  starting transfers between devices  12.6 us (16%)
    all_to_all x3, blocking collectives, exchange(): lax.all_to_all(buffer.reshape(shape), ('slab', 'grp'), 0, 0, tiled=True)  31.4 us
    pallas_call x10, Pallas kernels, call(): pl.pallas_call(kernel, out_shape=[shape if isinstance(shape, jax.ShapeDty...  17.6 us
    all_to_all x3, waiting for transfers between devices, exchange(): lax.all_to_all(buffer.reshape(shape), ('slab', 'grp'), 0, 0, tiled=True)  13.5 us
    all_to_all x3, starting transfers between devices, exchange(): lax.all_to_all(buffer.reshape(shape), ('slab', 'grp'), 0, 0, tiled=True)  12.5 us
  transfers between devices with their start and end apart: 4, of which 4 were waited for; matrix products, arithmetic and copies ran while one was open for 0% of the time, Pallas kernels for 10%

profile of v8, /device:TPU:0, one launch (start us, length us, event | category | flops | bytes accessed | tf_op | source)
XLA Modules:
  0.0 78.0 jit_solution(8253724599189129171)
XLA Ops:
  0.6 2.8 %shard_map.113 = (f32[160,128]{1,0:T(8,128)}, f32[416,256]{1,0:T(8,128)}, bf16[704,128]{1,0:T(8,128)(2,1)}) custom-call(f32[5,2,3200]{2,1,0:T(2,128)} %bitcast.32, f32[5,2,3200]{2,1,0:T(2,128)} %bitcast.33, s32[64]{0:T(128)} %start2_hbm.1, f32[4,64]{1,0:T(4,128)} %bitcast.35, s32[50]{0:T(128)} %start3_hbm.1, f32[4,50]{1,0:T(4,128)} %bitcast.36), custom_call_target="tpu_custom_call" | custom-call | tf_op jit(solution)/shard_map/pallas_call | solution.py:833
  3.4 7.3 %all-to-all-start = ((f32[32,1,640]{2,1,0:T(1,128)}), f32[32,1,640]{2,1,0:T(1,128)S(1)}, u32[]{:S(2)}, u32[]{:S(2)}) async-start(f32[32,1,640]{2,1,0:T(1,128)} %bitcast.34), calls=%async_computation | async-start | bytes 163840 | tf_op jit(solution)/shard_map/all_to_all | solution.py:857
  10.7 0.0 copy-start.3
  10.8 0.0 copy-start.2
  10.8 0.0 copy-start.4
  10.8 0.0 copy-start.5
  10.8 0.6 copy-done.3
  11.4 0.0 copy-done.2
  11.4 0.0 copy-done.4
  11.4 0.0 copy-done.5
  11.5 3.2 %shard_map.114 = (bf16[640,320]{1,0:T(8,128)(2,1)S(1)}, bf16[640,320]{1,0:T(8,128)(2,1)S(1)}, bf16[640,320]{1,0:T(8,128)(2,1)S(1)}, bf16[640,320]{1,0:T(8,128)(2...) custom-call(s32[1]{0:T(128)} %bitcast.6.group_ref, s32[32]{0:T(128)S(1)} %copy-done.4, ...), custom_call_target="tpu_custom_call" | custom-call | tf_op jit(solution)/shard_map/pallas_call | solution.py:833
  14.7 3.6 %all-to-all-done = f32[32,1,640]{2,1,0:T(1,128)S(1)} async-done(((f32[32,1,640]{2,1,0:T(1,128)}), f32[32,1,640]{2,1,0:T(1,128)S(1)}, u32[]{:S(2)}, u32[]{:S(2)}) %all-to-all-start) | async-done | bytes 81952 | tf_op jit(solution)/shard_map/all_to_all | solution.py:857
  18.3 0.0 copy-start
  18.3 1.0 %shard_map.115 = (f32[96,128]{1,0:T(8,128)S(1)}, f32[320,128]{1,0:T(8,128)S(1)}, f32[320,128]{1,0:T(8,128)S(1)}) custom-call(f32[160,128]{1,0:T(8,128)S(1)} %bitcast.24, bf16[640,320]{1,0:T(8,128)(2,1)S(1)} %get-tuple-element.29.gram_h_ref, bf16[640,320]{1,0:T(8,128)(2,1)S(1)} %get-tuple-element.30.gram_l_ref), custom_call_target="tpu_custom_call" | custom-call | tf_op jit(solution)/shard_map/pallas_call | solution.py:833
  19.3 9.3 %all_to_all.30 = f32[32,1,384]{2,1,0:T(1,128)S(1)} all-to-all(f32[32,1,384]{2,1,0:T(1,128)S(1)} %bitcast.29), channel_id=1, replica_groups=mesh['slab'=16,'grp'=2] {'slab','grp'}, dimensions={0} | all-to-all | bytes 98304 | tf_op jit(solution)/shard_map/all_to_all | solution.py:857
  28.7 0.0 copy-done
  28.7 0.0 copy-done.1
  28.7 1.2 %shard_map.116 = (f32[96,128]{1,0:T(8,128)S(1)}, f32[8,128]{1,0:T(8,128)S(1)}, f32[416,256]{1,0:T(8,128)S(1)}) custom-call(f32[96,128]{1,0:T(8,128)S(1)} %bitcast.26, f32[416,256]{1,0:T(8,128)S(1)} %copy-done, bf16[704,128]{1,0:T(8,128)(2,1)S(1)} %copy-done.1), custom_call_target="tpu_custom_call", output_to_operand_aliasing={{2}: (1, {})} | custom-call | tf_op jit(solution)/shard_map/pallas_call | solution.py:833
  29.8 9.0 %all_to_all.31 = f32[32,1,384]{2,1,0:T(1,128)S(1)} all-to-all(f32[32,1,384]{2,1,0:T(1,128)S(1)} %bitcast.28), channel_id=1, replica_groups=mesh['slab'=16,'grp'=2] {'slab','grp'}, dimensions={0} | all-to-all | bytes 98304 | tf_op jit(solution)/shard_map/all_to_all | solution.py:857
  38.9 1.2 %shard_map.117 = (f32[96,128]{1,0:T(8,128)}, f32[320,128]{1,0:T(8,128)S(1)}, f32[8,128]{1,0:T(8,128)S(1)}) custom-call(f32[96,128]{1,0:T(8,128)S(1)} %bitcast.27, bf16[640,320]{1,0:T(8,128)(2,1)S(1)} %get-tuple-element.29.gram_h_ref, bf16[640,320]{1,0:T(8,128)(2,1)S(1)} %get-tuple-element.30.gram_l_ref, ...), custom_call_target="tpu_custom_call", output_to_operand_aliasing={{1}: (3, {})} | custom-call | tf_op jit(solution)/shard_map/pallas_call | solution.py:833
  40.0 2.6 %all-to-all-start.3 = ((f32[32,1,384]{2,1,0:T(1,128)}), f32[32,1,384]{2,1,0:T(1,128)S(1)}, u32[]{:S(2)}, u32[]{:S(2)}) async-start(f32[32,1,384]{2,1,0:T(1,128)} %bitcast.13), calls=%async_computation.3 | async-start | bytes 98304 | tf_op jit(solution)/shard_map/all_to_all | solution.py:857
  42.6 2.4 %shard_map.118 = (f32[576,128]{1,0:T(8,128)S(1)}, f32[640,128]{1,0:T(8,128)S(1)}, f32[8,128]{1,0:T(8,128)S(1)}) custom-call(f32[320,128]{1,0:T(8,128)S(1)} %get-tuple-element.38.blend_ref, bf16[640,320]{1,0:T(8,128)(2,1)S(1)} %get-tuple-element.39.lift_h_ref, bf16[640,320]{1,0:T(8,128)(2,1)S(1)} %get-tuple-element.40.lift_l_ref, ...), custom_call_target="tpu_custom_call" | custom-call | tf_op jit(solution)/shard_map/pallas_call | solution.py:833
  45.1 4.9 %all-to-all-done.3 = f32[32,1,384]{2,1,0:T(1,128)S(1)} async-done(((f32[32,1,384]{2,1,0:T(1,128)}), f32[32,1,384]{2,1,0:T(1,128)S(1)}, u32[]{:S(2)}, u32[]{:S(2)}) %all-to-all-start.3) | async-done | bytes 49184 | tf_op jit(solution)/shard_map/all_to_all | solution.py:857
  49.9 1.2 %shard_map.119 = f32[576,128]{1,0:T(8,128)S(1)} custom-call(f32[576,128]{1,0:T(8,128)S(1)} %get-tuple-element.43.early_ref, f32[96,128]{1,0:T(8,128)S(1)} %bitcast.25, f32[8,128]{1,0:T(8,128)S(1)} %get-tuple-element.45.sums_ref, f32[8,128]{1,0:T(8,128)S(1)} %get-tuple-element.41.scalar_ref, ...), custom_call_target="tpu_custom_call", output_to_operand_aliasing={{}: (0, {})} | custom-call | tf_op jit(solution)/shard_map/pallas_call | solution.py:833
  51.2 13.1 %all_to_all.32 = f32[32,1,2304]{2,1,0:T(1,128)S(1)} all-to-all(f32[32,1,2304]{2,1,0:T(1,128)S(1)} %bitcast.22), channel_id=1, replica_groups=mesh['slab'=16,'grp'=2] {'slab','grp'}, dimensions={0} | all-to-all | bytes 589824 | tf_op jit(solution)/shard_map/all_to_all | solution.py:857
  64.3 1.2 %shard_map.120 = (f32[320,128]{1,0:T(8,128)}, f32[8,128]{1,0:T(8,128)S(1)}) custom-call(f32[576,128]{1,0:T(8,128)S(1)} %bitcast.19, bf16[64,32]{1,0:T(8,128)(2,1)S(1)} %get-tuple-element.47.small_h_ref, bf16[64,32]{1,0:T(8,128)(2,1)S(1)} %get-tuple-element.48.small_l_ref, f32[640,128]{1,0:T(8,128)S(1)} %get-tuple-element.49.keep_ref, ...), custom_call_target="tpu_custom_call" | custom-call | tf_op jit(solution)/shard_map/pallas_call | solution.py:833
  65.5 2.6 %all-to-all-start.5 = ((f32[32,1,1280]{2,1,0:T(1,128)}), f32[32,1,1280]{2,1,0:T(1,128)S(1)}, u32[]{:S(2)}, u32[]{:S(2)}) async-start(f32[32,1,1280]{2,1,0:T(1,128)} %bitcast.17), calls=%async_computation.5 | async-start | bytes 327680 | tf_op jit(solution)/shard_map/all_to_all | solution.py:857
  68.1 0.2 collective-permute-start
  68.3 1.5 %collective-permute-done.partner_ref = f32[576,128]{1,0:T(8,128)S(1)} collective-permute-done((f32[576,128]{1,0:T(8,128)S(1)}, f32[576,128]{1,0:T(8,128)S(1)}, u32[]{:S(2)}, u32[]{:S(2)}) %collective-permute-start) | collective-permute-done | bytes 294944 | tf_op jit(solution)/shard_map/ppermute | solution.py:940
  69.7 2.0 %shard_map.121 = (f32[4,32,1024]{2,1,0:T(8,128)}, f32[128,1024]{1,0:T(8,128)S(1)}) custom-call(f32[576,128]{1,0:T(8,128)S(1)} %bitcast.21, f32[576,128]{1,0:T(8,128)S(1)} %collective-permute-done.partner_ref, f32[192,384]{1,0:T(8,128)S(1)} %get-tuple-element.42.side_ref, f32[8,128]{1,0:T(8,128)S(1)} %get-tuple-element.50.scalar_ref), custom_call_target="tpu_custom_call" | custom-call | tf_op jit(solution)/shard_map/pallas_call | solution.py:833
  71.7 4.9 %all-to-all-done.5 = f32[32,1,1280]{2,1,0:T(1,128)S(1)} async-done(((f32[32,1,1280]{2,1,0:T(1,128)}), f32[32,1,1280]{2,1,0:T(1,128)S(1)}, u32[]{:S(2)}, u32[]{:S(2)}) %all-to-all-start.5) | async-done | bytes 163872 | tf_op jit(solution)/shard_map/all_to_all | solution.py:857
  76.7 1.3 %shard_map.122 = f32[4,32,1024]{2,1,0:T(8,128)} custom-call(f32[320,128]{1,0:T(8,128)S(1)} %bitcast.23, f32[192,384]{1,0:T(8,128)S(1)} %get-tuple-element.42.side_ref, f32[128,1024]{1,0:T(8,128)S(1)} %get-tuple-element.53.part_ref), custom_call_target="tpu_custom_call" | custom-call | tf_op jit(solution)/shard_map/pallas_call | solution.py:833
  (1 shorter events, 0.0 us)
Async XLA Ops:
  3.4 14.9 %all-to-all-start = ((f32[32,1,640]{2,1,0:T(1,128)}), f32[32,1,640]{2,1,0:T(1,128)S(1)}, u32[]{:S(2)}, u32[]{:S(2)}) async-start(f32[32,1,640]{2,1,0:T(1,128)} %bitcast.34), calls=%async_computation | async-start | bytes 163840 | tf_op jit(solution)/shard_map/all_to_all | solution.py:857
  10.7 0.7 copy-start.3
  10.8 0.7 copy-start.2
  10.8 0.7 copy-start.4
  10.8 0.7 copy-start.5
  18.3 10.3 %copy-start = (f32[416,256]{1,0:T(8,128)S(1)}, f32[416,256]{1,0:T(8,128)}, u32[]{:S(2)}) copy-start(f32[416,256]{1,0:T(8,128)} %get-tuple-element.32.wide_ref) | copy-start | bytes 1277956
  18.3 10.3 %copy-start.1 = (bf16[704,128]{1,0:T(8,128)(2,1)S(1)}, bf16[704,128]{1,0:T(8,128)(2,1)}, u32[]{:S(2)}) copy-start(bf16[704,128]{1,0:T(8,128)(2,1)} %get-tuple-element.33.inner_ref) | copy-start | bytes 540676
  40.0 9.9 %all-to-all-start.3 = ((f32[32,1,384]{2,1,0:T(1,128)}), f32[32,1,384]{2,1,0:T(1,128)S(1)}, u32[]{:S(2)}, u32[]{:S(2)}) async-start(f32[32,1,384]{2,1,0:T(1,128)} %bitcast.13), calls=%async_computation.3 | async-start | bytes 98304 | tf_op jit(solution)/shard_map/all_to_all | solution.py:857
  65.5 11.2 %all-to-all-start.5 = ((f32[32,1,1280]{2,1,0:T(1,128)}), f32[32,1,1280]{2,1,0:T(1,128)S(1)}, u32[]{:S(2)}, u32[]{:S(2)}) async-start(f32[32,1,1280]{2,1,0:T(1,128)} %bitcast.17), calls=%async_computation.5 | async-start | bytes 327680 | tf_op jit(solution)/shard_map/all_to_all | solution.py:857
  68.1 1.6 %collective-permute-start = (f32[576,128]{1,0:T(8,128)S(1)}, f32[576,128]{1,0:T(8,128)S(1)}, u32[]{:S(2)}, u32[]{:S(2)}) collective-permute-start(f32[576,128]{1,0:T(8,128)S(1)} %bitcast.20), channel_id=1, source_target_pairs={{0,1},{1,0},{2,3},{3,2},{4,5},{5,4},{6,7},{7,6},{8,9},{9,8},{10,11... | collective-permute-start | bytes 884744 | tf_op jit(solution)/shard_map/ppermute | solution.py:940

commit v9 on v8

--- a/solution.py
+++ b/solution.py
@@ -186,6 +186,9 @@
     def one(x, y):
         return lax.dot_general(x, y, dims, preferred_element_type=f32)
 
+    if b[0].shape[1] == 128 and not transposed:
+        both = one(a[0], jnp.concatenate(b, axis=1))
+        return both[:, 0:128] + (both[:, 128:256] + one(a[1], b[0]))
     return one(a[0], b[0]) + (one(a[0], b[1]) + one(a[1], b[0]))
 
 

time: 78.3 us -> 78.1 us (level)
  no operation moved by 1% of the time
where the time goes in v9:
time: 78.1 us; the launch traced here: 77.8 us
  blocking collectives  31.5 us (40%)
  Pallas kernels  17.1 us (22%)
  waiting for transfers between devices  15.1 us (19%)
  starting transfers between devices  12.6 us (16%)
    all_to_all x3, blocking collectives, exchange(): lax.all_to_all(buffer.reshape(shape), ('slab', 'grp'), 0, 0, tiled=True)  31.5 us
    pallas_call x10, Pallas kernels, call(): pl.pallas_call(kernel, out_shape=[shape if isinstance(shape, jax.ShapeDty...  17.1 us
    all_to_all x3, waiting for transfers between devices, exchange(): lax.all_to_all(buffer.reshape(shape), ('slab', 'grp'), 0, 0, tiled=True)  13.6 us
    all_to_all x3, starting transfers between devices, exchange(): lax.all_to_all(buffer.reshape(shape), ('slab', 'grp'), 0, 0, tiled=True)  12.5 us
  transfers between devices with their start and end apart: 4, of which 4 were waited for; matrix products, arithmetic and copies ran while one was open for 0% of the time, Pallas kernels for 10%

profile of v9, /device:TPU:0, one launch (start us, length us, event | category | flops | bytes accessed | tf_op | source)
XLA Modules:
  0.0 77.8 jit_solution(12331784922125675364)
XLA Ops:
  0.6 2.7 %shard_map.113 = (f32[160,128]{1,0:T(8,128)}, f32[416,256]{1,0:T(8,128)}, bf16[704,128]{1,0:T(8,128)(2,1)}) custom-call(f32[5,2,3200]{2,1,0:T(2,128)} %bitcast.32, f32[5,2,3200]{2,1,0:T(2,128)} %bitcast.33, s32[64]{0:T(128)} %start2_hbm.1, f32[4,64]{1,0:T(4,128)} %bitcast.35, s32[50]{0:T(128)} %start3_hbm.1, f32[4,50]{1,0:T(4,128)} %bitcast.36), custom_call_target="tpu_custom_call" | custom-call | tf_op jit(solution)/shard_map/pallas_call | solution.py:836
  3.4 7.3 %all-to-all-start = ((f32[32,1,640]{2,1,0:T(1,128)}), f32[32,1,640]{2,1,0:T(1,128)S(1)}, u32[]{:S(2)}, u32[]{:S(2)}) async-start(f32[32,1,640]{2,1,0:T(1,128)} %bitcast.34), calls=%async_computation | async-start | bytes 163840 | tf_op jit(solution)/shard_map/all_to_all | solution.py:860
  10.7 0.0 copy-start.3
  10.7 0.0 copy-start.2
  10.7 0.0 copy-start.4
  10.7 0.0 copy-start.5
  10.7 0.6 copy-done.3
  11.4 0.0 copy-done.2
  11.4 0.0 copy-done.4
  11.4 0.0 copy-done.5
  11.4 3.3 %shard_map.114 = (bf16[640,320]{1,0:T(8,128)(2,1)S(1)}, bf16[640,320]{1,0:T(8,128)(2,1)S(1)}, bf16[640,320]{1,0:T(8,128)(2,1)S(1)}, bf16[640,320]{1,0:T(8,128)(2...) custom-call(s32[1]{0:T(128)} %bitcast.6.group_ref, s32[32]{0:T(128)S(1)} %copy-done.4, ...), custom_call_target="tpu_custom_call" | custom-call | tf_op jit(solution)/shard_map/pallas_call | solution.py:836
  14.7 3.6 %all-to-all-done = f32[32,1,640]{2,1,0:T(1,128)S(1)} async-done(((f32[32,1,640]{2,1,0:T(1,128)}), f32[32,1,640]{2,1,0:T(1,128)S(1)}, u32[]{:S(2)}, u32[]{:S(2)}) %all-to-all-start) | async-done | bytes 81952 | tf_op jit(solution)/shard_map/all_to_all | solution.py:860
  18.3 0.0 copy-start
  18.3 0.9 %shard_map.115 = (f32[96,128]{1,0:T(8,128)S(1)}, f32[320,128]{1,0:T(8,128)S(1)}, f32[320,128]{1,0:T(8,128)S(1)}) custom-call(f32[160,128]{1,0:T(8,128)S(1)} %bitcast.24, bf16[640,320]{1,0:T(8,128)(2,1)S(1)} %get-tuple-element.29.gram_h_ref, bf16[640,320]{1,0:T(8,128)(2,1)S(1)} %get-tuple-element.30.gram_l_ref), custom_call_target="tpu_custom_call" | custom-call | tf_op jit(solution)/shard_map/pallas_call | solution.py:836
  19.2 9.4 %all_to_all.30 = f32[32,1,384]{2,1,0:T(1,128)S(1)} all-to-all(f32[32,1,384]{2,1,0:T(1,128)S(1)} %bitcast.29), channel_id=1, replica_groups=mesh['slab'=16,'grp'=2] {'slab','grp'}, dimensions={0} | all-to-all | bytes 98304 | tf_op jit(solution)/shard_map/all_to_all | solution.py:860
  28.6 0.0 copy-done
  28.6 0.0 copy-done.1
  28.6 1.1 %shard_map.116 = (f32[96,128]{1,0:T(8,128)S(1)}, f32[8,128]{1,0:T(8,128)S(1)}, f32[416,256]{1,0:T(8,128)S(1)}) custom-call(f32[96,128]{1,0:T(8,128)S(1)} %bitcast.26, f32[416,256]{1,0:T(8,128)S(1)} %copy-done, bf16[704,128]{1,0:T(8,128)(2,1)S(1)} %copy-done.1), custom_call_target="tpu_custom_call", output_to_operand_aliasing={{2}: (1, {})} | custom-call | tf_op jit(solution)/shard_map/pallas_call | solution.py:836
  29.7 9.0 %all_to_all.31 = f32[32,1,384]{2,1,0:T(1,128)S(1)} all-to-all(f32[32,1,384]{2,1,0:T(1,128)S(1)} %bitcast.28), channel_id=1, replica_groups=mesh['slab'=16,'grp'=2] {'slab','grp'}, dimensions={0} | all-to-all | bytes 98304 | tf_op jit(solution)/shard_map/all_to_all | solution.py:860
  38.7 1.1 %shard_map.117 = (f32[96,128]{1,0:T(8,128)}, f32[320,128]{1,0:T(8,128)S(1)}, f32[8,128]{1,0:T(8,128)S(1)}) custom-call(f32[96,128]{1,0:T(8,128)S(1)} %bitcast.27, bf16[640,320]{1,0:T(8,128)(2,1)S(1)} %get-tuple-element.29.gram_h_ref, bf16[640,320]{1,0:T(8,128)(2,1)S(1)} %get-tuple-element.30.gram_l_ref, ...), custom_call_target="tpu_custom_call", output_to_operand_aliasing={{1}: (3, {})} | custom-call | tf_op jit(solution)/shard_map/pallas_call | solution.py:836
  39.8 2.6 %all-to-all-start.3 = ((f32[32,1,384]{2,1,0:T(1,128)}), f32[32,1,384]{2,1,0:T(1,128)S(1)}, u32[]{:S(2)}, u32[]{:S(2)}) async-start(f32[32,1,384]{2,1,0:T(1,128)} %bitcast.13), calls=%async_computation.3 | async-start | bytes 98304 | tf_op jit(solution)/shard_map/all_to_all | solution.py:860
  42.4 2.3 %shard_map.118 = (f32[576,128]{1,0:T(8,128)S(1)}, f32[640,128]{1,0:T(8,128)S(1)}, f32[8,128]{1,0:T(8,128)S(1)}) custom-call(f32[320,128]{1,0:T(8,128)S(1)} %get-tuple-element.38.blend_ref, bf16[640,320]{1,0:T(8,128)(2,1)S(1)} %get-tuple-element.39.lift_h_ref, bf16[640,320]{1,0:T(8,128)(2,1)S(1)} %get-tuple-element.40.lift_l_ref, ...), custom_call_target="tpu_custom_call" | custom-call | tf_op jit(solution)/shard_map/pallas_call | solution.py:836
  44.7 5.0 %all-to-all-done.3 = f32[32,1,384]{2,1,0:T(1,128)S(1)} async-done(((f32[32,1,384]{2,1,0:T(1,128)}), f32[32,1,384]{2,1,0:T(1,128)S(1)}, u32[]{:S(2)}, u32[]{:S(2)}) %all-to-all-start.3) | async-done | bytes 49184 | tf_op jit(solution)/shard_map/all_to_all | solution.py:860
  49.7 1.2 %shard_map.119 = f32[576,128]{1,0:T(8,128)S(1)} custom-call(f32[576,128]{1,0:T(8,128)S(1)} %get-tuple-element.43.early_ref, f32[96,128]{1,0:T(8,128)S(1)} %bitcast.25, f32[8,128]{1,0:T(8,128)S(1)} %get-tuple-element.45.sums_ref, f32[8,128]{1,0:T(8,128)S(1)} %get-tuple-element.41.scalar_ref, ...), custom_call_target="tpu_custom_call", output_to_operand_aliasing={{}: (0, {})} | custom-call | tf_op jit(solution)/shard_map/pallas_call | solution.py:836
  50.9 13.1 %all_to_all.32 = f32[32,1,2304]{2,1,0:T(1,128)S(1)} all-to-all(f32[32,1,2304]{2,1,0:T(1,128)S(1)} %bitcast.22), channel_id=1, replica_groups=mesh['slab'=16,'grp'=2] {'slab','grp'}, dimensions={0} | all-to-all | bytes 589824 | tf_op jit(solution)/shard_map/all_to_all | solution.py:860
  64.0 1.2 %shard_map.120 = (f32[320,128]{1,0:T(8,128)}, f32[8,128]{1,0:T(8,128)S(1)}) custom-call(f32[576,128]{1,0:T(8,128)S(1)} %bitcast.19, bf16[64,32]{1,0:T(8,128)(2,1)S(1)} %get-tuple-element.47.small_h_ref, bf16[64,32]{1,0:T(8,128)(2,1)S(1)} %get-tuple-element.48.small_l_ref, f32[640,128]{1,0:T(8,128)S(1)} %get-tuple-element.49.keep_ref, ...), custom_call_target="tpu_custom_call" | custom-call | tf_op jit(solution)/shard_map/pallas_call | solution.py:836
  65.3 2.6 %all-to-all-start.5 = ((f32[32,1,1280]{2,1,0:T(1,128)}), f32[32,1,1280]{2,1,0:T(1,128)S(1)}, u32[]{:S(2)}, u32[]{:S(2)}) async-start(f32[32,1,1280]{2,1,0:T(1,128)} %bitcast.17), calls=%async_computation.5 | async-start | bytes 327680 | tf_op jit(solution)/shard_map/all_to_all | solution.py:860
  67.8 0.2 collective-permute-start
  68.0 1.5 %collective-permute-done.partner_ref = f32[576,128]{1,0:T(8,128)S(1)} collective-permute-done((f32[576,128]{1,0:T(8,128)S(1)}, f32[576,128]{1,0:T(8,128)S(1)}, u32[]{:S(2)}, u32[]{:S(2)}) %collective-permute-start) | collective-permute-done | bytes 294944 | tf_op jit(solution)/shard_map/ppermute | solution.py:943
  69.5 1.9 %shard_map.121 = (f32[4,32,1024]{2,1,0:T(8,128)}, f32[128,1024]{1,0:T(8,128)S(1)}) custom-call(f32[576,128]{1,0:T(8,128)S(1)} %bitcast.21, f32[576,128]{1,0:T(8,128)S(1)} %collective-permute-done.partner_ref, f32[192,384]{1,0:T(8,128)S(1)} %get-tuple-element.42.side_ref, f32[8,128]{1,0:T(8,128)S(1)} %get-tuple-element.50.scalar_ref), custom_call_target="tpu_custom_call" | custom-call | tf_op jit(solution)/shard_map/pallas_call | solution.py:836
  71.4 5.0 %all-to-all-done.5 = f32[32,1,1280]{2,1,0:T(1,128)S(1)} async-done(((f32[32,1,1280]{2,1,0:T(1,128)}), f32[32,1,1280]{2,1,0:T(1,128)S(1)}, u32[]{:S(2)}, u32[]{:S(2)}) %all-to-all-start.5) | async-done | bytes 163872 | tf_op jit(solution)/shard_map/all_to_all | solution.py:860
  76.4 1.3 %shard_map.122 = f32[4,32,1024]{2,1,0:T(8,128)} custom-call(f32[320,128]{1,0:T(8,128)S(1)} %bitcast.23, f32[192,384]{1,0:T(8,128)S(1)} %get-tuple-element.42.side_ref, f32[128,1024]{1,0:T(8,128)S(1)} %get-tuple-element.53.part_ref), custom_call_target="tpu_custom_call" | custom-call | tf_op jit(solution)/shard_map/pallas_call | solution.py:836
  (1 shorter events, 0.0 us)
Async XLA Ops:
  3.4 14.9 %all-to-all-start = ((f32[32,1,640]{2,1,0:T(1,128)}), f32[32,1,640]{2,1,0:T(1,128)S(1)}, u32[]{:S(2)}, u32[]{:S(2)}) async-start(f32[32,1,640]{2,1,0:T(1,128)} %bitcast.34), calls=%async_computation | async-start | bytes 163840 | tf_op jit(solution)/shard_map/all_to_all | solution.py:860
  10.7 0.7 copy-start.3
  10.7 0.7 copy-start.2
  10.7 0.7 copy-start.4
  10.7 0.7 copy-start.5
  18.3 10.3 %copy-start = (f32[416,256]{1,0:T(8,128)S(1)}, f32[416,256]{1,0:T(8,128)}, u32[]{:S(2)}) copy-start(f32[416,256]{1,0:T(8,128)} %get-tuple-element.32.wide_ref) | copy-start | bytes 1277956
  18.3 10.3 %copy-start.1 = (bf16[704,128]{1,0:T(8,128)(2,1)S(1)}, bf16[704,128]{1,0:T(8,128)(2,1)}, u32[]{:S(2)}) copy-start(bf16[704,128]{1,0:T(8,128)(2,1)} %get-tuple-element.33.inner_ref) | copy-start | bytes 540676
  39.8 9.9 %all-to-all-start.3 = ((f32[32,1,384]{2,1,0:T(1,128)}), f32[32,1,384]{2,1,0:T(1,128)S(1)}, u32[]{:S(2)}, u32[]{:S(2)}) async-start(f32[32,1,384]{2,1,0:T(1,128)} %bitcast.13), calls=%async_computation.3 | async-start | bytes 98304 | tf_op jit(solution)/shard_map/all_to_all | solution.py:860
  65.3 11.2 %all-to-all-start.5 = ((f32[32,1,1280]{2,1,0:T(1,128)}), f32[32,1,1280]{2,1,0:T(1,128)S(1)}, u32[]{:S(2)}, u32[]{:S(2)}) async-start(f32[32,1,1280]{2,1,0:T(1,128)} %bitcast.17), calls=%async_computation.5 | async-start | bytes 327680 | tf_op jit(solution)/shard_map/all_to_all | solution.py:860
  67.8 1.6 %collective-permute-start = (f32[576,128]{1,0:T(8,128)S(1)}, f32[576,128]{1,0:T(8,128)S(1)}, u32[]{:S(2)}, u32[]{:S(2)}) collective-permute-start(f32[576,128]{1,0:T(8,128)S(1)} %bitcast.20), channel_id=1, source_target_pairs={{0,1},{1,0},{2,3},{3,2},{4,5},{5,4},{6,7},{7,6},{8,9},{9,8},{10,11... | collective-permute-start | bytes 884744 | tf_op jit(solution)/shard_map/ppermute | solution.py:943

commit v10 on v8

--- a/solution.py
+++ b/solution.py
@@ -584,7 +584,6 @@
     weighted = wide_ref[0:256, :] * field
     energy = jnp.sum(field * weighted)
     mixed = table_to_mixed(weighted, kron, turned, rows_ref, stack_ref)
-    carried_ref[...] = wide_ref[...]
     keep_rows(carried_ref, 0, mixed)
     for j in range(2):
         put(send_ref, j, PLAIN, tile_of(mixed, j))
@@ -705,7 +704,6 @@
     send_ref, rows_ref, stack_ref,
 ):
     kron, second, turned = constants(inner_ref)
-    send_ref[...] = early_ref[...]
     image = received_rows(recv_ref)
     step = pick(scalar_ref, 1)
     reduced = kept_rows(wide_ref, 1) - step * (

time: 78.3 us -> 78.3 us (level)
  no operation moved by 1% of the time
where the time goes in v10:
time: 78.3 us; the launch traced here: 78 us
  blocking collectives  31.4 us (40%)
  Pallas kernels  17.6 us (22%)
  waiting for transfers between devices  14.9 us (19%)
  starting transfers between devices  12.6 us (16%)
    all_to_all x3, blocking collectives, exchange(): lax.all_to_all(buffer.reshape(shape), ('slab', 'grp'), 0, 0, tiled=True)  31.4 us
    pallas_call x10, Pallas kernels, call(): pl.pallas_call(kernel, out_shape=[shape if isinstance(shape, jax.ShapeDty...  17.6 us
    all_to_all x3, waiting for transfers between devices, exchange(): lax.all_to_all(buffer.reshape(shape), ('slab', 'grp'), 0, 0, tiled=True)  13.5 us
    all_to_all x3, starting transfers between devices, exchange(): lax.all_to_all(buffer.reshape(shape), ('slab', 'grp'), 0, 0, tiled=True)  12.5 us
  transfers between devices with their start and end apart: 4, of which 4 were waited for; matrix products, arithmetic and copies ran while one was open for 0% of the time, Pallas kernels for 10%

profile of v10, /device:TPU:0, one launch (start us, length us, event | category | flops | bytes accessed | tf_op | source)
XLA Modules:
  0.0 78.0 jit_solution(12057432396224417686)
XLA Ops:
  0.6 2.8 %shard_map.113 = (f32[160,128]{1,0:T(8,128)}, f32[416,256]{1,0:T(8,128)}, bf16[704,128]{1,0:T(8,128)(2,1)}) custom-call(f32[5,2,3200]{2,1,0:T(2,128)} %bitcast.32, f32[5,2,3200]{2,1,0:T(2,128)} %bitcast.33, s32[64]{0:T(128)} %start2_hbm.1, f32[4,64]{1,0:T(4,128)} %bitcast.35, s32[50]{0:T(128)} %start3_hbm.1, f32[4,50]{1,0:T(4,128)} %bitcast.36), custom_call_target="tpu_custom_call" | custom-call | tf_op jit(solution)/shard_map/pallas_call | solution.py:831
  3.4 7.3 %all-to-all-start = ((f32[32,1,640]{2,1,0:T(1,128)}), f32[32,1,640]{2,1,0:T(1,128)S(1)}, u32[]{:S(2)}, u32[]{:S(2)}) async-start(f32[32,1,640]{2,1,0:T(1,128)} %bitcast.34), calls=%async_computation | async-start | bytes 163840 | tf_op jit(solution)/shard_map/all_to_all | solution.py:855
  10.7 0.0 copy-start.3
  10.8 0.0 copy-start.2
  10.8 0.0 copy-start.4
  10.8 0.0 copy-start.5
  10.8 0.6 copy-done.3
  11.4 0.0 copy-done.2
  11.4 0.0 copy-done.4
  11.4 0.0 copy-done.5
  11.5 3.2 %shard_map.114 = (bf16[640,320]{1,0:T(8,128)(2,1)S(1)}, bf16[640,320]{1,0:T(8,128)(2,1)S(1)}, bf16[640,320]{1,0:T(8,128)(2,1)S(1)}, bf16[640,320]{1,0:T(8,128)(2...) custom-call(s32[1]{0:T(128)} %bitcast.6.group_ref, s32[32]{0:T(128)S(1)} %copy-done.4, ...), custom_call_target="tpu_custom_call" | custom-call | tf_op jit(solution)/shard_map/pallas_call | solution.py:831
  14.7 3.6 %all-to-all-done = f32[32,1,640]{2,1,0:T(1,128)S(1)} async-done(((f32[32,1,640]{2,1,0:T(1,128)}), f32[32,1,640]{2,1,0:T(1,128)S(1)}, u32[]{:S(2)}, u32[]{:S(2)}) %all-to-all-start) | async-done | bytes 81952 | tf_op jit(solution)/shard_map/all_to_all | solution.py:855
  18.3 0.0 copy-start
  18.3 1.0 %shard_map.115 = (f32[96,128]{1,0:T(8,128)S(1)}, f32[320,128]{1,0:T(8,128)S(1)}, f32[320,128]{1,0:T(8,128)S(1)}) custom-call(f32[160,128]{1,0:T(8,128)S(1)} %bitcast.24, bf16[640,320]{1,0:T(8,128)(2,1)S(1)} %get-tuple-element.29.gram_h_ref, bf16[640,320]{1,0:T(8,128)(2,1)S(1)} %get-tuple-element.30.gram_l_ref), custom_call_target="tpu_custom_call" | custom-call | tf_op jit(solution)/shard_map/pallas_call | solution.py:831
  19.3 9.3 %all_to_all.30 = f32[32,1,384]{2,1,0:T(1,128)S(1)} all-to-all(f32[32,1,384]{2,1,0:T(1,128)S(1)} %bitcast.29), channel_id=1, replica_groups=mesh['slab'=16,'grp'=2] {'slab','grp'}, dimensions={0} | all-to-all | bytes 98304 | tf_op jit(solution)/shard_map/all_to_all | solution.py:855
  28.7 0.0 copy-done
  28.7 0.0 copy-done.1
  28.7 1.1 %shard_map.116 = (f32[96,128]{1,0:T(8,128)S(1)}, f32[8,128]{1,0:T(8,128)S(1)}, f32[416,256]{1,0:T(8,128)S(1)}) custom-call(f32[96,128]{1,0:T(8,128)S(1)} %bitcast.26, f32[416,256]{1,0:T(8,128)S(1)} %copy-done, bf16[704,128]{1,0:T(8,128)(2,1)S(1)} %copy-done.1), custom_call_target="tpu_custom_call", output_to_operand_aliasing={{2}: (1, {})} | custom-call | tf_op jit(solution)/shard_map/pallas_call | solution.py:831
  29.8 9.0 %all_to_all.31 = f32[32,1,384]{2,1,0:T(1,128)S(1)} all-to-all(f32[32,1,384]{2,1,0:T(1,128)S(1)} %bitcast.28), channel_id=1, replica_groups=mesh['slab'=16,'grp'=2] {'slab','grp'}, dimensions={0} | all-to-all | bytes 98304 | tf_op jit(solution)/shard_map/all_to_all | solution.py:855
  38.8 1.2 %shard_map.117 = (f32[96,128]{1,0:T(8,128)}, f32[320,128]{1,0:T(8,128)S(1)}, f32[8,128]{1,0:T(8,128)S(1)}) custom-call(f32[96,128]{1,0:T(8,128)S(1)} %bitcast.27, bf16[640,320]{1,0:T(8,128)(2,1)S(1)} %get-tuple-element.29.gram_h_ref, bf16[640,320]{1,0:T(8,128)(2,1)S(1)} %get-tuple-element.30.gram_l_ref, ...), custom_call_target="tpu_custom_call", output_to_operand_aliasing={{1}: (3, {})} | custom-call | tf_op jit(solution)/shard_map/pallas_call | solution.py:831
  40.0 2.6 %all-to-all-start.3 = ((f32[32,1,384]{2,1,0:T(1,128)}), f32[32,1,384]{2,1,0:T(1,128)S(1)}, u32[]{:S(2)}, u32[]{:S(2)}) async-start(f32[32,1,384]{2,1,0:T(1,128)} %bitcast.13), calls=%async_computation.3 | async-start | bytes 98304 | tf_op jit(solution)/shard_map/all_to_all | solution.py:855
  42.6 2.4 %shard_map.118 = (f32[576,128]{1,0:T(8,128)S(1)}, f32[640,128]{1,0:T(8,128)S(1)}, f32[8,128]{1,0:T(8,128)S(1)}) custom-call(f32[320,128]{1,0:T(8,128)S(1)} %get-tuple-element.38.blend_ref, bf16[640,320]{1,0:T(8,128)(2,1)S(1)} %get-tuple-element.39.lift_h_ref, bf16[640,320]{1,0:T(8,128)(2,1)S(1)} %get-tuple-element.40.lift_l_ref, ...), custom_call_target="tpu_custom_call" | custom-call | tf_op jit(solution)/shard_map/pallas_call | solution.py:831
  45.0 4.9 %all-to-all-done.3 = f32[32,1,384]{2,1,0:T(1,128)S(1)} async-done(((f32[32,1,384]{2,1,0:T(1,128)}), f32[32,1,384]{2,1,0:T(1,128)S(1)}, u32[]{:S(2)}, u32[]{:S(2)}) %all-to-all-start.3) | async-done | bytes 49184 | tf_op jit(solution)/shard_map/all_to_all | solution.py:855
  49.9 1.2 %shard_map.119 = f32[576,128]{1,0:T(8,128)S(1)} custom-call(f32[576,128]{1,0:T(8,128)S(1)} %get-tuple-element.43.early_ref, f32[96,128]{1,0:T(8,128)S(1)} %bitcast.25, f32[8,128]{1,0:T(8,128)S(1)} %get-tuple-element.45.sums_ref, f32[8,128]{1,0:T(8,128)S(1)} %get-tuple-element.41.scalar_ref, ...), custom_call_target="tpu_custom_call", output_to_operand_aliasing={{}: (0, {})} | custom-call | tf_op jit(solution)/shard_map/pallas_call | solution.py:831
  51.1 13.1 %all_to_all.32 = f32[32,1,2304]{2,1,0:T(1,128)S(1)} all-to-all(f32[32,1,2304]{2,1,0:T(1,128)S(1)} %bitcast.22), channel_id=1, replica_groups=mesh['slab'=16,'grp'=2] {'slab','grp'}, dimensions={0} | all-to-all | bytes 589824 | tf_op jit(solution)/shard_map/all_to_all | solution.py:855
  64.2 1.2 %shard_map.120 = (f32[320,128]{1,0:T(8,128)}, f32[8,128]{1,0:T(8,128)S(1)}) custom-call(f32[576,128]{1,0:T(8,128)S(1)} %bitcast.19, bf16[64,32]{1,0:T(8,128)(2,1)S(1)} %get-tuple-element.47.small_h_ref, bf16[64,32]{1,0:T(8,128)(2,1)S(1)} %get-tuple-element.48.small_l_ref, f32[640,128]{1,0:T(8,128)S(1)} %get-tuple-element.49.keep_ref, ...), custom_call_target="tpu_custom_call" | custom-call | tf_op jit(solution)/shard_map/pallas_call | solution.py:831
  65.5 2.6 %all-to-all-start.5 = ((f32[32,1,1280]{2,1,0:T(1,128)}), f32[32,1,1280]{2,1,0:T(1,128)S(1)}, u32[]{:S(2)}, u32[]{:S(2)}) async-start(f32[32,1,1280]{2,1,0:T(1,128)} %bitcast.17), calls=%async_computation.5 | async-start | bytes 327680 | tf_op jit(solution)/shard_map/all_to_all | solution.py:855
  68.1 0.2 collective-permute-start
  68.2 1.5 %collective-permute-done.partner_ref = f32[576,128]{1,0:T(8,128)S(1)} collective-permute-done((f32[576,128]{1,0:T(8,128)S(1)}, f32[576,128]{1,0:T(8,128)S(1)}, u32[]{:S(2)}, u32[]{:S(2)}) %collective-permute-start) | collective-permute-done | bytes 294944 | tf_op jit(solution)/shard_map/ppermute | solution.py:938
  69.7 2.0 %shard_map.121 = (f32[4,32,1024]{2,1,0:T(8,128)}, f32[128,1024]{1,0:T(8,128)S(1)}) custom-call(f32[576,128]{1,0:T(8,128)S(1)} %bitcast.21, f32[576,128]{1,0:T(8,128)S(1)} %collective-permute-done.partner_ref, f32[192,384]{1,0:T(8,128)S(1)} %get-tuple-element.42.side_ref, f32[8,128]{1,0:T(8,128)S(1)} %get-tuple-element.50.scalar_ref), custom_call_target="tpu_custom_call" | custom-call | tf_op jit(solution)/shard_map/pallas_call | solution.py:831
  71.7 4.9 %all-to-all-done.5 = f32[32,1,1280]{2,1,0:T(1,128)S(1)} async-done(((f32[32,1,1280]{2,1,0:T(1,128)}), f32[32,1,1280]{2,1,0:T(1,128)S(1)}, u32[]{:S(2)}, u32[]{:S(2)}) %all-to-all-start.5) | async-done | bytes 163872 | tf_op jit(solution)/shard_map/all_to_all | solution.py:855
  76.6 1.3 %shard_map.122 = f32[4,32,1024]{2,1,0:T(8,128)} custom-call(f32[320,128]{1,0:T(8,128)S(1)} %bitcast.23, f32[192,384]{1,0:T(8,128)S(1)} %get-tuple-element.42.side_ref, f32[128,1024]{1,0:T(8,128)S(1)} %get-tuple-element.53.part_ref), custom_call_target="tpu_custom_call" | custom-call | tf_op jit(solution)/shard_map/pallas_call | solution.py:831
  (1 shorter events, 0.0 us)
Async XLA Ops:
  3.4 14.9 %all-to-all-start = ((f32[32,1,640]{2,1,0:T(1,128)}), f32[32,1,640]{2,1,0:T(1,128)S(1)}, u32[]{:S(2)}, u32[]{:S(2)}) async-start(f32[32,1,640]{2,1,0:T(1,128)} %bitcast.34), calls=%async_computation | async-start | bytes 163840 | tf_op jit(solution)/shard_map/all_to_all | solution.py:855
  10.7 0.7 copy-start.3
  10.8 0.7 copy-start.2
  10.8 0.7 copy-start.4
  10.8 0.7 copy-start.5
  18.3 10.3 %copy-start = (f32[416,256]{1,0:T(8,128)S(1)}, f32[416,256]{1,0:T(8,128)}, u32[]{:S(2)}) copy-start(f32[416,256]{1,0:T(8,128)} %get-tuple-element.32.wide_ref) | copy-start | bytes 1277956
  18.3 10.3 %copy-start.1 = (bf16[704,128]{1,0:T(8,128)(2,1)S(1)}, bf16[704,128]{1,0:T(8,128)(2,1)}, u32[]{:S(2)}) copy-start(bf16[704,128]{1,0:T(8,128)(2,1)} %get-tuple-element.33.inner_ref) | copy-start | bytes 540676
  40.0 9.9 %all-to-all-start.3 = ((f32[32,1,384]{2,1,0:T(1,128)}), f32[32,1,384]{2,1,0:T(1,128)S(1)}, u32[]{:S(2)}, u32[]{:S(2)}) async-start(f32[32,1,384]{2,1,0:T(1,128)} %bitcast.13), calls=%async_computation.3 | async-start | bytes 98304 | tf_op jit(solution)/shard_map/all_to_all | solution.py:855
  65.5 11.2 %all-to-all-start.5 = ((f32[32,1,1280]{2,1,0:T(1,128)}), f32[32,1,1280]{2,1,0:T(1,128)S(1)}, u32[]{:S(2)}, u32[]{:S(2)}) async-start(f32[32,1,1280]{2,1,0:T(1,128)} %bitcast.17), calls=%async_computation.5 | async-start | bytes 327680 | tf_op jit(solution)/shard_map/all_to_all | solution.py:855
  68.1 1.6 %collective-permute-start = (f32[576,128]{1,0:T(8,128)S(1)}, f32[576,128]{1,0:T(8,128)S(1)}, u32[]{:S(2)}, u32[]{:S(2)}) collective-permute-start(f32[576,128]{1,0:T(8,128)S(1)} %bitcast.20), channel_id=1, source_target_pairs={{0,1},{1,0},{2,3},{3,2},{4,5},{5,4},{6,7},{7,6},{8,9},{9,8},{10,11... | collective-permute-start | bytes 884744 | tf_op jit(solution)/shard_map/ppermute | solution.py:938
